TPU v7x, 256 devices: a whole 4x4x8 slice. The times are simulated.
256 devices in a mesh: tile: 128 (over y, z, x), basin: 2 (over core).
Axes of the slice: x: 4, y: 4, z: 8, core: 2. Of those that a mesh axis runs over, the one named last changes fastest.
Arguments:
- cell_features: bfloat16 [65536, 512], P(('tile', 'basin')), may hold values from -6 to 6
- encoded: bfloat16 [1024, 512], P('tile'), may hold values from -6 to 6
- w_query: bfloat16 [512, 512], replicated, may hold values from -0.375 to 0.375
- w_key: bfloat16 [512, 512], replicated, may hold values from -0.375 to 0.375
- w_value: bfloat16 [512, 512], replicated, may hold values from -0.25 to 0.25
- w_out: bfloat16 [512, 512], replicated, may hold values from -0.25 to 0.25
- pattern: int32 [256, 16], P(('tile', 'basin')), may hold values from 0 to 127, all different within a row
- cell_basin: int32 [65536], P(('tile', 'basin')), may hold values from 0 to 511, as said below
- pooled_grad: bfloat16 [512, 512], P(('tile', 'basin')), may hold values from -24 to 24
Outputs:
- pooled: bfloat16 [512, 512], P(('tile', 'basin'))
- grad_cells: bfloat16 [65536, 512], P(('tile', 'basin'))
- grad_gauges: bfloat16 [1024, 512], P('tile')
- grad_query_weight: float32 [512, 512], replicated
- grad_key_weight: float32 [512, 512], replicated
- grad_value_weight: float32 [512, 512], replicated
- grad_out_weight: float32 [512, 512], replicated
Inputs may be any that keep to these rules, and one draw needn't show every extreme that they name: `pattern`: each row names 16 different gauge blocks; every block is named by some row. `cell_basin`: cell c lies in basin (2 * (c // 256) + k) mod 512 for some k with -2 <= k < 4; when c % 256 < 6, k = c % 256 - 2.
All inputs are finite; a program needn't handle non-finite values.
Results may differ from a plain program's by a relative error of at most 0.012.
The roundings to bfloat16 on the way count: a program that leaves them out, or rounds other values in their place, can miss the bound.
Values may be sent and summed in bfloat16 or wider, within the bound.
No kernel may reach another device: no remote copies, remote signals or barrier semaphores. Data moves between devices by JAX's collectives and lax.ppermute only.
A program may use at most 64 MiB of HBM per device.

v0:
```python
import math

import jax
import jax.numpy as jnp
from jax import lax
from jax.sharding import PartitionSpec as P

HEADS = 8
HEAD_DIM = 64


score_cap = 30.0


def shifted(value, axis, steps):
    count = lax.axis_size(axis)
    pairs = [(source, (source + steps) % count) for source in range(count)]
    return lax.ppermute(value, axis, pairs)


def forward_heads(queries, key_sel, value_sel):
    row_count = queries.shape[0]
    key_count = key_sel.shape[0]
    query_heads = queries.reshape(row_count, HEADS, HEAD_DIM)
    key_heads = key_sel.reshape(key_count, HEADS, HEAD_DIM)
    value_heads = value_sel.reshape(key_count, HEADS, HEAD_DIM)
    scores = jnp.einsum(
        "rhd,khd->hrk", query_heads, key_heads, preferred_element_type=jnp.float32
    ) * (1.0 / math.sqrt(HEAD_DIM))
    tanh_val = jnp.tanh(scores / score_cap)
    exponent = jnp.exp(score_cap * tanh_val)
    weights = exponent / jnp.sum(exponent, axis=-1, keepdims=True)
    weights_bf = weights.astype(jnp.bfloat16)
    attended = jnp.einsum(
        "hrk,khd->rhd", weights_bf, value_heads, preferred_element_type=jnp.float32
    )
    attended = attended.reshape(row_count, HEADS * HEAD_DIM).astype(jnp.bfloat16)
    return (attended, weights, weights_bf, tanh_val)


def backward_heads(queries, key_sel, value_sel, weights, weights_bf, tanh_val, attended_grad):
    row_count = queries.shape[0]
    key_count = key_sel.shape[0]
    query_heads = queries.reshape(row_count, HEADS, HEAD_DIM)
    key_heads = key_sel.reshape(key_count, HEADS, HEAD_DIM)
    value_heads = value_sel.reshape(key_count, HEADS, HEAD_DIM)
    grad_heads = attended_grad.reshape(row_count, HEADS, HEAD_DIM)
    weight_grad = jnp.einsum(
        "rhd,khd->hrk", grad_heads, value_heads, preferred_element_type=jnp.float32
    )
    value_grad = jnp.einsum(
        "hrk,rhd->khd", weights_bf, grad_heads, preferred_element_type=jnp.float32
    )
    inner_sum = jnp.sum(weights * weight_grad, axis=-1, keepdims=True)
    score_grad = (
        weights
        * (weight_grad - inner_sum)
        * (1.0 - tanh_val * tanh_val)
        * (1.0 / math.sqrt(HEAD_DIM))
    )
    score_grad = score_grad.astype(jnp.bfloat16)
    query_grad = jnp.einsum(
        "hrk,khd->rhd", score_grad, key_heads, preferred_element_type=jnp.float32
    )
    query_grad = query_grad.reshape(row_count, HEADS * HEAD_DIM).astype(jnp.bfloat16)
    key_grad = jnp.einsum(
        "hrk,rhd->khd", score_grad, query_heads, preferred_element_type=jnp.float32
    )
    return (
        query_grad,
        key_grad.reshape(key_count, HEADS * HEAD_DIM),
        value_grad.reshape(key_count, HEADS * HEAD_DIM),
    )


def fetch_gauges(moving):
    return lax.all_gather(moving, "tile", axis=0, tiled=True)


def sum_cores(partial_value):
    return lax.psum(partial_value, "basin")


def contract_rows(left_side, right_side):
    return lax.dot_general(
        left_side, right_side, (((0,), (0,)), ((), ())), preferred_element_type=jnp.float32
    )


def contract_cols(left_side, right_side):
    return lax.dot_general(
        left_side, right_side, (((1,), (1,)), ((), ())), preferred_element_type=jnp.float32
    )


def per_device(
    cell_features, encoded, w_query, w_key, w_value, w_out, pattern, cell_basin, pooled_grad
):
    highest = lax.Precision.HIGHEST
    cell_count = cell_features.shape[0]
    model_width = cell_features.shape[1]
    gauge_rows = encoded.shape[0]
    chosen_blocks = pattern[0]
    block_count = chosen_blocks.shape[0]
    tile_count = lax.axis_size("tile")
    queries = jnp.dot(cell_features, w_query, preferred_element_type=jnp.float32).astype(
        jnp.bfloat16
    )
    own_keys = jnp.dot(encoded, w_key, preferred_element_type=jnp.float32).astype(jnp.bfloat16)
    own_values = jnp.dot(encoded, w_value, preferred_element_type=jnp.float32).astype(jnp.bfloat16)
    moving = jnp.concatenate([own_keys, own_values], axis=1)
    gathered = fetch_gauges(moving)
    shaped = gathered.reshape(tile_count, gauge_rows, gathered.shape[1])
    picked = jnp.take(shaped, chosen_blocks, axis=0).reshape(
        block_count * gauge_rows, gathered.shape[1]
    )
    key_sel = picked[:, :model_width]
    value_sel = picked[:, model_width:]
    block_rows = min(512, cell_count)
    block_total = cell_count // block_rows
    query_blocks = queries.reshape(block_total, block_rows, model_width)

    def attend_block(query_block):
        return forward_heads(query_block, key_sel, value_sel)[0]

    attended = lax.map(attend_block, query_blocks).reshape(cell_count, model_width)
    cell_out = jnp.dot(attended, w_out, preferred_element_type=jnp.float32).astype(jnp.bfloat16)
    device = lax.axis_index(("tile", "basin"))
    own_basins = pooled_grad.shape[0]
    basin_total = own_basins * lax.axis_size(("tile", "basin"))
    basin_slot = (cell_basin - device * own_basins + own_basins) % basin_total
    slot_count = 3 * own_basins
    onehot = (basin_slot[:, None] == jnp.arange(slot_count, dtype=jnp.int32)[None, :]).astype(
        jnp.bfloat16
    )
    basin_sums = contract_rows(onehot, cell_out)
    slot_counts = jnp.sum(onehot, axis=0, dtype=jnp.float32)
    lower_part = (basin_sums[:own_basins], slot_counts[:own_basins])
    upper_part = (basin_sums[2 * own_basins :], slot_counts[2 * own_basins :])
    from_above = shifted((lower_part[0], lower_part[1]), ("tile", "basin"), -1)
    from_below = shifted((upper_part[0], upper_part[1]), ("tile", "basin"), 1)
    own_sums = basin_sums[own_basins : 2 * own_basins] + from_above[0] + from_below[0]
    own_counts = slot_counts[own_basins : 2 * own_basins] + from_above[1] + from_below[1]
    count_root = jnp.sqrt(own_counts)
    pooled = (own_sums / count_root[:, None]).astype(jnp.bfloat16)
    scaled_table = pooled_grad.astype(jnp.float32) / count_root[:, None]
    below_table = shifted(scaled_table, ("tile", "basin"), 1)
    above_table = shifted(scaled_table, ("tile", "basin"), -1)
    grad_table = jnp.concatenate([below_table, scaled_table, above_table], axis=0)
    out_grad = jnp.take(grad_table, basin_slot, axis=0).astype(jnp.bfloat16)
    grad_out_local = contract_rows(attended, out_grad)
    attended_grad = contract_cols(out_grad, w_out).astype(jnp.bfloat16)
    grad_blocks = attended_grad.reshape(block_total, block_rows, model_width)

    def backward_block(running, pieces):
        query_block, grad_block = pieces
        unused, weights, weights_bf, tanh_val = forward_heads(query_block, key_sel, value_sel)
        query_grad, key_grad, value_grad = backward_heads(
            query_block, key_sel, value_sel, weights, weights_bf, tanh_val, grad_block
        )
        return ((running[0] + key_grad, running[1] + value_grad), query_grad)

    empty = jnp.zeros((key_sel.shape[0], model_width), jnp.float32)
    (key_grad_sel, value_grad_sel), query_grad = lax.scan(
        backward_block, (empty, empty), (query_blocks, grad_blocks)
    )
    query_grad = query_grad.reshape(cell_count, model_width)
    grad_query_local = contract_rows(cell_features, query_grad)
    grad_cells = contract_cols(query_grad, w_query).astype(jnp.bfloat16)
    both_grads = jnp.concatenate([key_grad_sel, value_grad_sel], axis=1)
    both_weights = jnp.concatenate([w_key, w_value], axis=1).astype(jnp.float32)
    column_width = both_grads.shape[1]
    return_term = jnp.zeros((tile_count, gauge_rows, column_width), jnp.float32)
    return_term = return_term.at[chosen_blocks].set(
        both_grads.reshape(block_count, gauge_rows, column_width)
    )
    return_term = return_term.reshape(tile_count * gauge_rows, column_width)
    returned = lax.psum_scatter(return_term, "tile", scatter_dimension=0, tiled=True)
    pair_local = lax.dot_general(
        encoded.astype(jnp.float32), returned, (((0,), (0,)), ((), ())), precision=highest
    )
    partial_value = lax.dot_general(
        returned, both_weights, (((1,), (1,)), ((), ())), precision=highest
    )
    grad_gauges = sum_cores(partial_value)
    grad_gauges = grad_gauges.astype(jnp.bfloat16)
    summed = lax.psum((grad_query_local, grad_out_local, pair_local), ("tile", "basin"))
    grad_query_weight = summed[0]
    grad_out_weight = summed[1]
    grad_key_weight = summed[2][:, :model_width]
    grad_value_weight = summed[2][:, model_width:]
    return (
        pooled,
        grad_cells,
        grad_gauges,
        grad_query_weight,
        grad_key_weight,
        grad_value_weight,
        grad_out_weight,
    )


def solution(mesh):
    return jax.shard_map(
        per_device,
        mesh=mesh,
        in_specs=(
            P(("tile", "basin"), None),
            P("tile", None),
            P(),
            P(),
            P(),
            P(),
            P(("tile", "basin"), None),
            P(("tile", "basin")),
            P(("tile", "basin"), None),
        ),
        out_specs=(
            P(("tile", "basin"), None),
            P(("tile", "basin"), None),
            P("tile", None),
            P(),
            P(),
            P(),
            P(),
        ),
        check_vma=False,
    )
```

profile of v0, /device:TPU:1, one launch (start us, length us, event | category | flops | bytes accessed | tf_op | source)
XLA Modules:
  0.0 1124.7 jit_solution(10916404886895113197)
XLA Ops:
  7.2 1.3 convolution_convert_fusion.6
  8.5 1.2 convolution_convert_fusion.7
  10.5 0.7 compare_and_fusion
  11.3 2.6 collective-permute-start.3
  14.0 0.7 collective-permute-start.2
  16.0 1.2 convolution_convert_fusion.5
  17.5 8.2 collective-permute-start.5
  26.5 5.6 collective-permute-done.4
  32.1 1.2 gather_fusion.1
  33.8 91.9 %all-gather.2.cloned.1.call-done = bf16[1024,1024]{1,0:T(8,128)(2,1)} async-done(((bf16[8,1024]{1,0:T(8,128)(2,1)}), bf16[1024,1024]{1,0:T(8,128)(2,1)}) %all-gather.2.cloned.1.call-update) | async-done | bytes 2097168 | tf_op jit(solution)/shard_map/all_gather | solution.py:77
  125.7 2.2 gather_fusion
  130.3 2.3 convolution_bitcast_fusion.3
  133.0 2.5 broadcast_in_dim.53
  135.5 2.6 scatter_fusion
  138.2 1.1 copy-done.11
  139.3 0.7 convolution_convert_fusion.1
  141.0 1.3 convolution_bitcast_fusion.1
  142.2 1.3 fusion.39
  143.6 593.4 %reduce-scatter.2.cloned.1.call-done = f32[8,1024]{1,0:T(8,128)} async-done(((f32[1024,1024]{1,0:T(8,128)}), f32[8,1024]{1,0:T(8,128)}) %reduce-scatter.2.cloned.1.call-update) | async-done | bytes 32784 | tf_op jit(solution)/shard_map/reduce_scatter | solution.py:178
  737.0 3.1 convolution_bitcast_fusion
  740.2 1.0 copy-done.9
  741.6 101.3 %collective-permute-start.1 = (f32[2,512]{1,0:T(2,128)S(1)}, f32[2,512]{1,0:T(2,128)S(1)}, u32[]{:S(2)}, u32[]{:S(2)}) collective-permute-start(f32[2,512]{1,0:T(2,128)S(1)} %get-tuple-element.77), channel_id=1, source_target_pairs={{0,1},{1,2},{2,3},{3,4},{4,5},{5,6},{6,7},{7,8},{8,9},{9,10},{10,1... | collective-permute-start | bytes 12296 | tf_op jit(solution)/shard_map/ppermute | solution.py:18
  842.9 5.0 collective-permute-start
  848.0 1.1 convolution_convert_fusion
  849.7 0.9 fusion.8
  850.6 11.1 psum.28
  861.7 248.6 %all-reduce.3.cloned.1.call-done = (f32[512,512]{0,1:T(8,128)}, f32[512,1024]{0,1:T(8,128)}, f32[512,512]{1,0:T(8,128)}) async-done(((f32[512,512]{0,1:T(8,128)}, f32[512,1024]{0,1:T(8,128)}, f32[512,512]{1,0:T(8,128)}), (f32[512,512]{0,1:T(8,128)}, f32[512,1024]{0,1:T(8,128)}, f32[512,512]{1,0:T(8,128)})) %all-reduce.3.cloned.1.call-update) | async-done | bytes 4194320 | tf_op jit(solution)/shard_map/psum | solution.py:187
  1110.3 2.5 copy.49
  1112.9 1.7 fusion.46
  1114.6 1.3 copy.50
  1115.9 1.3 copy.51
  1117.2 1.0 copy.60
  (65 shorter events, 8.6 us)
Async XLA Ops:
  7.2 8.9 copy-start
  7.2 10.2 copy-start.7
  7.2 118.5 %all-gather.2.cloned.1.call-start = ((), (), s32[]{:S(2)}) async-start(), calls=%async_computation.1 | async-start | bytes 2113536 | tf_op jit(solution)/shard_map/all_gather | solution.py:77
  9.8 23.5 %copy-start.8 = (bf16[512,512]{1,0:T(8,128)(2,1)S(1)}, bf16[512,512]{1,0:T(8,128)(2,1)}, u32[]{:S(2)}) copy-start(bf16[512,512]{1,0:T(8,128)(2,1)} %param.14) | copy-start | bytes 1572868
  10.4 726.6 %reduce-scatter.2.cloned.1.call-start = ((), (), s32[]{:S(2)}) async-start(), calls=%async_computation.2 | async-start | bytes 4227072 | tf_op jit(solution)/shard_map/reduce_scatter | solution.py:178
  11.3 5.9 collective-permute-start.3
  14.0 3.3 collective-permute-start.2
  17.5 9.0 collective-permute-start.5
  25.7 6.4 collective-permute-start.4
  128.6 1.0 copy-start.10
  138.1 1.2 copy-start.11
  138.1 972.2 %all-reduce.3.cloned.1.call-start = ((), (), s32[]{:S(2)}) async-start(), calls=%async_computation.3 | async-start | bytes 8388608 | tf_op jit(solution)/shard_map/psum | solution.py:187
  140.0 1.0 copy-start.2
  140.4 596.7 %copy-start.5 = (bf16[8,512]{1,0:T(8,128)(2,1)S(1)}, bf16[8,512]{1,0:T(8,128)(2,1)}, u32[]{:S(2)}) copy-start(bf16[8,512]{1,0:T(8,128)(2,1)} %param.10) | copy-start | bytes 24580
  740.1 1.0 copy-start.9
  740.1 109.6 %copy-start.3 = (bf16[512,512]{1,0:T(8,128)(2,1)S(1)}, bf16[512,512]{1,0:T(8,128)(2,1)}, u32[]{:S(2)}) copy-start(bf16[512,512]{1,0:T(8,128)(2,1)} %param.13) | copy-start | bytes 1572868
  740.1 109.6 %copy-start.4 = (bf16[512,512]{1,0:T(8,128)(2,1)S(1)}, bf16[512,512]{1,0:T(8,128)(2,1)}, u32[]{:S(2)}) copy-start(bf16[512,512]{1,0:T(8,128)(2,1)} %param.12) | copy-start | bytes 1572868
  740.1 109.6 %copy-start.6 = (f32[8,1024]{1,0:T(8,128)S(1)}, f32[8,1024]{1,0:T(8,128)}, u32[]{:S(2)}) copy-start(f32[8,1024]{1,0:T(8,128)} %reduce-scatter.2.cloned.1.call-done) | copy-start | bytes 98308
  741.6 107.4 %collective-permute-start.1 = (f32[2,512]{1,0:T(2,128)S(1)}, f32[2,512]{1,0:T(2,128)S(1)}, u32[]{:S(2)}, u32[]{:S(2)}) collective-permute-start(f32[2,512]{1,0:T(2,128)S(1)} %get-tuple-element.77), channel_id=1, source_target_pairs={{0,1},{1,2},{2,3},{3,4},{4,5},{5,6},{6,7},{7,8},{8,9},{9,10},{10,1... | collective-permute-start | bytes 12296 | tf_op jit(solution)/shard_map/ppermute | solution.py:18
  842.9 6.1 collective-permute-start
  1115.9 1.3 copy-start.1
Sparse Core Ops, SparseCore 0:
  12.2 113.4 all-gather.1
  138.2 598.7 reduce-scatter.1
  744.4 365.8 all-reduce.2
where the time goes:
time: 1130 us; the launch traced here: 1120 us
  waiting for transfers between devices  940 us (83%)
  starting transfers between devices  118 us (10%)
  local copies, waits for them, and re-layouts  21.1 us (2%)
  matrix products  16.7 us (1%)
  between operations  14 us (1%)
    reduce_scatter x1, waiting for transfers between devices, per_device(): lax.psum_scatter(return_term, 'tile', scatter_dimension=0, tiled=True)  593 us
    psum x1, waiting for transfers between devices, per_device(): lax.psum((grad_query_local, grad_out_local, pair_local), ('tile', 'basin'))  249 us
    ppermute x6, starting transfers between devices, shifted(): return lax.ppermute(value, axis, pairs)  118 us
    all_gather x1, waiting for transfers between devices, fetch_gauges(): return lax.all_gather(moving, 'tile', axis=0, tiled=True)  91.9 us
  transfers between devices with their start and end apart: 9, of which 5 were waited for; matrix products, arithmetic and copies ran while one was open for 1% of the time, Pallas kernels for 0%

commit v1 on v0

v1 whole, which is shorter than its diff:
```python
import functools
import math

import jax
import jax.numpy as jnp
from jax import lax
from jax.experimental import pallas as pl
from jax.experimental.pallas import tpu as pltpu
from jax.sharding import Mesh
from jax.sharding import PartitionSpec as P

HEADS = 8
HEAD_DIM = 64
PAIR = 2 * HEAD_DIM
KEYS = 128
GAUGE_ROWS = 8
SLOTS = 16
score_cap = 30.0

EVERY = ("y", "z", "x", "c")
PLANE = ("y", "x")
SIZES = {"y": 4, "z": 8, "x": 4, "c": 2}

bf16 = jnp.bfloat16
f32 = jnp.float32


def mm(left, right):
    return jnp.dot(left, right, preferred_element_type=f32)


def mm_cols(left, right):
    return lax.dot_general(left, right, (((1,), (1,)), ((), ())), preferred_element_type=f32)


def mm_rows(left, right):
    return lax.dot_general(left, right, (((0,), (0,)), ((), ())), preferred_element_type=f32)


def two_parts(value):
    high = value.astype(bf16)
    return high, (value - high.astype(f32)).astype(bf16)


def group_kernel(
    core_ref, rows_ref, slot_ref, table_ref, mine_ref, other_ref, cells_ref,
    wq_ref, wk_ref, wv_ref, wo_ref,
    grad_cells_ref, sums_ref, keep_ref, send_ref,
):
    core = core_ref[0]
    first = core == 0
    width = 2 * mine_ref.shape[1]
    half = width // 2
    gauges = mine_ref.shape[0]
    pairs = width // PAIR
    plane = SIZES["y"] * SIZES["x"]
    gauge_chunk = gauges // plane
    weight_chunk = 4 * width // plane
    chunk = gauge_chunk + weight_chunk

    def store(row, value):
        low, high = value[:, :half].astype(bf16), value[:, half:].astype(bf16)
        count = value.shape[0]
        keep_ref[row : row + count, :] = jnp.where(first, low, high)
        send_ref[row : row + count, :] = jnp.where(first, high, low)

    def store_weight(which, value):
        per = value.shape[0] // weight_chunk
        for j in range(per):
            store(
                (which * per + j) * chunk,
                value[j * weight_chunk : (j + 1) * weight_chunk, :],
            )

    picks = jnp.where(
        lax.broadcasted_iota(jnp.int32, (gauges, KEYS), 0) == rows_ref[...], 1.0, 0.0
    ).astype(bf16)
    sel_mine = mm_rows(picks, mine_ref[...])
    sel_other = mm_rows(picks, other_ref[...])
    encoded_sel = jnp.concatenate(
        [jnp.where(first, sel_mine, sel_other), jnp.where(first, sel_other, sel_mine)], axis=1
    ).astype(bf16)
    keys = mm(encoded_sel, wk_ref[...]).astype(bf16)
    values = mm(encoded_sel, wv_ref[...]).astype(bf16)
    queries = mm(cells_ref[...], wq_ref[...]).astype(bf16)
    even = lax.broadcasted_iota(jnp.int32, (KEYS, PAIR), 1) < HEAD_DIM
    zero = jnp.zeros((KEYS, PAIR), bf16)
    scale = 1.0 / math.sqrt(HEAD_DIM)

    saved = []
    attended = []
    for p in range(pairs):
        columns = slice(p * PAIR, (p + 1) * PAIR)
        key_pair, value_pair = keys[:, columns], values[:, columns]
        key_two = jnp.concatenate(
            [jnp.where(even, key_pair, zero), jnp.where(even, zero, key_pair)], axis=0
        )
        value_two = jnp.concatenate(
            [jnp.where(even, value_pair, zero), jnp.where(even, zero, value_pair)], axis=0
        )
        query_pair = queries[:, columns]
        scores = mm_cols(query_pair, key_two) * scale
        tanh_val = jnp.tanh(scores / score_cap)
        exponent = jnp.exp(score_cap * tanh_val)
        parts = []
        for side in range(2):
            part = exponent[:, side * KEYS : (side + 1) * KEYS]
            parts.append(part / jnp.sum(part, axis=-1, keepdims=True))
        weights = jnp.concatenate(parts, axis=1)
        weights_bf = weights.astype(bf16)
        attended.append(mm(weights_bf, value_two).astype(bf16))
        saved.append((key_two, value_two, query_pair, tanh_val, weights, weights_bf))
    attended = jnp.concatenate(attended, axis=1)
    cell_out = mm(attended, wo_ref[...]).astype(bf16)
    onehot = jnp.where(
        lax.broadcasted_iota(jnp.int32, (SLOTS, cell_out.shape[0]), 0) == slot_ref[...], 1.0, 0.0
    ).astype(bf16)
    sums_ref[...] = mm(onehot, cell_out)
    out_grad = mm_rows(onehot, table_ref[...]).astype(bf16)
    attended_grad = mm_cols(out_grad, wo_ref[...]).astype(bf16)
    store_weight(3, mm_rows(attended, out_grad))

    query_grad, key_grad, value_grad = [], [], []
    for p in range(pairs):
        key_two, value_two, query_pair, tanh_val, weights, weights_bf = saved[p]
        grad_pair = attended_grad[:, p * PAIR : (p + 1) * PAIR]
        weight_grad = mm_cols(grad_pair, value_two)
        two = mm_rows(weights_bf, grad_pair)
        value_grad.append(jnp.where(even, two[:KEYS], two[KEYS:]))
        product = weights * weight_grad
        parts = []
        for side in range(2):
            columns = slice(side * KEYS, (side + 1) * KEYS)
            parts.append(
                weight_grad[:, columns] - jnp.sum(product[:, columns], axis=-1, keepdims=True)
            )
        centred = jnp.concatenate(parts, axis=1)
        score_grad = (weights * centred * (1.0 - tanh_val * tanh_val) * scale).astype(bf16)
        query_grad.append(mm(score_grad, key_two).astype(bf16))
        two = mm_rows(score_grad, query_pair)
        key_grad.append(jnp.where(even, two[:KEYS], two[KEYS:]))
    query_grad = jnp.concatenate(query_grad, axis=1)
    grad_cells_ref[...] = mm_cols(query_grad, wq_ref[...]).astype(bf16)
    store_weight(0, mm_rows(cells_ref[...], query_grad))
    key_high, key_low = two_parts(jnp.concatenate(key_grad, axis=1))
    value_high, value_low = two_parts(jnp.concatenate(value_grad, axis=1))
    store_weight(1, mm_rows(encoded_sel, key_high) + mm_rows(encoded_sel, key_low))
    store_weight(2, mm_rows(encoded_sel, value_high) + mm_rows(encoded_sel, value_low))
    grad_gauges = (
        mm_cols(key_high, wk_ref[...])
        + mm_cols(key_low, wk_ref[...])
        + mm_cols(value_high, wv_ref[...])
        + mm_cols(value_low, wv_ref[...])
    ).astype(bf16)
    for j in range(plane):
        store(
            j * chunk + weight_chunk,
            mm(picks[j * gauge_chunk : (j + 1) * gauge_chunk, :], grad_gauges),
        )


def swap(value):
    return lax.ppermute(value, "c", [(0, 1), (1, 0)])


def shifted(value, steps):
    count = lax.axis_size(EVERY)
    return lax.ppermute(value, EVERY, [(i, (i + steps) % count) for i in range(count)])


def spread(value, axes, count):
    rows, width = value.shape
    copies = jnp.broadcast_to(value[None], (count, rows, width)).reshape(count * rows, width)
    return lax.all_to_all(copies, axes, 0, 0, tiled=True)


def gathered(value):
    column = spread(value, "z", SIZES["z"])
    return spread(column, PLANE, SIZES["y"] * SIZES["x"])


def per_device(cells, encoded, w_query, w_key, w_value, w_out, pattern, cell_basin, pooled_grad):
    width = cells.shape[1]
    half = width // 2
    plane, depth = SIZES["y"] * SIZES["x"], SIZES["z"]
    core = lax.axis_index("c")
    device = lax.axis_index(EVERY)
    own = pooled_grad.shape[0]
    total = own * lax.axis_size(EVERY)

    slot = (cell_basin - device * own + own) % total
    counts = jnp.sum(
        (slot[None, :] == jnp.arange(3 * own, dtype=jnp.int32)[:, None]).astype(f32), axis=1
    )
    count_row = jnp.pad(counts.astype(bf16), (0, width - 3 * own))[None, :]
    packet = jnp.concatenate([pooled_grad, count_row], axis=0)
    below, above = shifted(packet, 1), shifted(packet, -1)
    below_two, above_two = shifted(count_row[:, :128], 2), shifted(count_row[:, :128], -2)
    own_counts = counts
    down, up = below[own, : 3 * own].astype(f32), above[own, : 3 * own].astype(f32)
    down_two, up_two = below_two[0, : 3 * own].astype(f32), above_two[0, : 3 * own].astype(f32)
    low, mid, top = slice(0, own), slice(own, 2 * own), slice(2 * own, 3 * own)
    all_counts = jnp.concatenate(
        [
            down_two[top] + down[mid] + own_counts[low],
            down[top] + own_counts[mid] + up[low],
            own_counts[top] + up[mid] + up_two[low],
        ]
    )
    roots = jnp.sqrt(all_counts)
    table = jnp.concatenate([below[:own], pooled_grad, above[:own]], axis=0).astype(f32)
    table = (table / roots[:, None]).astype(bf16)
    table = jnp.pad(table, ((0, SLOTS - 3 * own), (0, 0)))

    mine = gathered(lax.dynamic_slice_in_dim(encoded, core * half, half, 1))
    other = swap(mine)
    block = pattern[0]
    along_x = block % SIZES["x"]
    along_z = (block // SIZES["x"]) % depth
    along_y = block // (SIZES["x"] * depth)
    place = (along_y * SIZES["x"] + along_x) * depth + along_z
    rows = (
        place[:, None] * GAUGE_ROWS + jnp.arange(GAUGE_ROWS, dtype=jnp.int32)[None, :]
    ).reshape(1, KEYS)

    gauges = mine.shape[0]
    payload = gauges + 4 * width
    vmem = pl.BlockSpec(memory_space=pltpu.VMEM)
    grad_cells, sums, keep, send = pl.pallas_call(
        group_kernel,
        out_shape=(
            jax.ShapeDtypeStruct(cells.shape, bf16),
            jax.ShapeDtypeStruct((SLOTS, width), f32),
            jax.ShapeDtypeStruct((payload, half), bf16),
            jax.ShapeDtypeStruct((payload, half), bf16),
        ),
        in_specs=[pl.BlockSpec(memory_space=pltpu.SMEM)] + [vmem] * 10,
        out_specs=(vmem,) * 4,
        compiler_params=pltpu.CompilerParams(vmem_limit_bytes=48 << 20),
        name="group_kernel",
    )(
        core.reshape(1), rows, slot[None, :], table, mine, other, cells,
        w_query, w_key, w_value, w_out,
    )

    from_above, from_below = shifted(sums[low], -1), shifted(sums[top], 1)
    pooled = ((sums[mid] + from_above + from_below) / roots[mid][:, None]).astype(bf16)

    chip = (keep.astype(f32) + swap(send).astype(f32)).astype(bf16)
    chunk = payload // plane
    gauge_chunk = gauges // plane
    weight_chunk = chunk - gauge_chunk
    parts = lax.all_to_all(chip, PLANE, 0, 0, tiled=True).reshape(plane, chunk, half)
    column = jnp.sum(parts.astype(f32), axis=0).astype(bf16)
    column = jnp.concatenate(
        [
            column[:weight_chunk].reshape(depth, weight_chunk // depth, half),
            column[weight_chunk:].reshape(depth, gauge_chunk // depth, half),
        ],
        axis=1,
    )
    parts = lax.all_to_all(column, "z", 0, 0, tiled=True)
    reduced = jnp.sum(parts.astype(f32), axis=0).astype(bf16)
    own_weight = reduced[: weight_chunk // depth]
    own_gauge = reduced[weight_chunk // depth :]

    weights = gathered(own_weight)
    both = jnp.concatenate([weights, own_gauge], axis=0)
    far = swap(both)
    full = jnp.where(
        core == 0,
        jnp.concatenate([both, far], axis=1),
        jnp.concatenate([far, both], axis=1),
    )
    grads = [full[i * width : (i + 1) * width].astype(f32) for i in range(4)]
    grad_gauges = full[4 * width :]
    return (pooled, grad_cells, grad_gauges, grads[0], grads[1], grads[2], grads[3])


def solution(mesh):
    grid = Mesh(mesh.devices.reshape(tuple(SIZES[a] for a in EVERY)), EVERY)
    tiles = ("y", "z", "x")
    return jax.shard_map(
        per_device,
        mesh=grid,
        in_specs=(
            P(EVERY, None), P(tiles, None), P(), P(), P(), P(),
            P(EVERY, None), P(EVERY), P(EVERY, None),
        ),
        out_specs=(P(EVERY, None), P(EVERY, None), P(tiles, None), P(), P(), P(), P()),
        check_vma=False,
    )
```

time: 1130 us -> 144 us (0.13)
  the two profiles are of different devices: /device:TPU:1 before, /device:TPU:0 now
where the time goes in v1:
time: 144 us
  blocking collectives  48.2 us (33%)
  waiting for transfers between devices  45.6 us (32%)
  starting transfers between devices  28.1 us (20%)
  other arithmetic  9.48 us (7%)
  Pallas kernels  6.26 us (4%)
  local copies, waits for them, and re-layouts  5.37 us (4%)
    all_to_all x3, waiting for transfers between devices, spread(): return lax.all_to_all(copies, axes, 0, 0, tiled=True)  33.4 us
    all_to_all x1, blocking collectives, per_device(): lax.all_to_all(chip, PLANE, 0, 0, tiled=True).reshape(plane, chunk, half)  26.3 us
    ppermute x6, starting transfers between devices, shifted(): lax.ppermute(value, EVERY, [(i, (i + steps) % count) for i in range(count)])  16 us
    all_to_all x1, blocking collectives, per_device(): parts = lax.all_to_all(column, 'z', 0, 0, tiled=True)  11.1 us
    all_to_all x1, blocking collectives, spread(): return lax.all_to_all(copies, axes, 0, 0, tiled=True)  10.8 us
    all_to_all x3, starting transfers between devices, spread(): return lax.all_to_all(copies, axes, 0, 0, tiled=True)  10.6 us
    ppermute x6, waiting for transfers between devices, shifted(): lax.ppermute(value, EVERY, [(i, (i + steps) % count) for i in range(count)])  8.4 us
    pallas_call x1, Pallas kernels, per_device(): pl.pallas_call(group_kernel, out_shape=(jax.ShapeDtypeStruct(cells.shape,...  6.26 us
  transfers between devices with their start and end apart: 12, of which 7 were waited for; matrix products, arithmetic and copies ran while one was open for 3% of the time, Pallas kernels for 0%

profile of v1, /device:TPU:0, one launch (start us, length us, event | category | flops | bytes accessed | tf_op | source)
XLA Modules:
  0.0 143.9 jit_solution(6479743866623960057)
XLA Ops:
  0.7 0.8 and_select_fusion
  1.7 8.8 %collective-permute-start.3 = (bf16[1,128]{1,0:T(2,128)(2,1)S(1)}, bf16[1,128]{1,0:T(2,128)(2,1)S(1)}, u32[]{:S(2)}, u32[]{:S(2)}) collective-permute-start(bf16[1,128]{1,0:T(2,128)(2,1)S(1)} %slice.142), channel_id=1, source_target_pairs={{0,254},{1,255},{2,0},{3,1},{4,2},{5,3},{6,4},{7,5},{8,6},{9,7},{1... | collective-permute-start | bytes 776 | tf_op jit(solution)/shard_map/ppermute | solution.py:168
  10.5 0.7 pad_maximum_fusion.2
  11.2 6.3 %collective-permute-start.1 = (bf16[3,512]{1,0:T(4,128)(2,1)S(1)}, bf16[3,512]{1,0:T(4,128)(2,1)S(1)}, u32[]{:S(2)}, u32[]{:S(2)}) collective-permute-start(bf16[3,512]{1,0:T(4,128)(2,1)S(1)} %pad_maximum_fusion.2), channel_id=1, source_target_pairs={{0,255},{1,0},{2,1},{3,2},{4,3},{5,4},{6,5},{7,6},{8,7},{9,8},{10,... | collective-permute-start | bytes 9224 | tf_op jit(solution)/shard_map/ppermute | solution.py:168
  17.5 0.6 broadcast_in_dim.18
  18.2 3.3 %all-to-all-start = ((bf16[8,8,256]{2,1,0:T(8,128)(2,1)}), bf16[8,8,256]{2,1,0:T(8,128)(2,1)S(1)}, u32[]{:S(2)}, u32[]{:S(2)}) async-start(bf16[8,8,256]{2,1,0:T(8,128)(2,1)} %broadcast_in_dim.18), calls=%async_computation | async-start | bytes 65536 | tf_op jit(solution)/shard_map/all_to_all | solution.py:174
  21.5 0.7 fusion.5
  22.2 7.3 %all-to-all-done = bf16[8,8,256]{2,1,0:T(8,128)(2,1)S(1)} async-done(((bf16[8,8,256]{2,1,0:T(8,128)(2,1)}), bf16[8,8,256]{2,1,0:T(8,128)(2,1)S(1)}, u32[]{:S(2)}, u32[]{:S(2)}) %all-to-all-start) | async-done | bytes 32800 | tf_op jit(solution)/shard_map/all_to_all | solution.py:174
  29.4 0.8 broadcast_in_dim.20
  30.3 3.6 %all-to-all-start.1 = ((bf16[16,64,256]{2,1,0:T(8,128)(2,1)}), bf16[16,64,256]{2,1,0:T(8,128)(2,1)S(1)}, u32[]{:S(2)}, u32[]{:S(2)}) async-start(bf16[16,64,256]{2,1,0:T(8,128)(2,1)} %broadcast_in_dim.20), calls=%async_computation.1 | async-start | bytes 1048576 | tf_op jit(solution)/shard_map/all_to_all | solution.py:174
  34.1 11.4 %all-to-all-done.1 = bf16[16,64,256]{2,1,0:T(8,128)(2,1)S(1)} async-done(((bf16[16,64,256]{2,1,0:T(8,128)(2,1)}), bf16[16,64,256]{2,1,0:T(8,128)(2,1)S(1)}, u32[]{:S(2)}, u32[]{:S(2)}) %all-to-all-start.1) | async-done | bytes 524320 | tf_op jit(solution)/shard_map/all_to_all | solution.py:174
  45.5 1.1 collective-permute-start.4
  46.8 0.8 divide_convert_fusion
  47.5 0.6 collective-permute-done.4.other_ref
  48.2 1.0 copy-done.4
  49.2 0.9 copy-done.5
  50.1 6.3 %group_kernel.1 = (bf16[256,512]{1,0:T(8,128)(2,1)}, f32[16,512]{1,0:T(8,128)S(1)}, bf16[3072,256]{1,0:T(8,128)(2,1)S(1)}, bf16[3072,256]{1,0:T(8,128)(2,1)}) custom-call(s32[1]{0:T(128)} %bitcast.core_ref, s32[1,128]{1,0:T(1,128)S(1)} %add.130.rows_ref, s32[1,256]{1,0:T(1,128)S(1)} %bitcast.45, bf16[16,512]{1,0:T(8,128)(2,1)S(1)} %pad.9.table_ref, ...), custom_call_target="tpu_custom_call" | custom-call | tf_op jit(solution)/shard_map/group_kernel/pallas_call | solution.py:229
  56.8 3.2 %collective-permute-done.7 = bf16[3072,256]{1,0:T(8,128)(2,1)S(1)} collective-permute-done((bf16[3072,256]{1,0:T(8,128)(2,1)}, bf16[3072,256]{1,0:T(8,128)(2,1)S(1)}, u32[]{:S(2)}, u32[]{:S(2)}) %collective-permute-start.7) | collective-permute-done | bytes 1572896 | tf_op jit(solution)/shard_map/ppermute | solution.py:163
  60.5 26.3 %all_to_all.43 = bf16[16,192,256]{2,1,0:T(8,128)(2,1)S(1)} all-to-all(bf16[16,192,256]{2,1,0:T(8,128)(2,1)S(1)} %bitcast.48), channel_id=1, replica_groups=mesh['y'=4,'z'=8,'x'=4,'c'=2] {'y','x'}, dimensions={0} | all-to-all | bytes 3145728 | tf_op jit(solution)/shard_map/all_to_all | solution.py:253
  87.1 11.1 %all_to_all.44 = bf16[8,24,256]{2,1,0:T(8,128)(2,1)S(1)} all-to-all(bf16[8,24,256]{2,1,0:T(8,128)(2,1)S(1)} %pad_maximum_fusion.1), channel_id=1, replica_groups=mesh['y'=4,'z'=8,'x'=4,'c'=2] {'z'}, dimensions={0} | all-to-all | bytes 196608 | tf_op jit(solution)/shard_map/all_to_all | solution.py:262
  98.3 10.8 %all_to_all.45 = bf16[8,16,256]{2,1,0:T(8,128)(2,1)S(1)} all-to-all(bf16[8,16,256]{2,1,0:T(8,128)(2,1)S(1)} %broadcast_in_dim.21), channel_id=1, replica_groups=mesh['y'=4,'z'=8,'x'=4,'c'=2] {'z'}, dimensions={0} | all-to-all | bytes 131072 | tf_op jit(solution)/shard_map/all_to_all | solution.py:174
  109.0 1.1 broadcast_in_dim.23
  110.1 3.7 %all-to-all-start.5 = ((bf16[16,128,256]{2,1,0:T(8,128)(2,1)}), bf16[16,128,256]{2,1,0:T(8,128)(2,1)S(1)}, u32[]{:S(2)}, u32[]{:S(2)}) async-start(bf16[16,128,256]{2,1,0:T(8,128)(2,1)} %broadcast_in_dim.23), calls=%async_computation.5 | async-start | bytes 2097152 | tf_op jit(solution)/shard_map/all_to_all | solution.py:174
  113.8 14.7 %all-to-all-done.5 = bf16[16,128,256]{2,1,0:T(8,128)(2,1)S(1)} async-done(((bf16[16,128,256]{2,1,0:T(8,128)(2,1)}), bf16[16,128,256]{2,1,0:T(8,128)(2,1)S(1)}, u32[]{:S(2)}, u32[]{:S(2)}) %all-to-all-start.5) | async-done | bytes 1048608 | tf_op jit(solution)/shard_map/all_to_all | solution.py:174
  128.5 1.0 pad_maximum_fusion
  129.6 0.8 collective-permute-start.5
  130.4 1.3 collective-permute-done.5
  131.7 7.1 %collective-permute-done.6 = f32[2,512]{1,0:T(2,128)S(1)} collective-permute-done((f32[2,512]{1,0:T(2,128)S(1)}, f32[2,512]{1,0:T(2,128)S(1)}, u32[]{:S(2)}, u32[]{:S(2)}) %collective-permute-start.6) | collective-permute-done | bytes 4128 | tf_op jit(solution)/shard_map/ppermute | solution.py:168
  138.8 0.7 fusion
  139.5 1.5 %maximum_select_fusion = bf16[2056,512]{1,0:T(8,128)(2,1)S(1)} fusion(bf16[2056,256]{1,0:T(8,128)(2,1)S(1)} %collective-permute-done.8, bf16[8,256]{1,0:T(8,128)(2,1)S(1)} %slice.148, bf16[2048,256]{1,0:T(8,128)(2,1)S(1)} %bitcast.47, pred[]{:T(512)S(6)} %eq.24), kind=kLoop, calls=%fused_computation.1 | loop fusion | flops 13684736 | bytes 4210689 | tf_op jit(solution)/shard_map/jit(_where)/select_n | solution.py:270
  141.0 0.6 slice.149
  141.6 2.2 %slice_convert_fusion = (f32[512,512]{1,0:T(8,128)}, f32[512,512]{1,0:T(8,128)}, f32[512,512]{1,0:T(8,128)}, f32[512,512]{1,0:T(8,128)}) fusion(bf16[2056,512]{1,0:T(8,128)(2,1)S(1)} %maximum_select_fusion), kind=kLoop, calls=%fused_computation.3 | loop fusion | flops 1048576 | bytes 6291456 | tf_op jit(solution)/shard_map/convert_element_type | solution.py:275
  (46 shorter events, 1.7 us)
Async XLA Ops:
  0.6 16.9 %copy-start = (bf16[8,512]{1,0:T(8,128)(2,1)S(1)}, bf16[8,512]{1,0:T(8,128)(2,1)}, u32[]{:S(2)}) copy-start(bf16[8,512]{1,0:T(8,128)(2,1)} %param.10) | copy-start | bytes 24580
  0.6 47.5 %copy-start.3 = (bf16[512,512]{1,0:T(8,128)(2,1)S(1)}, bf16[512,512]{1,0:T(8,128)(2,1)}, u32[]{:S(2)}) copy-start(bf16[512,512]{1,0:T(8,128)(2,1)} %wv_ref.1) | copy-start | bytes 1572868
  0.7 47.5 %copy-start.2 = (bf16[512,512]{1,0:T(8,128)(2,1)S(1)}, bf16[512,512]{1,0:T(8,128)(2,1)}, u32[]{:S(2)}) copy-start(bf16[512,512]{1,0:T(8,128)(2,1)} %wk_ref.1) | copy-start | bytes 1572868
  0.7 47.5 %copy-start.1 = (bf16[512,512]{1,0:T(8,128)(2,1)S(1)}, bf16[512,512]{1,0:T(8,128)(2,1)}, u32[]{:S(2)}) copy-start(bf16[512,512]{1,0:T(8,128)(2,1)} %wq_ref.1) | copy-start | bytes 1572868
  1.7 45.0 %collective-permute-start.3 = (bf16[1,128]{1,0:T(2,128)(2,1)S(1)}, bf16[1,128]{1,0:T(2,128)(2,1)S(1)}, u32[]{:S(2)}, u32[]{:S(2)}) collective-permute-start(bf16[1,128]{1,0:T(2,128)(2,1)S(1)} %slice.142), channel_id=1, source_target_pairs={{0,254},{1,255},{2,0},{3,1},{4,2},{5,3},{6,4},{7,5},{8,6},{9,7},{1... | collective-permute-start | bytes 776 | tf_op jit(solution)/shard_map/ppermute | solution.py:168
  10.5 36.1 %collective-permute-start.2 = (bf16[1,128]{1,0:T(2,128)(2,1)S(1)}, bf16[1,128]{1,0:T(2,128)(2,1)S(1)}, u32[]{:S(2)}, u32[]{:S(2)}) collective-permute-start(bf16[1,128]{1,0:T(2,128)(2,1)S(1)} %slice.142), channel_id=1, source_target_pairs={{0,2},{1,3},{2,4},{3,5},{4,6},{5,7},{6,8},{7,9},{8,10},{9,11},{10,... | collective-permute-start | bytes 776 | tf_op jit(solution)/shard_map/ppermute | solution.py:168
  11.2 22.8 %collective-permute-start.1 = (bf16[3,512]{1,0:T(4,128)(2,1)S(1)}, bf16[3,512]{1,0:T(4,128)(2,1)S(1)}, u32[]{:S(2)}, u32[]{:S(2)}) collective-permute-start(bf16[3,512]{1,0:T(4,128)(2,1)S(1)} %pad_maximum_fusion.2), channel_id=1, source_target_pairs={{0,255},{1,0},{2,1},{3,2},{4,3},{5,4},{6,5},{7,6},{8,7},{9,8},{10,... | collective-permute-start | bytes 9224 | tf_op jit(solution)/shard_map/ppermute | solution.py:168
  17.5 16.5 %collective-permute-start = (bf16[3,512]{1,0:T(4,128)(2,1)S(1)}, bf16[3,512]{1,0:T(4,128)(2,1)S(1)}, u32[]{:S(2)}, u32[]{:S(2)}) collective-permute-start(bf16[3,512]{1,0:T(4,128)(2,1)S(1)} %pad_maximum_fusion.2), channel_id=1, source_target_pairs={{0,1},{1,2},{2,3},{3,4},{4,5},{5,6},{6,7},{7,8},{8,9},{9,10},{10,1... | collective-permute-start | bytes 9224 | tf_op jit(solution)/shard_map/ppermute | solution.py:168
  18.2 11.3 %all-to-all-start = ((bf16[8,8,256]{2,1,0:T(8,128)(2,1)}), bf16[8,8,256]{2,1,0:T(8,128)(2,1)S(1)}, u32[]{:S(2)}, u32[]{:S(2)}) async-start(bf16[8,8,256]{2,1,0:T(8,128)(2,1)} %broadcast_in_dim.18), calls=%async_computation | async-start | bytes 65536 | tf_op jit(solution)/shard_map/all_to_all | solution.py:174
  30.3 15.2 %all-to-all-start.1 = ((bf16[16,64,256]{2,1,0:T(8,128)(2,1)}), bf16[16,64,256]{2,1,0:T(8,128)(2,1)S(1)}, u32[]{:S(2)}, u32[]{:S(2)}) async-start(bf16[16,64,256]{2,1,0:T(8,128)(2,1)} %broadcast_in_dim.20), calls=%async_computation.1 | async-start | bytes 1048576 | tf_op jit(solution)/shard_map/all_to_all | solution.py:174
  45.5 2.7 %collective-permute-start.4 = (bf16[1024,256]{1,0:T(8,128)(2,1)S(1)}, bf16[1024,256]{1,0:T(8,128)(2,1)S(1)}, u32[]{:S(2)}, u32[]{:S(2)}) collective-permute-start(bf16[1024,256]{1,0:T(8,128)(2,1)S(1)} %bitcast.43), channel_id=1, source_target_pairs={{0,1},{1,0},{2,3},{3,2},{4,5},{5,4},{6,7},{7,6},{8,9},{9,8},{10,11... | collective-permute-start | bytes 1572872 | tf_op jit(solution)/shard_map/ppermute | solution.py:163
  48.2 1.0 copy-start.4
  49.2 0.9 copy-start.5
  56.4 3.6 %collective-permute-start.7 = (bf16[3072,256]{1,0:T(8,128)(2,1)}, bf16[3072,256]{1,0:T(8,128)(2,1)S(1)}, u32[]{:S(2)}, u32[]{:S(2)}) collective-permute-start(bf16[3072,256]{1,0:T(8,128)(2,1)} %get-tuple-element.14), channel_id=1, source_target_pairs={{0,1},{1,0},{2,3},{3,2},{4,5},{5,4},{6,7},{7,6},{8,9},{9,8},{10,11... | collective-permute-start | bytes 4718600 | tf_op jit(solution)/shard_map/ppermute | solution.py:163
  110.1 18.4 %all-to-all-start.5 = ((bf16[16,128,256]{2,1,0:T(8,128)(2,1)}), bf16[16,128,256]{2,1,0:T(8,128)(2,1)S(1)}, u32[]{:S(2)}, u32[]{:S(2)}) async-start(bf16[16,128,256]{2,1,0:T(8,128)(2,1)} %broadcast_in_dim.23), calls=%async_computation.5 | async-start | bytes 2097152 | tf_op jit(solution)/shard_map/all_to_all | solution.py:174
  129.5 9.9 %collective-permute-start.8 = (bf16[2056,256]{1,0:T(8,128)(2,1)}, bf16[2056,256]{1,0:T(8,128)(2,1)S(1)}, u32[]{:S(2)}, u32[]{:S(2)}) collective-permute-start(bf16[2056,256]{1,0:T(8,128)(2,1)} %pad_maximum_fusion), channel_id=1, source_target_pairs={{0,1},{1,0},{2,3},{3,2},{4,5},{5,4},{6,7},{7,6},{8,9},{9,8},{10,11... | collective-permute-start | bytes 3158024 | tf_op jit(solution)/shard_map/ppermute | solution.py:163
  129.6 2.1 %collective-permute-start.5 = (f32[2,512]{1,0:T(2,128)S(1)}, f32[2,512]{1,0:T(2,128)S(1)}, u32[]{:S(2)}, u32[]{:S(2)}) collective-permute-start(f32[2,512]{1,0:T(2,128)S(1)} %get-tuple-element.19), channel_id=1, source_target_pairs={{0,255},{1,0},{2,1},{3,2},{4,3},{5,4},{6,5},{7,6},{8,7},{9,8},{10,... | collective-permute-start | bytes 12296 | tf_op jit(solution)/shard_map/ppermute | solution.py:168
  130.4 8.5 %collective-permute-start.6 = (f32[2,512]{1,0:T(2,128)S(1)}, f32[2,512]{1,0:T(2,128)S(1)}, u32[]{:S(2)}, u32[]{:S(2)}) collective-permute-start(f32[2,512]{1,0:T(2,128)S(1)} %get-tuple-element.20), channel_id=1, source_target_pairs={{0,1},{1,2},{2,3},{3,4},{4,5},{5,6},{6,7},{7,8},{8,9},{9,10},{10,1... | collective-permute-start | bytes 12296 | tf_op jit(solution)/shard_map/ppermute | solution.py:168

commit v2 on v1

--- a/solution.py
+++ b/solution.py
@@ -43,10 +43,15 @@
 
 
 def group_kernel(
-    core_ref, rows_ref, slot_ref, table_ref, mine_ref, other_ref, cells_ref,
-    wq_ref, wk_ref, wv_ref, wo_ref,
+    core_ref, rows_ref, places_ref, slot_ref, table_ref, mine_ref, other_ref,
+    wk_ref, wv_ref, wq_ref, cells_hbm, wo_hbm,
     grad_cells_ref, sums_ref, keep_ref, send_ref,
+    cells_ref, wo_ref, sems,
 ):
+    load_cells = pltpu.make_async_copy(cells_hbm, cells_ref, sems.at[0])
+    load_wo = pltpu.make_async_copy(wo_hbm, wo_ref, sems.at[1])
+    load_cells.start()
+    load_wo.start()
     core = core_ref[0]
     first = core == 0
     width = 2 * mine_ref.shape[1]
@@ -72,9 +77,8 @@
                 value[j * weight_chunk : (j + 1) * weight_chunk, :],
             )
 
-    picks = jnp.where(
-        lax.broadcasted_iota(jnp.int32, (gauges, KEYS), 0) == rows_ref[...], 1.0, 0.0
-    ).astype(bf16)
+    gauge_ids = lax.broadcasted_iota(jnp.int32, (gauges, KEYS), 0)
+    picks = jnp.where(gauge_ids == rows_ref[...], 1.0, 0.0).astype(bf16)
     sel_mine = mm_rows(picks, mine_ref[...])
     sel_other = mm_rows(picks, other_ref[...])
     encoded_sel = jnp.concatenate(
@@ -82,6 +86,7 @@
     ).astype(bf16)
     keys = mm(encoded_sel, wk_ref[...]).astype(bf16)
     values = mm(encoded_sel, wv_ref[...]).astype(bf16)
+    load_cells.wait()
     queries = mm(cells_ref[...], wq_ref[...]).astype(bf16)
     even = lax.broadcasted_iota(jnp.int32, (KEYS, PAIR), 1) < HEAD_DIM
     zero = jnp.zeros((KEYS, PAIR), bf16)
@@ -111,6 +116,7 @@
         attended.append(mm(weights_bf, value_two).astype(bf16))
         saved.append((key_two, value_two, query_pair, tanh_val, weights, weights_bf))
     attended = jnp.concatenate(attended, axis=1)
+    load_wo.wait()
     cell_out = mm(attended, wo_ref[...]).astype(bf16)
     onehot = jnp.where(
         lax.broadcasted_iota(jnp.int32, (SLOTS, cell_out.shape[0]), 0) == slot_ref[...], 1.0, 0.0
@@ -152,11 +158,21 @@
         + mm_cols(value_high, wv_ref[...])
         + mm_cols(value_low, wv_ref[...])
     ).astype(bf16)
+    places = jnp.where(gauge_ids == places_ref[...], 1.0, 0.0).astype(bf16)
     for j in range(plane):
         store(
             j * chunk + weight_chunk,
-            mm(picks[j * gauge_chunk : (j + 1) * gauge_chunk, :], grad_gauges),
+            mm(places[j * gauge_chunk : (j + 1) * gauge_chunk, :], grad_gauges),
         )
+
+
+def widen_kernel(core_ref, mine_ref, far_ref, *out_refs):
+    first = core_ref[0] == 0
+    half = mine_ref.shape[2]
+    for i, out_ref in enumerate(out_refs):
+        mine, far = mine_ref[i], far_ref[i]
+        out_ref[:, :half] = jnp.where(first, mine, far).astype(f32)
+        out_ref[:, half:] = jnp.where(first, far, mine).astype(f32)
 
 
 def swap(value):
@@ -174,9 +190,8 @@
     return lax.all_to_all(copies, axes, 0, 0, tiled=True)
 
 
-def gathered(value):
-    column = spread(value, "z", SIZES["z"])
-    return spread(column, PLANE, SIZES["y"] * SIZES["x"])
+def after(value, *others):
+    return lax.optimization_barrier((value,) + others)[0]
 
 
 def per_device(cells, encoded, w_query, w_key, w_value, w_out, pattern, cell_basin, pooled_grad):
@@ -188,14 +203,22 @@
     own = pooled_grad.shape[0]
     total = own * lax.axis_size(EVERY)
 
+    tiles = ("y", "z", "x")
+    rows_own = lax.dynamic_slice_in_dim(encoded, core * half, half, 1)
+    copies = jnp.broadcast_to(rows_own[None], (plane * depth,) + rows_own.shape)
+    copies = copies.reshape(plane * depth * rows_own.shape[0], half)
+    mine = lax.all_to_all(copies, tiles, 0, 0, tiled=True)
+    other = swap(mine)
+
     slot = (cell_basin - device * own + own) % total
     counts = jnp.sum(
         (slot[None, :] == jnp.arange(3 * own, dtype=jnp.int32)[:, None]).astype(f32), axis=1
     )
     count_row = jnp.pad(counts.astype(bf16), (0, width - 3 * own))[None, :]
-    packet = jnp.concatenate([pooled_grad, count_row], axis=0)
+    packet = after(jnp.concatenate([pooled_grad, count_row], axis=0), copies)
+    small = packet[own:, :128]
     below, above = shifted(packet, 1), shifted(packet, -1)
-    below_two, above_two = shifted(count_row[:, :128], 2), shifted(count_row[:, :128], -2)
+    below_two, above_two = shifted(small, 2), shifted(small, -2)
     own_counts = counts
     down, up = below[own, : 3 * own].astype(f32), above[own, : 3 * own].astype(f32)
     down_two, up_two = below_two[0, : 3 * own].astype(f32), above_two[0, : 3 * own].astype(f32)
@@ -212,20 +235,20 @@
     table = (table / roots[:, None]).astype(bf16)
     table = jnp.pad(table, ((0, SLOTS - 3 * own), (0, 0)))
 
-    mine = gathered(lax.dynamic_slice_in_dim(encoded, core * half, half, 1))
-    other = swap(mine)
     block = pattern[0]
     along_x = block % SIZES["x"]
     along_z = (block // SIZES["x"]) % depth
     along_y = block // (SIZES["x"] * depth)
     place = (along_y * SIZES["x"] + along_x) * depth + along_z
-    rows = (
-        place[:, None] * GAUGE_ROWS + jnp.arange(GAUGE_ROWS, dtype=jnp.int32)[None, :]
-    ).reshape(1, KEYS)
+    within = jnp.arange(GAUGE_ROWS, dtype=jnp.int32)[None, :]
+    rows = (block[:, None] * GAUGE_ROWS + within).reshape(1, KEYS)
+    places = (place[:, None] * GAUGE_ROWS + within).reshape(1, KEYS)
 
     gauges = mine.shape[0]
     payload = gauges + 4 * width
     vmem = pl.BlockSpec(memory_space=pltpu.VMEM)
+    smem = pl.BlockSpec(memory_space=pltpu.SMEM)
+    hbm = pl.BlockSpec(memory_space=pltpu.HBM)
     grad_cells, sums, keep, send = pl.pallas_call(
         group_kernel,
         out_shape=(
@@ -234,13 +257,18 @@
             jax.ShapeDtypeStruct((payload, half), bf16),
             jax.ShapeDtypeStruct((payload, half), bf16),
         ),
-        in_specs=[pl.BlockSpec(memory_space=pltpu.SMEM)] + [vmem] * 10,
+        in_specs=[smem] + [vmem] * 9 + [hbm] * 2,
         out_specs=(vmem,) * 4,
+        scratch_shapes=[
+            pltpu.VMEM(cells.shape, bf16),
+            pltpu.VMEM(w_out.shape, bf16),
+            pltpu.SemaphoreType.DMA((2,)),
+        ],
         compiler_params=pltpu.CompilerParams(vmem_limit_bytes=48 << 20),
         name="group_kernel",
     )(
-        core.reshape(1), rows, slot[None, :], table, mine, other, cells,
-        w_query, w_key, w_value, w_out,
+        core.reshape(1), rows, places, slot[None, :], table, mine, other,
+        w_key, w_value, w_query, cells, w_out,
     )
 
     from_above, from_below = shifted(sums[low], -1), shifted(sums[top], 1)
@@ -251,29 +279,40 @@
     gauge_chunk = gauges // plane
     weight_chunk = chunk - gauge_chunk
     parts = lax.all_to_all(chip, PLANE, 0, 0, tiled=True).reshape(plane, chunk, half)
+    parts = after(parts, from_above, from_below)
     column = jnp.sum(parts.astype(f32), axis=0).astype(bf16)
     column = jnp.concatenate(
         [
-            column[:weight_chunk].reshape(depth, weight_chunk // depth, half),
+            jnp.broadcast_to(column[None, :weight_chunk], (depth, weight_chunk, half)),
             column[weight_chunk:].reshape(depth, gauge_chunk // depth, half),
         ],
         axis=1,
     )
     parts = lax.all_to_all(column, "z", 0, 0, tiled=True)
     reduced = jnp.sum(parts.astype(f32), axis=0).astype(bf16)
-    own_weight = reduced[: weight_chunk // depth]
-    own_gauge = reduced[weight_chunk // depth :]
-
-    weights = gathered(own_weight)
-    both = jnp.concatenate([weights, own_gauge], axis=0)
-    far = swap(both)
-    full = jnp.where(
+    own_gauge = reduced[weight_chunk:]
+    far_gauge = swap(own_gauge)
+    grad_gauges = jnp.where(
         core == 0,
-        jnp.concatenate([both, far], axis=1),
-        jnp.concatenate([far, both], axis=1),
-    )
-    grads = [full[i * width : (i + 1) * width].astype(f32) for i in range(4)]
-    grad_gauges = full[4 * width :]
+        jnp.concatenate([own_gauge, far_gauge], axis=1),
+        jnp.concatenate([far_gauge, own_gauge], axis=1),
+    )
+
+    weights = spread(reduced[:weight_chunk], PLANE, plane)
+    weights = after(weights, far_gauge)
+    far = swap(weights)
+    steps = 4
+    block_in = pl.BlockSpec((4, width // steps, half), lambda i: (0, i, 0))
+    block_out = pl.BlockSpec((width // steps, width), lambda i: (i, 0))
+    grads = pl.pallas_call(
+        widen_kernel,
+        out_shape=(jax.ShapeDtypeStruct((width, width), f32),) * 4,
+        grid=(steps,),
+        in_specs=[smem, block_in, block_in],
+        out_specs=(block_out,) * 4,
+        compiler_params=pltpu.CompilerParams(vmem_limit_bytes=48 << 20),
+        name="widen_kernel",
+    )(core.reshape(1), weights.reshape(4, width, half), far.reshape(4, width, half))
     return (pooled, grad_cells, grad_gauges, grads[0], grads[1], grads[2], grads[3])
 
 

time: 144 us -> 135 us (0.938)
  the two profiles are of different devices: /device:TPU:0 before, /device:TPU:1 now
where the time goes in v2:
time: 135 us; the launch traced here: 134 us
  waiting for transfers between devices  50.3 us (37%)
  starting transfers between devices  47 us (35%)
  blocking collectives  18.5 us (14%)
  Pallas kernels  9.09 us (7%)
  local copies, waits for them, and re-layouts  4.89 us (4%)
  other arithmetic  3.72 us (3%)
    ppermute x6, waiting for transfers between devices, shifted(): lax.ppermute(value, EVERY, [(i, (i + steps) % count) for i in range(count)])  25.8 us
    all_to_all x1, blocking collectives, per_device(): parts = lax.all_to_all(column, 'z', 0, 0, tiled=True)  18.5 us
    all_to_all x1, starting transfers between devices, per_device(): mine = lax.all_to_all(copies, tiles, 0, 0, tiled=True)  16.3 us
    all_to_all x1, waiting for transfers between devices, spread(): return lax.all_to_all(copies, axes, 0, 0, tiled=True)  13.3 us
    ppermute x4, starting transfers between devices, swap(): return lax.ppermute(value, 'c', [(0, 1), (1, 0)])  10.9 us
    ppermute x6, starting transfers between devices, shifted(): lax.ppermute(value, EVERY, [(i, (i + steps) % count) for i in range(count)])  10.7 us
    pallas_call x1, Pallas kernels, per_device(): pl.pallas_call(group_kernel, out_shape=(jax.ShapeDtypeStruct(cells.shape,...  6.64 us
    ppermute x4, waiting for transfers between devices, swap(): return lax.ppermute(value, 'c', [(0, 1), (1, 0)])  6.31 us
  transfers between devices with their start and end apart: 13, of which 10 were waited for; matrix products, arithmetic and copies ran while one was open for 2% of the time, Pallas kernels for 0%

profile of v2, /device:TPU:1, one launch (start us, length us, event | category | flops | bytes accessed | tf_op | source)
XLA Modules:
  0.0 134.4 jit_solution(5283238602397448165)
XLA Ops:
  0.7 0.6 copy-done
  1.3 0.8 broadcast_in_dim.12
  2.2 16.3 %all-to-all-start = ((bf16[128,8,256]{2,1,0:T(8,128)(2,1)}), bf16[128,8,256]{2,1,0:T(8,128)(2,1)S(1)}, u32[]{:S(2)}, u32[]{:S(2)}) async-start(bf16[128,8,256]{2,1,0:T(8,128)(2,1)} %broadcast_in_dim.12), calls=%async_computation | async-start | bytes 1048576 | tf_op jit(solution)/shard_map/all_to_all | solution.py:210
  18.7 6.8 %collective-permute-start.3 = (bf16[1,128]{1,0:T(2,128)(2,1)S(1)}, bf16[1,128]{1,0:T(2,128)(2,1)S(1)}, u32[]{:S(2)}, u32[]{:S(2)}) collective-permute-start(bf16[1,128]{1,0:T(2,128)(2,1)S(1)} %slice.121), channel_id=1, source_target_pairs={{0,254},{1,255},{2,0},{3,1},{4,2},{5,3},{6,4},{7,5},{8,6},{9,7},{1... | collective-permute-start | bytes 776 | tf_op jit(solution)/shard_map/ppermute | solution.py:184
  25.6 1.5 %collective-permute-start.1 = (bf16[3,512]{1,0:T(4,128)(2,1)S(1)}, bf16[3,512]{1,0:T(4,128)(2,1)S(1)}, u32[]{:S(2)}, u32[]{:S(2)}) collective-permute-start(bf16[3,512]{1,0:T(4,128)(2,1)S(1)} %pad_maximum_fusion.1), channel_id=1, source_target_pairs={{0,255},{1,0},{2,1},{3,2},{4,3},{5,4},{6,5},{7,6},{8,7},{9,8},{10,... | collective-permute-start | bytes 9224 | tf_op jit(solution)/shard_map/ppermute | solution.py:184
  27.6 1.3 collective-permute-done.1
  28.9 4.6 %collective-permute-done = bf16[3,512]{1,0:T(4,128)(2,1)S(1)} collective-permute-done((bf16[3,512]{1,0:T(4,128)(2,1)S(1)}, bf16[3,512]{1,0:T(4,128)(2,1)S(1)}, u32[]{:S(2)}, u32[]{:S(2)}) %collective-permute-start) | collective-permute-done | bytes 3104 | tf_op jit(solution)/shard_map/ppermute | solution.py:184
  33.5 1.8 %all-to-all-done = bf16[128,8,256]{2,1,0:T(8,128)(2,1)S(1)} async-done(((bf16[128,8,256]{2,1,0:T(8,128)(2,1)}), bf16[128,8,256]{2,1,0:T(8,128)(2,1)S(1)}, u32[]{:S(2)}, u32[]{:S(2)}) %all-to-all-start) | async-done | bytes 524320 | tf_op jit(solution)/shard_map/all_to_all | solution.py:210
  35.4 6.1 %collective-permute-start.4 = (bf16[1024,256]{1,0:T(8,128)(2,1)S(1)}, bf16[1024,256]{1,0:T(8,128)(2,1)S(1)}, u32[]{:S(2)}, u32[]{:S(2)}) collective-permute-start(bf16[1024,256]{1,0:T(8,128)(2,1)S(1)} %bitcast.45), channel_id=1, source_target_pairs={{0,1},{1,0},{2,3},{3,2},{4,5},{5,4},{6,7},{7,6},{8,9},{9,8},{10,11... | collective-permute-start | bytes 1572872 | tf_op jit(solution)/shard_map/ppermute | solution.py:179
  41.7 1.3 collective-permute-done.4.other_ref
  43.0 1.0 copy-done.4
  44.0 0.9 copy-done.5
  45.0 6.6 %group_kernel.1 = (bf16[256,512]{1,0:T(8,128)(2,1)}, f32[16,512]{1,0:T(8,128)S(1)}, bf16[3072,256]{1,0:T(8,128)(2,1)S(1)}, bf16[3072,256]{1,0:T(8,128)(2,1)}) custom-call(s32[1]{0:T(128)} %bitcast.core_ref, s32[1,128]{1,0:T(1,128)S(1)} %add.149.rows_ref, s32[1,128]{1,0:T(1,128)S(1)} %add.157.places_ref, s32[1,256]{1,0:T(1,128)S(1)} %bitcast.48, ...), custom_call_target="tpu_custom_call" | custom-call | tf_op jit(solution)/shard_map/group_kernel/pallas_call | solution.py:252
  51.6 0.5 collective-permute-start.7
  52.1 3.3 %collective-permute-done.7 = bf16[3072,256]{1,0:T(8,128)(2,1)S(1)} collective-permute-done((bf16[3072,256]{1,0:T(8,128)(2,1)}, bf16[3072,256]{1,0:T(8,128)(2,1)S(1)}, u32[]{:S(2)}, u32[]{:S(2)}) %collective-permute-start.7) | collective-permute-done | bytes 1572896 | tf_op jit(solution)/shard_map/ppermute | solution.py:179
  55.3 1.6 %add_convert_fusion = bf16[3072,256]{1,0:T(8,128)(2,1)} fusion(bf16[3072,256]{1,0:T(8,128)(2,1)S(1)} %collective-permute-done.7, bf16[3072,256]{1,0:T(8,128)(2,1)S(1)} %get-tuple-element.19), kind=kLoop, calls=%fused_computation | loop fusion | flops 3145728 | bytes 4718592 | tf_op jit(solution)/shard_map/convert_element_type | solution.py:277
  57.0 3.7 %all-to-all-start.1 = ((bf16[16,192,256]{2,1,0:T(8,128)(2,1)}), bf16[16,192,256]{2,1,0:T(8,128)(2,1)S(1)}, u32[]{:S(2)}, u32[]{:S(2)}) async-start(bf16[16,192,256]{2,1,0:T(8,128)(2,1)} %bitcast.49), calls=%async_computation.1 | async-start | bytes 3145728 | tf_op jit(solution)/shard_map/all_to_all | solution.py:281
  60.7 0.6 collective-permute-start.5
  61.3 1.5 %collective-permute-start.6 = (f32[2,512]{1,0:T(2,128)S(1)}, f32[2,512]{1,0:T(2,128)S(1)}, u32[]{:S(2)}, u32[]{:S(2)}) collective-permute-start(f32[2,512]{1,0:T(2,128)S(1)} %get-tuple-element.28), channel_id=1, source_target_pairs={{0,1},{1,2},{2,3},{3,4},{4,5},{5,6},{6,7},{7,8},{8,9},{9,10},{10,1... | collective-permute-start | bytes 12296 | tf_op jit(solution)/shard_map/ppermute | solution.py:184
  62.8 19.9 %collective-permute-done.5 = f32[2,512]{1,0:T(2,128)S(1)} collective-permute-done((f32[2,512]{1,0:T(2,128)S(1)}, f32[2,512]{1,0:T(2,128)S(1)}, u32[]{:S(2)}, u32[]{:S(2)}) %collective-permute-start.5) | collective-permute-done | bytes 4128 | tf_op jit(solution)/shard_map/ppermute | solution.py:184
  82.7 3.1 %all-to-all-done.1 = bf16[16,192,256]{2,1,0:T(8,128)(2,1)S(1)} async-done(((bf16[16,192,256]{2,1,0:T(8,128)(2,1)}), bf16[16,192,256]{2,1,0:T(8,128)(2,1)S(1)}, u32[]{:S(2)}, u32[]{:S(2)}) %all-to-all-start.1) | async-done | bytes 1572896 | tf_op jit(solution)/shard_map/all_to_all | solution.py:281
  86.1 18.5 %all_to_all.31 = bf16[8,136,256]{2,1,0:T(8,128)(2,1)S(1)} all-to-all(bf16[8,136,256]{2,1,0:T(8,128)(2,1)S(1)} %pad_maximum_fusion), channel_id=1, replica_groups=mesh['y'=4,'z'=8,'x'=4,'c'=2] {'z'}, dimensions={0} | all-to-all | bytes 1114112 | tf_op jit(solution)/shard_map/all_to_all | solution.py:291
  104.7 1.1 broadcast_in_dim.14
  105.8 5.3 %all-to-all-start.3 = ((bf16[16,128,256]{2,1,0:T(8,128)(2,1)}), bf16[16,128,256]{2,1,0:T(8,128)(2,1)S(1)}, u32[]{:S(2)}, u32[]{:S(2)}) async-start(bf16[16,128,256]{2,1,0:T(8,128)(2,1)} %broadcast_in_dim.14), calls=%async_computation.3 | async-start | bytes 2097152 | tf_op jit(solution)/shard_map/all_to_all | solution.py:190
  111.2 1.4 %collective-permute-start.8 = (bf16[8,256]{1,0:T(8,128)(2,1)S(1)}, bf16[8,256]{1,0:T(8,128)(2,1)S(1)}, u32[]{:S(2)}, u32[]{:S(2)}) collective-permute-start(bf16[8,256]{1,0:T(8,128)(2,1)S(1)} %slice.126), channel_id=1, source_target_pairs={{0,1},{1,0},{2,3},{3,2},{4,5},{5,4},{6,7},{7,6},{8,9},{9,8},{10,11... | collective-permute-start | bytes 12296 | tf_op jit(solution)/shard_map/ppermute | solution.py:179
  112.6 0.8 collective-permute-done.8
  113.4 13.3 %all-to-all-done.3 = bf16[16,128,256]{2,1,0:T(8,128)(2,1)S(1)} async-done(((bf16[16,128,256]{2,1,0:T(8,128)(2,1)}), bf16[16,128,256]{2,1,0:T(8,128)(2,1)S(1)}, u32[]{:S(2)}, u32[]{:S(2)}) %all-to-all-start.3) | async-done | bytes 1048608 | tf_op jit(solution)/shard_map/all_to_all | solution.py:190
  126.8 2.9 %collective-permute-start.9 = (bf16[2048,256]{1,0:T(8,128)(2,1)S(1)}, bf16[2048,256]{1,0:T(8,128)(2,1)S(1)}, u32[]{:S(2)}, u32[]{:S(2)}) collective-permute-start(bf16[2048,256]{1,0:T(8,128)(2,1)S(1)} %bitcast.43), channel_id=1, source_target_pairs={{0,1},{1,0},{2,3},{3,2},{4,5},{5,4},{6,7},{7,6},{8,9},{9,8},{10,11... | collective-permute-start | bytes 3145736 | tf_op jit(solution)/shard_map/ppermute | solution.py:179
  129.8 0.7 fusion
  130.4 0.6 maximum_select_fusion
  131.0 1.0 collective-permute-done.9
  132.0 2.5 %widen_kernel.1 = (f32[512,512]{1,0:T(8,128)}, f32[512,512]{1,0:T(8,128)}, f32[512,512]{1,0:T(8,128)}, f32[512,512]{1,0:T(8,128)}) custom-call(s32[1]{0:T(128)} %bitcast.core_ref, bf16[4,512,256]{2,1,0:T(8,128)(2,1)S(1)} %bitcast.44, bf16[4,512,256]{2,1,0:T(8,128)(2,1)S(1)} %bitcast.47), custom_call_target="tpu_custom_call" | custom-call | tf_op jit(solution)/shard_map/widen_kernel/pallas_call | solution.py:307
  (50 shorter events, 1.4 us)
Async XLA Ops:
  0.6 0.7 copy-start
  0.7 17.9 %copy-start.7 = (s32[256]{0:T(256)S(1)}, s32[256]{0:T(256)}, u32[]{:S(2)}) copy-start(s32[256]{0:T(256)} %param.16) | copy-start | bytes 3076
  0.7 18.0 %copy-start.6 = (bf16[2,512]{1,0:T(2,128)(2,1)S(1)}, bf16[2,512]{1,0:T(2,128)(2,1)}, u32[]{:S(2)}) copy-start(bf16[2,512]{1,0:T(2,128)(2,1)} %param.17) | copy-start | bytes 6148
  0.7 26.7 %copy-start.8 = (s32[1,16]{1,0:T(1,128)S(1)}, s32[1,16]{1,0:T(1,128)}, u32[]{:S(2)}) copy-start(s32[1,16]{1,0:T(1,128)} %param.15) | copy-start | bytes 196
  0.7 42.3 %copy-start.2 = (bf16[512,512]{1,0:T(8,128)(2,1)S(1)}, bf16[512,512]{1,0:T(8,128)(2,1)}, u32[]{:S(2)}) copy-start(bf16[512,512]{1,0:T(8,128)(2,1)} %wv_ref.1) | copy-start | bytes 1572868
  0.7 42.3 %copy-start.1 = (bf16[512,512]{1,0:T(8,128)(2,1)S(1)}, bf16[512,512]{1,0:T(8,128)(2,1)}, u32[]{:S(2)}) copy-start(bf16[512,512]{1,0:T(8,128)(2,1)} %wk_ref.1) | copy-start | bytes 1572868
  0.7 42.3 %copy-start.3 = (bf16[512,512]{1,0:T(8,128)(2,1)S(1)}, bf16[512,512]{1,0:T(8,128)(2,1)}, u32[]{:S(2)}) copy-start(bf16[512,512]{1,0:T(8,128)(2,1)} %wq_ref.1) | copy-start | bytes 1572868
  2.2 33.2 %all-to-all-start = ((bf16[128,8,256]{2,1,0:T(8,128)(2,1)}), bf16[128,8,256]{2,1,0:T(8,128)(2,1)S(1)}, u32[]{:S(2)}, u32[]{:S(2)}) async-start(bf16[128,8,256]{2,1,0:T(8,128)(2,1)} %broadcast_in_dim.12), calls=%async_computation | async-start | bytes 1048576 | tf_op jit(solution)/shard_map/all_to_all | solution.py:210
  18.7 22.7 %collective-permute-start.3 = (bf16[1,128]{1,0:T(2,128)(2,1)S(1)}, bf16[1,128]{1,0:T(2,128)(2,1)S(1)}, u32[]{:S(2)}, u32[]{:S(2)}) collective-permute-start(bf16[1,128]{1,0:T(2,128)(2,1)S(1)} %slice.121), channel_id=1, source_target_pairs={{0,254},{1,255},{2,0},{3,1},{4,2},{5,3},{6,4},{7,5},{8,6},{9,7},{1... | collective-permute-start | bytes 776 | tf_op jit(solution)/shard_map/ppermute | solution.py:184
  25.6 15.9 %collective-permute-start.2 = (bf16[1,128]{1,0:T(2,128)(2,1)S(1)}, bf16[1,128]{1,0:T(2,128)(2,1)S(1)}, u32[]{:S(2)}, u32[]{:S(2)}) collective-permute-start(bf16[1,128]{1,0:T(2,128)(2,1)S(1)} %slice.121), channel_id=1, source_target_pairs={{0,2},{1,3},{2,4},{3,5},{4,6},{5,7},{6,8},{7,9},{8,10},{9,11},{10,... | collective-permute-start | bytes 776 | tf_op jit(solution)/shard_map/ppermute | solution.py:184
  25.6 3.3 %collective-permute-start.1 = (bf16[3,512]{1,0:T(4,128)(2,1)S(1)}, bf16[3,512]{1,0:T(4,128)(2,1)S(1)}, u32[]{:S(2)}, u32[]{:S(2)}) collective-permute-start(bf16[3,512]{1,0:T(4,128)(2,1)S(1)} %pad_maximum_fusion.1), channel_id=1, source_target_pairs={{0,255},{1,0},{2,1},{3,2},{4,3},{5,4},{6,5},{7,6},{8,7},{9,8},{10,... | collective-permute-start | bytes 9224 | tf_op jit(solution)/shard_map/ppermute | solution.py:184
  27.1 6.4 %collective-permute-start = (bf16[3,512]{1,0:T(4,128)(2,1)S(1)}, bf16[3,512]{1,0:T(4,128)(2,1)S(1)}, u32[]{:S(2)}, u32[]{:S(2)}) collective-permute-start(bf16[3,512]{1,0:T(4,128)(2,1)S(1)} %pad_maximum_fusion.1), channel_id=1, source_target_pairs={{0,1},{1,2},{2,3},{3,4},{4,5},{5,6},{6,7},{7,8},{8,9},{9,10},{10,1... | collective-permute-start | bytes 9224 | tf_op jit(solution)/shard_map/ppermute | solution.py:184
  35.4 7.6 %collective-permute-start.4 = (bf16[1024,256]{1,0:T(8,128)(2,1)S(1)}, bf16[1024,256]{1,0:T(8,128)(2,1)S(1)}, u32[]{:S(2)}, u32[]{:S(2)}) collective-permute-start(bf16[1024,256]{1,0:T(8,128)(2,1)S(1)} %bitcast.45), channel_id=1, source_target_pairs={{0,1},{1,0},{2,3},{3,2},{4,5},{5,4},{6,7},{7,6},{8,9},{9,8},{10,11... | collective-permute-start | bytes 1572872 | tf_op jit(solution)/shard_map/ppermute | solution.py:179
  43.0 1.0 copy-start.4
  44.0 0.9 copy-start.5
  51.6 3.7 %collective-permute-start.7 = (bf16[3072,256]{1,0:T(8,128)(2,1)}, bf16[3072,256]{1,0:T(8,128)(2,1)S(1)}, u32[]{:S(2)}, u32[]{:S(2)}) collective-permute-start(bf16[3072,256]{1,0:T(8,128)(2,1)} %get-tuple-element.20), channel_id=1, source_target_pairs={{0,1},{1,0},{2,3},{3,2},{4,5},{5,4},{6,7},{7,6},{8,9},{9,8},{10,11... | collective-permute-start | bytes 4718600 | tf_op jit(solution)/shard_map/ppermute | solution.py:179
  57.0 28.8 %all-to-all-start.1 = ((bf16[16,192,256]{2,1,0:T(8,128)(2,1)}), bf16[16,192,256]{2,1,0:T(8,128)(2,1)S(1)}, u32[]{:S(2)}, u32[]{:S(2)}) async-start(bf16[16,192,256]{2,1,0:T(8,128)(2,1)} %bitcast.49), calls=%async_computation.1 | async-start | bytes 3145728 | tf_op jit(solution)/shard_map/all_to_all | solution.py:281
  60.7 22.0 %collective-permute-start.5 = (f32[2,512]{1,0:T(2,128)S(1)}, f32[2,512]{1,0:T(2,128)S(1)}, u32[]{:S(2)}, u32[]{:S(2)}) collective-permute-start(f32[2,512]{1,0:T(2,128)S(1)} %get-tuple-element.27), channel_id=1, source_target_pairs={{0,255},{1,0},{2,1},{3,2},{4,3},{5,4},{6,5},{7,6},{8,7},{9,8},{10,... | collective-permute-start | bytes 12296 | tf_op jit(solution)/shard_map/ppermute | solution.py:184
  61.3 21.4 %collective-permute-start.6 = (f32[2,512]{1,0:T(2,128)S(1)}, f32[2,512]{1,0:T(2,128)S(1)}, u32[]{:S(2)}, u32[]{:S(2)}) collective-permute-start(f32[2,512]{1,0:T(2,128)S(1)} %get-tuple-element.28), channel_id=1, source_target_pairs={{0,1},{1,2},{2,3},{3,4},{4,5},{5,6},{6,7},{7,8},{8,9},{9,10},{10,1... | collective-permute-start | bytes 12296 | tf_op jit(solution)/shard_map/ppermute | solution.py:184
  105.8 20.9 %all-to-all-start.3 = ((bf16[16,128,256]{2,1,0:T(8,128)(2,1)}), bf16[16,128,256]{2,1,0:T(8,128)(2,1)S(1)}, u32[]{:S(2)}, u32[]{:S(2)}) async-start(bf16[16,128,256]{2,1,0:T(8,128)(2,1)} %broadcast_in_dim.14), calls=%async_computation.3 | async-start | bytes 2097152 | tf_op jit(solution)/shard_map/all_to_all | solution.py:190
  111.2 2.3 %collective-permute-start.8 = (bf16[8,256]{1,0:T(8,128)(2,1)S(1)}, bf16[8,256]{1,0:T(8,128)(2,1)S(1)}, u32[]{:S(2)}, u32[]{:S(2)}) collective-permute-start(bf16[8,256]{1,0:T(8,128)(2,1)S(1)} %slice.126), channel_id=1, source_target_pairs={{0,1},{1,0},{2,3},{3,2},{4,5},{5,4},{6,7},{7,6},{8,9},{9,8},{10,11... | collective-permute-start | bytes 12296 | tf_op jit(solution)/shard_map/ppermute | solution.py:179
  126.8 5.2 %collective-permute-start.9 = (bf16[2048,256]{1,0:T(8,128)(2,1)S(1)}, bf16[2048,256]{1,0:T(8,128)(2,1)S(1)}, u32[]{:S(2)}, u32[]{:S(2)}) collective-permute-start(bf16[2048,256]{1,0:T(8,128)(2,1)S(1)} %bitcast.43), channel_id=1, source_target_pairs={{0,1},{1,0},{2,3},{3,2},{4,5},{5,4},{6,7},{7,6},{8,9},{9,8},{10,11... | collective-permute-start | bytes 3145736 | tf_op jit(solution)/shard_map/ppermute | solution.py:179

commit v3 on v2

--- a/solution.py
+++ b/solution.py
@@ -268,38 +268,41 @@
         name="group_kernel",
     )(
         core.reshape(1), rows, places, slot[None, :], table, mine, other,
-        w_key, w_value, w_query, cells, w_out,
-    )
-
-    from_above, from_below = shifted(sums[low], -1), shifted(sums[top], 1)
-    pooled = ((sums[mid] + from_above + from_below) / roots[mid][:, None]).astype(bf16)
+        w_key, w_value, w_query,
+        pltpu.with_memory_space_constraint(cells, pltpu.HBM),
+        pltpu.with_memory_space_constraint(w_out, pltpu.HBM),
+    )
 
     chip = (keep.astype(f32) + swap(send).astype(f32)).astype(bf16)
     chunk = payload // plane
     gauge_chunk = gauges // plane
     weight_chunk = chunk - gauge_chunk
     parts = lax.all_to_all(chip, PLANE, 0, 0, tiled=True).reshape(plane, chunk, half)
-    parts = after(parts, from_above, from_below)
     column = jnp.sum(parts.astype(f32), axis=0).astype(bf16)
     column = jnp.concatenate(
         [
-            jnp.broadcast_to(column[None, :weight_chunk], (depth, weight_chunk, half)),
+            column[:weight_chunk].reshape(depth, weight_chunk // depth, half),
             column[weight_chunk:].reshape(depth, gauge_chunk // depth, half),
         ],
         axis=1,
     )
     parts = lax.all_to_all(column, "z", 0, 0, tiled=True)
     reduced = jnp.sum(parts.astype(f32), axis=0).astype(bf16)
-    own_gauge = reduced[weight_chunk:]
-    far_gauge = swap(own_gauge)
+    own_weight = reduced[: weight_chunk // depth]
+    own_gauge = reduced[weight_chunk // depth :]
+
+    line = spread(own_weight, "z", depth)
+    weights = spread(line, PLANE, plane)
+    late_sums, late_gauge = lax.optimization_barrier((sums, own_gauge, line))[:2]
+    far_gauge = swap(late_gauge)
+    from_above, from_below = shifted(late_sums[low], -1), shifted(late_sums[top], 1)
+    weights = after(weights, far_gauge, from_above, from_below)
+    pooled = ((sums[mid] + from_above + from_below) / roots[mid][:, None]).astype(bf16)
     grad_gauges = jnp.where(
         core == 0,
         jnp.concatenate([own_gauge, far_gauge], axis=1),
         jnp.concatenate([far_gauge, own_gauge], axis=1),
     )
-
-    weights = spread(reduced[:weight_chunk], PLANE, plane)
-    weights = after(weights, far_gauge)
     far = swap(weights)
     steps = 4
     block_in = pl.BlockSpec((4, width // steps, half), lambda i: (0, i, 0))

time: 135 us -> 126 us (0.933)
  waiting for transfers between devices: 50.3 us -> 22.1 us
  blocking collectives: 18.5 us -> 44.6 us
  starting transfers between devices: 47 us -> 44.6 us
  local copies, waits for them, and re-layouts: 4.89 us -> 2.87 us
    all_to_all x0 -> x2, blocking collectives: none -> 34.6 us  [the longest x1 24.9 us: per_device(): lax.all_to_all(chip, PLANE, 0, 0, tiled=True).reshape(plane, chunk, half)]
    all_to_all x1, waiting for transfers between devices: 13.3 us -> 0.01 us  [spread(): return lax.all_to_all(copies, axes, 0, 0, tiled=True)]
    ppermute x6, waiting for transfers between devices: 25.8 us -> 15 us  [shifted(): lax.ppermute(value, EVERY, [(i, (i + steps) % count) for i in range(count)])]
    all_to_all x1, blocking collectives: 18.5 us -> 9.96 us  [per_device(): parts = lax.all_to_all(column, 'z', 0, 0, tiled=True)]
    all_to_all x1 -> x0, starting transfers between devices: 3.71 us -> none  [per_device(): lax.all_to_all(chip, PLANE, 0, 0, tiled=True).reshape(plane, chunk, half)]
    ppermute x6, starting transfers between devices: 10.7 us -> 13.9 us  [shifted(): lax.ppermute(value, EVERY, [(i, (i + steps) % count) for i in range(count)])]
    all_to_all x1 -> x0, waiting for transfers between devices: 3.07 us -> none  [per_device(): lax.all_to_all(chip, PLANE, 0, 0, tiled=True).reshape(plane, chunk, half)]
    unnamed x18 -> x14, local copies, waits for them, and re-layouts: 2.64 us -> 0.65 us
  transfers between devices with their start and end apart: 13 -> 12, of which waited for: 10 -> 7; matrix products, arithmetic and copies ran while one was open for 2% -> 2% of each run, Pallas kernels for 0% -> 0%
where the time goes in v3:
time: 126 us
  starting transfers between devices  44.6 us (35%)
  blocking collectives  44.6 us (35%)
  waiting for transfers between devices  22.1 us (18%)
  Pallas kernels  8.43 us (7%)
  local copies, waits for them, and re-layouts  2.87 us (2%)
  other arithmetic  2.46 us (2%)
    all_to_all x1, blocking collectives, per_device(): lax.all_to_all(chip, PLANE, 0, 0, tiled=True).reshape(plane, chunk, half)  24.9 us
    all_to_all x1, starting transfers between devices, per_device(): mine = lax.all_to_all(copies, tiles, 0, 0, tiled=True)  16.3 us
    ppermute x6, waiting for transfers between devices, shifted(): lax.ppermute(value, EVERY, [(i, (i + steps) % count) for i in range(count)])  15 us
    ppermute x6, starting transfers between devices, shifted(): lax.ppermute(value, EVERY, [(i, (i + steps) % count) for i in range(count)])  13.9 us
    ppermute x4, starting transfers between devices, swap(): return lax.ppermute(value, 'c', [(0, 1), (1, 0)])  10.7 us
    all_to_all x1, blocking collectives, per_device(): parts = lax.all_to_all(column, 'z', 0, 0, tiled=True)  9.96 us
    all_to_all x1, blocking collectives, spread(): return lax.all_to_all(copies, axes, 0, 0, tiled=True)  9.67 us
    pallas_call x1, Pallas kernels, per_device(): pl.pallas_call(group_kernel, out_shape=(jax.ShapeDtypeStruct(cells.shape,...  5.97 us
  transfers between devices with their start and end apart: 12, of which 7 were waited for; matrix products, arithmetic and copies ran while one was open for 2% of the time, Pallas kernels for 0%

profile of v3, /device:TPU:1, one launch (start us, length us, event | category | flops | bytes accessed | tf_op | source)
XLA Modules:
  0.0 125.9 jit_solution(2420324321493538169)
XLA Ops:
  0.7 0.6 copy-done
  1.3 0.8 broadcast_in_dim.14
  2.2 16.3 %all-to-all-start = ((bf16[128,8,256]{2,1,0:T(8,128)(2,1)}), bf16[128,8,256]{2,1,0:T(8,128)(2,1)S(1)}, u32[]{:S(2)}, u32[]{:S(2)}) async-start(bf16[128,8,256]{2,1,0:T(8,128)(2,1)} %broadcast_in_dim.14), calls=%async_computation | async-start | bytes 1048576 | tf_op jit(solution)/shard_map/all_to_all | solution.py:210
  18.6 0.1 convert_reduce_fusion
  18.7 6.8 %collective-permute-start.3 = (bf16[1,128]{1,0:T(2,128)(2,1)S(1)}, bf16[1,128]{1,0:T(2,128)(2,1)S(1)}, u32[]{:S(2)}, u32[]{:S(2)}) collective-permute-start(bf16[1,128]{1,0:T(2,128)(2,1)S(1)} %slice.121), channel_id=1, source_target_pairs={{0,254},{1,255},{2,0},{3,1},{4,2},{5,3},{6,4},{7,5},{8,6},{9,7},{1... | collective-permute-start | bytes 776 | tf_op jit(solution)/shard_map/ppermute | solution.py:184
  25.6 1.5 %collective-permute-start.1 = (bf16[3,512]{1,0:T(4,128)(2,1)S(1)}, bf16[3,512]{1,0:T(4,128)(2,1)S(1)}, u32[]{:S(2)}, u32[]{:S(2)}) collective-permute-start(bf16[3,512]{1,0:T(4,128)(2,1)S(1)} %pad_maximum_fusion.1), channel_id=1, source_target_pairs={{0,255},{1,0},{2,1},{3,2},{4,3},{5,4},{6,5},{7,6},{8,7},{9,8},{10,... | collective-permute-start | bytes 9224 | tf_op jit(solution)/shard_map/ppermute | solution.py:184
  27.1 0.2 collective-permute-start
  27.4 0.1 add.157.places_ref
  27.5 0.1 add.149.rows_ref
  27.6 1.3 %collective-permute-done.1 = bf16[3,512]{1,0:T(4,128)(2,1)S(1)} collective-permute-done((bf16[3,512]{1,0:T(4,128)(2,1)S(1)}, bf16[3,512]{1,0:T(4,128)(2,1)S(1)}, u32[]{:S(2)}, u32[]{:S(2)}) %collective-permute-start.1) | collective-permute-done | bytes 3104 | tf_op jit(solution)/shard_map/ppermute | solution.py:184
  28.9 4.6 %collective-permute-done = bf16[3,512]{1,0:T(4,128)(2,1)S(1)} collective-permute-done((bf16[3,512]{1,0:T(4,128)(2,1)S(1)}, bf16[3,512]{1,0:T(4,128)(2,1)S(1)}, u32[]{:S(2)}, u32[]{:S(2)}) %collective-permute-start) | collective-permute-done | bytes 3104 | tf_op jit(solution)/shard_map/ppermute | solution.py:184
  33.5 1.8 %all-to-all-done = bf16[128,8,256]{2,1,0:T(8,128)(2,1)S(1)} async-done(((bf16[128,8,256]{2,1,0:T(8,128)(2,1)}), bf16[128,8,256]{2,1,0:T(8,128)(2,1)S(1)}, u32[]{:S(2)}, u32[]{:S(2)}) %all-to-all-start) | async-done | bytes 524320 | tf_op jit(solution)/shard_map/all_to_all | solution.py:210
  35.4 6.1 %collective-permute-start.4 = (bf16[1024,256]{1,0:T(8,128)(2,1)S(1)}, bf16[1024,256]{1,0:T(8,128)(2,1)S(1)}, u32[]{:S(2)}, u32[]{:S(2)}) collective-permute-start(bf16[1024,256]{1,0:T(8,128)(2,1)S(1)} %bitcast.47), channel_id=1, source_target_pairs={{0,1},{1,0},{2,3},{3,2},{4,5},{5,4},{6,7},{7,6},{8,9},{9,8},{10,11... | collective-permute-start | bytes 1572872 | tf_op jit(solution)/shard_map/ppermute | solution.py:179
  41.7 1.3 %collective-permute-done.4.other_ref = bf16[1024,256]{1,0:T(8,128)(2,1)S(1)} collective-permute-done((bf16[1024,256]{1,0:T(8,128)(2,1)S(1)}, bf16[1024,256]{1,0:T(8,128)(2,1)S(1)}, u32[]{:S(2)}, u32[]{:S(2)}) %collective-permute-start.4) | collective-permute-done | bytes 524320 | tf_op jit(solution)/shard_map/ppermute | solution.py:179
  43.0 6.0 %group_kernel.1 = (bf16[256,512]{1,0:T(8,128)(2,1)}, f32[16,512]{1,0:T(8,128)S(1)}, bf16[3072,256]{1,0:T(8,128)(2,1)S(1)}, bf16[3072,256]{1,0:T(8,128)(2,1)S(1)}) custom-call(s32[1]{0:T(128)} %bitcast.core_ref, s32[1,128]{1,0:T(1,128)S(1)} %add.149.rows_ref, s32[1,128]{1,0:T(1,128)S(1)} %add.157.places_ref, s32[1,256]{1,0:T(1,128)S(1)} %bitcast.50, ...), custom_call_target="tpu_custom_call" | custom-call | tf_op jit(solution)/shard_map/group_kernel/pallas_call | solution.py:252
  49.0 0.5 collective-permute-start.5
  49.4 3.0 %collective-permute-done.5 = bf16[3072,256]{1,0:T(8,128)(2,1)S(1)} collective-permute-done((bf16[3072,256]{1,0:T(8,128)(2,1)S(1)}, bf16[3072,256]{1,0:T(8,128)(2,1)S(1)}, u32[]{:S(2)}, u32[]{:S(2)}) %collective-permute-start.5) | collective-permute-done | bytes 1572896 | tf_op jit(solution)/shard_map/ppermute | solution.py:179
  52.5 0.5 add_convert_fusion
  53.0 24.9 %all_to_all.37 = bf16[16,192,256]{2,1,0:T(8,128)(2,1)S(1)} all-to-all(bf16[16,192,256]{2,1,0:T(8,128)(2,1)S(1)} %bitcast.51), channel_id=1, replica_groups=mesh['y'=4,'z'=8,'x'=4,'c'=2] {'y','x'}, dimensions={0} | all-to-all | bytes 3145728 | tf_op jit(solution)/shard_map/all_to_all | solution.py:280
  77.9 0.2 reduce_sum.34
  78.2 10.0 %all_to_all.38 = bf16[8,24,256]{2,1,0:T(8,128)(2,1)S(1)} all-to-all(bf16[8,24,256]{2,1,0:T(8,128)(2,1)S(1)} %pad_maximum_fusion), channel_id=1, replica_groups=mesh['y'=4,'z'=8,'x'=4,'c'=2] {'z'}, dimensions={0} | all-to-all | bytes 196608 | tf_op jit(solution)/shard_map/all_to_all | solution.py:289
  88.2 9.7 %all_to_all.39 = bf16[8,16,256]{2,1,0:T(8,128)(2,1)S(1)} all-to-all(bf16[8,16,256]{2,1,0:T(8,128)(2,1)S(1)} %broadcast_in_dim.15), channel_id=1, replica_groups=mesh['y'=4,'z'=8,'x'=4,'c'=2] {'z'}, dimensions={0} | all-to-all | bytes 131072 | tf_op jit(solution)/shard_map/all_to_all | solution.py:190
  97.8 1.1 broadcast_in_dim.17
  98.9 3.7 %all-to-all-start.4 = ((bf16[16,128,256]{2,1,0:T(8,128)(2,1)}), bf16[16,128,256]{2,1,0:T(8,128)(2,1)S(1)}, u32[]{:S(2)}, u32[]{:S(2)}) async-start(bf16[16,128,256]{2,1,0:T(8,128)(2,1)} %broadcast_in_dim.17), calls=%async_computation.4 | async-start | bytes 2097152 | tf_op jit(solution)/shard_map/all_to_all | solution.py:190
  102.6 3.8 %collective-permute-start.6 = (f32[2,512]{1,0:T(2,128)S(1)}, f32[2,512]{1,0:T(2,128)S(1)}, u32[]{:S(2)}, u32[]{:S(2)}) collective-permute-start(f32[2,512]{1,0:T(2,128)S(1)} %get-tuple-element.29), channel_id=1, source_target_pairs={{0,255},{1,0},{2,1},{3,2},{4,3},{5,4},{6,5},{7,6},{8,7},{9,8},{10,... | collective-permute-start | bytes 12296 | tf_op jit(solution)/shard_map/ppermute | solution.py:184
  106.4 1.5 %collective-permute-start.7 = (f32[2,512]{1,0:T(2,128)S(1)}, f32[2,512]{1,0:T(2,128)S(1)}, u32[]{:S(2)}, u32[]{:S(2)}) collective-permute-start(f32[2,512]{1,0:T(2,128)S(1)} %get-tuple-element.30), channel_id=1, source_target_pairs={{0,1},{1,2},{2,3},{3,4},{4,5},{5,6},{6,7},{7,8},{8,9},{9,10},{10,1... | collective-permute-start | bytes 12296 | tf_op jit(solution)/shard_map/ppermute | solution.py:184
  107.9 9.0 %collective-permute-done.6 = f32[2,512]{1,0:T(2,128)S(1)} collective-permute-done((f32[2,512]{1,0:T(2,128)S(1)}, f32[2,512]{1,0:T(2,128)S(1)}, u32[]{:S(2)}, u32[]{:S(2)}) %collective-permute-start.6) | collective-permute-done | bytes 4128 | tf_op jit(solution)/shard_map/ppermute | solution.py:184
  117.0 4.2 %collective-permute-start.9 = (bf16[2048,256]{1,0:T(8,128)(2,1)S(1)}, bf16[2048,256]{1,0:T(8,128)(2,1)S(1)}, u32[]{:S(2)}, u32[]{:S(2)}) collective-permute-start(bf16[2048,256]{1,0:T(8,128)(2,1)S(1)} %bitcast.45), channel_id=1, source_target_pairs={{0,1},{1,0},{2,3},{3,2},{4,5},{5,4},{6,7},{7,6},{8,9},{9,8},{10,11... | collective-permute-start | bytes 3145736 | tf_op jit(solution)/shard_map/ppermute | solution.py:179
  121.2 0.6 maximum_select_fusion
  121.8 0.7 fusion
  122.5 1.0 collective-permute-done.9
  123.4 2.5 %widen_kernel.1 = (f32[512,512]{1,0:T(8,128)}, f32[512,512]{1,0:T(8,128)}, f32[512,512]{1,0:T(8,128)}, f32[512,512]{1,0:T(8,128)}) custom-call(s32[1]{0:T(128)} %bitcast.core_ref, bf16[4,512,256]{2,1,0:T(8,128)(2,1)S(1)} %bitcast.46, bf16[4,512,256]{2,1,0:T(8,128)(2,1)S(1)} %bitcast.49), custom_call_target="tpu_custom_call" | custom-call | tf_op jit(solution)/shard_map/widen_kernel/pallas_call | solution.py:310
  (46 shorter events, 0.6 us)
Async XLA Ops:
  0.6 0.7 copy-start
  0.7 17.9 %copy-start.5 = (s32[256]{0:T(256)S(1)}, s32[256]{0:T(256)}, u32[]{:S(2)}) copy-start(s32[256]{0:T(256)} %param.16) | copy-start | bytes 3076
  0.7 18.0 %copy-start.4 = (bf16[2,512]{1,0:T(2,128)(2,1)S(1)}, bf16[2,512]{1,0:T(2,128)(2,1)}, u32[]{:S(2)}) copy-start(bf16[2,512]{1,0:T(2,128)(2,1)} %param.17) | copy-start | bytes 6148
  0.7 26.7 %copy-start.6 = (s32[1,16]{1,0:T(1,128)S(1)}, s32[1,16]{1,0:T(1,128)}, u32[]{:S(2)}) copy-start(s32[1,16]{1,0:T(1,128)} %param.15) | copy-start | bytes 196
  0.7 42.3 %copy-start.2 = (bf16[512,512]{1,0:T(8,128)(2,1)S(1)}, bf16[512,512]{1,0:T(8,128)(2,1)}, u32[]{:S(2)}) copy-start(bf16[512,512]{1,0:T(8,128)(2,1)} %wv_ref.1) | copy-start | bytes 1572868
  0.7 42.3 %copy-start.1 = (bf16[512,512]{1,0:T(8,128)(2,1)S(1)}, bf16[512,512]{1,0:T(8,128)(2,1)}, u32[]{:S(2)}) copy-start(bf16[512,512]{1,0:T(8,128)(2,1)} %wk_ref.1) | copy-start | bytes 1572868
  0.7 42.3 %copy-start.3 = (bf16[512,512]{1,0:T(8,128)(2,1)S(1)}, bf16[512,512]{1,0:T(8,128)(2,1)}, u32[]{:S(2)}) copy-start(bf16[512,512]{1,0:T(8,128)(2,1)} %wq_ref.1) | copy-start | bytes 1572868
  2.2 33.2 %all-to-all-start = ((bf16[128,8,256]{2,1,0:T(8,128)(2,1)}), bf16[128,8,256]{2,1,0:T(8,128)(2,1)S(1)}, u32[]{:S(2)}, u32[]{:S(2)}) async-start(bf16[128,8,256]{2,1,0:T(8,128)(2,1)} %broadcast_in_dim.14), calls=%async_computation | async-start | bytes 1048576 | tf_op jit(solution)/shard_map/all_to_all | solution.py:210
  18.7 22.7 %collective-permute-start.3 = (bf16[1,128]{1,0:T(2,128)(2,1)S(1)}, bf16[1,128]{1,0:T(2,128)(2,1)S(1)}, u32[]{:S(2)}, u32[]{:S(2)}) collective-permute-start(bf16[1,128]{1,0:T(2,128)(2,1)S(1)} %slice.121), channel_id=1, source_target_pairs={{0,254},{1,255},{2,0},{3,1},{4,2},{5,3},{6,4},{7,5},{8,6},{9,7},{1... | collective-permute-start | bytes 776 | tf_op jit(solution)/shard_map/ppermute | solution.py:184
  25.6 15.9 %collective-permute-start.2 = (bf16[1,128]{1,0:T(2,128)(2,1)S(1)}, bf16[1,128]{1,0:T(2,128)(2,1)S(1)}, u32[]{:S(2)}, u32[]{:S(2)}) collective-permute-start(bf16[1,128]{1,0:T(2,128)(2,1)S(1)} %slice.121), channel_id=1, source_target_pairs={{0,2},{1,3},{2,4},{3,5},{4,6},{5,7},{6,8},{7,9},{8,10},{9,11},{10,... | collective-permute-start | bytes 776 | tf_op jit(solution)/shard_map/ppermute | solution.py:184
  25.6 3.3 %collective-permute-start.1 = (bf16[3,512]{1,0:T(4,128)(2,1)S(1)}, bf16[3,512]{1,0:T(4,128)(2,1)S(1)}, u32[]{:S(2)}, u32[]{:S(2)}) collective-permute-start(bf16[3,512]{1,0:T(4,128)(2,1)S(1)} %pad_maximum_fusion.1), channel_id=1, source_target_pairs={{0,255},{1,0},{2,1},{3,2},{4,3},{5,4},{6,5},{7,6},{8,7},{9,8},{10,... | collective-permute-start | bytes 9224 | tf_op jit(solution)/shard_map/ppermute | solution.py:184
  27.1 6.4 %collective-permute-start = (bf16[3,512]{1,0:T(4,128)(2,1)S(1)}, bf16[3,512]{1,0:T(4,128)(2,1)S(1)}, u32[]{:S(2)}, u32[]{:S(2)}) collective-permute-start(bf16[3,512]{1,0:T(4,128)(2,1)S(1)} %pad_maximum_fusion.1), channel_id=1, source_target_pairs={{0,1},{1,2},{2,3},{3,4},{4,5},{5,6},{6,7},{7,8},{8,9},{9,10},{10,1... | collective-permute-start | bytes 9224 | tf_op jit(solution)/shard_map/ppermute | solution.py:184
  35.4 7.6 %collective-permute-start.4 = (bf16[1024,256]{1,0:T(8,128)(2,1)S(1)}, bf16[1024,256]{1,0:T(8,128)(2,1)S(1)}, u32[]{:S(2)}, u32[]{:S(2)}) collective-permute-start(bf16[1024,256]{1,0:T(8,128)(2,1)S(1)} %bitcast.47), channel_id=1, source_target_pairs={{0,1},{1,0},{2,3},{3,2},{4,5},{5,4},{6,7},{7,6},{8,9},{9,8},{10,11... | collective-permute-start | bytes 1572872 | tf_op jit(solution)/shard_map/ppermute | solution.py:179
  49.0 3.5 %collective-permute-start.5 = (bf16[3072,256]{1,0:T(8,128)(2,1)S(1)}, bf16[3072,256]{1,0:T(8,128)(2,1)S(1)}, u32[]{:S(2)}, u32[]{:S(2)}) collective-permute-start(bf16[3072,256]{1,0:T(8,128)(2,1)S(1)} %get-tuple-element.20), channel_id=1, source_target_pairs={{0,1},{1,0},{2,3},{3,2},{4,5},{5,4},{6,7},{7,6},{8,9},{9,8},{10,11... | collective-permute-start | bytes 4718600 | tf_op jit(solution)/shard_map/ppermute | solution.py:179
  98.9 18.0 %all-to-all-start.4 = ((bf16[16,128,256]{2,1,0:T(8,128)(2,1)}), bf16[16,128,256]{2,1,0:T(8,128)(2,1)S(1)}, u32[]{:S(2)}, u32[]{:S(2)}) async-start(bf16[16,128,256]{2,1,0:T(8,128)(2,1)} %broadcast_in_dim.17), calls=%async_computation.4 | async-start | bytes 2097152 | tf_op jit(solution)/shard_map/all_to_all | solution.py:190
  102.6 14.3 %collective-permute-start.6 = (f32[2,512]{1,0:T(2,128)S(1)}, f32[2,512]{1,0:T(2,128)S(1)}, u32[]{:S(2)}, u32[]{:S(2)}) collective-permute-start(f32[2,512]{1,0:T(2,128)S(1)} %get-tuple-element.29), channel_id=1, source_target_pairs={{0,255},{1,0},{2,1},{3,2},{4,3},{5,4},{6,5},{7,6},{8,7},{9,8},{10,... | collective-permute-start | bytes 12296 | tf_op jit(solution)/shard_map/ppermute | solution.py:184
  106.4 10.5 %collective-permute-start.7 = (f32[2,512]{1,0:T(2,128)S(1)}, f32[2,512]{1,0:T(2,128)S(1)}, u32[]{:S(2)}, u32[]{:S(2)}) collective-permute-start(f32[2,512]{1,0:T(2,128)S(1)} %get-tuple-element.30), channel_id=1, source_target_pairs={{0,1},{1,2},{2,3},{3,4},{4,5},{5,6},{6,7},{7,8},{8,9},{9,10},{10,1... | collective-permute-start | bytes 12296 | tf_op jit(solution)/shard_map/ppermute | solution.py:184
  107.9 9.0 %collective-permute-start.8 = (bf16[8,256]{1,0:T(8,128)(2,1)S(1)}, bf16[8,256]{1,0:T(8,128)(2,1)S(1)}, u32[]{:S(2)}, u32[]{:S(2)}) collective-permute-start(bf16[8,256]{1,0:T(8,128)(2,1)S(1)} %slice.126), channel_id=1, source_target_pairs={{0,1},{1,0},{2,3},{3,2},{4,5},{5,4},{6,7},{7,6},{8,9},{9,8},{10,11... | collective-permute-start | bytes 12296 | tf_op jit(solution)/shard_map/ppermute | solution.py:179
  117.0 6.5 %collective-permute-start.9 = (bf16[2048,256]{1,0:T(8,128)(2,1)S(1)}, bf16[2048,256]{1,0:T(8,128)(2,1)S(1)}, u32[]{:S(2)}, u32[]{:S(2)}) collective-permute-start(bf16[2048,256]{1,0:T(8,128)(2,1)S(1)} %bitcast.45), channel_id=1, source_target_pairs={{0,1},{1,0},{2,3},{3,2},{4,5},{5,4},{6,7},{7,6},{8,9},{9,8},{10,11... | collective-permute-start | bytes 3145736 | tf_op jit(solution)/shard_map/ppermute | solution.py:179

commit v4 on v3

--- a/solution.py
+++ b/solution.py
@@ -166,13 +166,31 @@
         )
 
 
-def widen_kernel(core_ref, mine_ref, far_ref, *out_refs):
-    first = core_ref[0] == 0
-    half = mine_ref.shape[2]
-    for i, out_ref in enumerate(out_refs):
-        mine, far = mine_ref[i], far_ref[i]
-        out_ref[:, :half] = jnp.where(first, mine, far).astype(f32)
-        out_ref[:, half:] = jnp.where(first, far, mine).astype(f32)
+def widen_kernel(side_ref, part_ref, *refs):
+    for i, out_ref in enumerate(refs[-4:]):
+        out_ref[...] = part_ref[i].astype(f32)
+
+
+def widen(side, part, grads):
+    half = part.shape[1]
+    width = 2 * half
+    steps = 4
+    given = () if grads is None else tuple(grads)
+    block_in = pl.BlockSpec((4, width // steps, half), lambda i, side: (0, i, 0))
+    block_out = pl.BlockSpec((width // steps, half), lambda i, side: (i, side[0]))
+    return pl.pallas_call(
+        widen_kernel,
+        out_shape=(jax.ShapeDtypeStruct((width, width), f32),) * 4,
+        grid_spec=pltpu.PrefetchScalarGridSpec(
+            num_scalar_prefetch=1,
+            grid=(steps,),
+            in_specs=[block_in] + [pl.BlockSpec(memory_space=pl.ANY)] * len(given),
+            out_specs=(block_out,) * 4,
+        ),
+        input_output_aliases={2 + i: i for i in range(len(given))},
+        compiler_params=pltpu.CompilerParams(vmem_limit_bytes=48 << 20),
+        name="widen_kernel",
+    )(side.reshape(1), part.reshape(4, width, half), *given)
 
 
 def swap(value):
@@ -292,11 +310,11 @@
     own_gauge = reduced[weight_chunk // depth :]
 
     line = spread(own_weight, "z", depth)
-    weights = spread(line, PLANE, plane)
-    late_sums, late_gauge = lax.optimization_barrier((sums, own_gauge, line))[:2]
+    late_sums, late_gauge = lax.optimization_barrier((sums, own_gauge))
     far_gauge = swap(late_gauge)
     from_above, from_below = shifted(late_sums[low], -1), shifted(late_sums[top], 1)
-    weights = after(weights, far_gauge, from_above, from_below)
+    line = after(line, far_gauge, from_above, from_below)
+    weights = spread(line, PLANE, plane)
     pooled = ((sums[mid] + from_above + from_below) / roots[mid][:, None]).astype(bf16)
     grad_gauges = jnp.where(
         core == 0,
@@ -304,18 +322,8 @@
         jnp.concatenate([far_gauge, own_gauge], axis=1),
     )
     far = swap(weights)
-    steps = 4
-    block_in = pl.BlockSpec((4, width // steps, half), lambda i: (0, i, 0))
-    block_out = pl.BlockSpec((width // steps, width), lambda i: (i, 0))
-    grads = pl.pallas_call(
-        widen_kernel,
-        out_shape=(jax.ShapeDtypeStruct((width, width), f32),) * 4,
-        grid=(steps,),
-        in_specs=[smem, block_in, block_in],
-        out_specs=(block_out,) * 4,
-        compiler_params=pltpu.CompilerParams(vmem_limit_bytes=48 << 20),
-        name="widen_kernel",
-    )(core.reshape(1), weights.reshape(4, width, half), far.reshape(4, width, half))
+    grads = widen(core, weights, None)
+    grads = widen(1 - core, far, grads)
     return (pooled, grad_cells, grad_gauges, grads[0], grads[1], grads[2], grads[3])
 
 

time: 126 us -> 126 us (level)
  waiting for transfers between devices: 22.1 us -> 15.2 us
  blocking collectives: 44.6 us -> 50.3 us
  Pallas kernels: 8.43 us -> 9.76 us
    ppermute x6, waiting for transfers between devices: 15 us -> 6.58 us  [shifted(): lax.ppermute(value, EVERY, [(i, (i + steps) % count) for i in range(count)])]
    all_to_all x1, blocking collectives: 9.67 us -> 15.4 us  [spread(): return lax.all_to_all(copies, axes, 0, 0, tiled=True)]
    ppermute x4, starting transfers between devices: 10.7 us -> 13.4 us  [swap(): return lax.ppermute(value, 'c', [(0, 1), (1, 0)])]
    all_to_all x1, waiting for transfers between devices: 0.01 us -> 2.32 us  [spread(): return lax.all_to_all(copies, axes, 0, 0, tiled=True)]
    ppermute x6, starting transfers between devices: 13.9 us -> 11.6 us  [shifted(): lax.ppermute(value, EVERY, [(i, (i + steps) % count) for i in range(count)])]
    pallas_call x1 -> x2, Pallas kernels: 2.46 us -> 3.78 us  [widen(): pl.pallas_call(widen_kernel, out_shape=(jax.ShapeDtypeStruct((width, widt...]
  transfers between devices with their start and end apart: 12 -> 12, of which waited for: 7 -> 9; matrix products, arithmetic and copies ran while one was open for 2% -> 2% of each run, Pallas kernels for 0% -> 1%
where the time goes in v4:
time: 126 us
  blocking collectives  50.3 us (40%)
  starting transfers between devices  44.7 us (35%)
  waiting for transfers between devices  15.2 us (12%)
  Pallas kernels  9.76 us (8%)
  local copies, waits for them, and re-layouts  2.52 us (2%)
  other arithmetic  2.46 us (2%)
    all_to_all x1, blocking collectives, per_device(): lax.all_to_all(chip, PLANE, 0, 0, tiled=True).reshape(plane, chunk, half)  24.9 us
    all_to_all x1, starting transfers between devices, per_device(): mine = lax.all_to_all(copies, tiles, 0, 0, tiled=True)  16.3 us
    all_to_all x1, blocking collectives, spread(): return lax.all_to_all(copies, axes, 0, 0, tiled=True)  15.4 us
    ppermute x4, starting transfers between devices, swap(): return lax.ppermute(value, 'c', [(0, 1), (1, 0)])  13.4 us
    ppermute x6, starting transfers between devices, shifted(): lax.ppermute(value, EVERY, [(i, (i + steps) % count) for i in range(count)])  11.6 us
    all_to_all x1, blocking collectives, per_device(): parts = lax.all_to_all(column, 'z', 0, 0, tiled=True)  9.96 us
    ppermute x6, waiting for transfers between devices, shifted(): lax.ppermute(value, EVERY, [(i, (i + steps) % count) for i in range(count)])  6.58 us
    pallas_call x1, Pallas kernels, per_device(): pl.pallas_call(group_kernel, out_shape=(jax.ShapeDtypeStruct(cells.shape,...  5.97 us
  transfers between devices with their start and end apart: 12, of which 9 were waited for; matrix products, arithmetic and copies ran while one was open for 2% of the time, Pallas kernels for 1%

profile of v4, /device:TPU:1, one launch (start us, length us, event | category | flops | bytes accessed | tf_op | source)
XLA Modules:
  0.0 125.8 jit_solution(15727945856584778046)
XLA Ops:
  0.7 0.6 copy-done
  1.3 0.8 broadcast_in_dim.12
  2.2 16.3 %all-to-all-start = ((bf16[128,8,256]{2,1,0:T(8,128)(2,1)}), bf16[128,8,256]{2,1,0:T(8,128)(2,1)S(1)}, u32[]{:S(2)}, u32[]{:S(2)}) async-start(bf16[128,8,256]{2,1,0:T(8,128)(2,1)} %broadcast_in_dim.12), calls=%async_computation | async-start | bytes 1048576 | tf_op jit(solution)/shard_map/all_to_all | solution.py:228
  18.7 6.8 %collective-permute-start.3 = (bf16[1,128]{1,0:T(2,128)(2,1)S(1)}, bf16[1,128]{1,0:T(2,128)(2,1)S(1)}, u32[]{:S(2)}, u32[]{:S(2)}) collective-permute-start(bf16[1,128]{1,0:T(2,128)(2,1)S(1)} %slice.121), channel_id=1, source_target_pairs={{0,254},{1,255},{2,0},{3,1},{4,2},{5,3},{6,4},{7,5},{8,6},{9,7},{1... | collective-permute-start | bytes 776 | tf_op jit(solution)/shard_map/ppermute | solution.py:202
  25.6 1.5 %collective-permute-start.1 = (bf16[3,512]{1,0:T(4,128)(2,1)S(1)}, bf16[3,512]{1,0:T(4,128)(2,1)S(1)}, u32[]{:S(2)}, u32[]{:S(2)}) collective-permute-start(bf16[3,512]{1,0:T(4,128)(2,1)S(1)} %pad_maximum_fusion.1), channel_id=1, source_target_pairs={{0,255},{1,0},{2,1},{3,2},{4,3},{5,4},{6,5},{7,6},{8,7},{9,8},{10,... | collective-permute-start | bytes 9224 | tf_op jit(solution)/shard_map/ppermute | solution.py:202
  27.1 0.2 collective-permute-start
  27.6 1.3 %collective-permute-done.1 = bf16[3,512]{1,0:T(4,128)(2,1)S(1)} collective-permute-done((bf16[3,512]{1,0:T(4,128)(2,1)S(1)}, bf16[3,512]{1,0:T(4,128)(2,1)S(1)}, u32[]{:S(2)}, u32[]{:S(2)}) %collective-permute-start.1) | collective-permute-done | bytes 3104 | tf_op jit(solution)/shard_map/ppermute | solution.py:202
  28.9 4.6 %collective-permute-done = bf16[3,512]{1,0:T(4,128)(2,1)S(1)} collective-permute-done((bf16[3,512]{1,0:T(4,128)(2,1)S(1)}, bf16[3,512]{1,0:T(4,128)(2,1)S(1)}, u32[]{:S(2)}, u32[]{:S(2)}) %collective-permute-start) | collective-permute-done | bytes 3104 | tf_op jit(solution)/shard_map/ppermute | solution.py:202
  33.5 1.8 %all-to-all-done = bf16[128,8,256]{2,1,0:T(8,128)(2,1)S(1)} async-done(((bf16[128,8,256]{2,1,0:T(8,128)(2,1)}), bf16[128,8,256]{2,1,0:T(8,128)(2,1)S(1)}, u32[]{:S(2)}, u32[]{:S(2)}) %all-to-all-start) | async-done | bytes 524320 | tf_op jit(solution)/shard_map/all_to_all | solution.py:228
  35.4 6.1 %collective-permute-start.4 = (bf16[1024,256]{1,0:T(8,128)(2,1)S(1)}, bf16[1024,256]{1,0:T(8,128)(2,1)S(1)}, u32[]{:S(2)}, u32[]{:S(2)}) collective-permute-start(bf16[1024,256]{1,0:T(8,128)(2,1)S(1)} %bitcast.48), channel_id=1, source_target_pairs={{0,1},{1,0},{2,3},{3,2},{4,5},{5,4},{6,7},{7,6},{8,9},{9,8},{10,11... | collective-permute-start | bytes 1572872 | tf_op jit(solution)/shard_map/ppermute | solution.py:197
  41.7 1.3 %collective-permute-done.4.other_ref = bf16[1024,256]{1,0:T(8,128)(2,1)S(1)} collective-permute-done((bf16[1024,256]{1,0:T(8,128)(2,1)S(1)}, bf16[1024,256]{1,0:T(8,128)(2,1)S(1)}, u32[]{:S(2)}, u32[]{:S(2)}) %collective-permute-start.4) | collective-permute-done | bytes 524320 | tf_op jit(solution)/shard_map/ppermute | solution.py:197
  43.0 6.0 %group_kernel.1 = (bf16[256,512]{1,0:T(8,128)(2,1)}, f32[16,512]{1,0:T(8,128)S(1)}, bf16[3072,256]{1,0:T(8,128)(2,1)S(1)}, bf16[3072,256]{1,0:T(8,128)(2,1)S(1)}) custom-call(s32[1]{0:T(128)} %bitcast.core_ref.side_ref, s32[1,128]{1,0:T(1,128)S(1)} %add.149.rows_ref, s32[1,128]{1,0:T(1,128)S(1)} %add.157.places_ref, s32[1,256]{1,0:T(1,128)S(1)} %bitcast.51, ...), custom_call_target="tpu_custom_call" | custom-call | tf_op jit(solution)/shard_map/group_kernel/pallas_call | solution.py:270
  49.0 0.5 collective-permute-start.5
  49.4 3.0 %collective-permute-done.5 = bf16[3072,256]{1,0:T(8,128)(2,1)S(1)} collective-permute-done((bf16[3072,256]{1,0:T(8,128)(2,1)S(1)}, bf16[3072,256]{1,0:T(8,128)(2,1)S(1)}, u32[]{:S(2)}, u32[]{:S(2)}) %collective-permute-start.5) | collective-permute-done | bytes 1572896 | tf_op jit(solution)/shard_map/ppermute | solution.py:197
  52.5 0.5 add_convert_fusion
  53.0 24.9 %all_to_all.40 = bf16[16,192,256]{2,1,0:T(8,128)(2,1)S(1)} all-to-all(bf16[16,192,256]{2,1,0:T(8,128)(2,1)S(1)} %bitcast.52), channel_id=1, replica_groups=mesh['y'=4,'z'=8,'x'=4,'c'=2] {'y','x'}, dimensions={0} | all-to-all | bytes 3145728 | tf_op jit(solution)/shard_map/all_to_all | solution.py:298
  77.9 0.2 reduce_sum.34
  78.2 10.0 %all_to_all.41 = bf16[8,24,256]{2,1,0:T(8,128)(2,1)S(1)} all-to-all(bf16[8,24,256]{2,1,0:T(8,128)(2,1)S(1)} %pad_maximum_fusion), channel_id=1, replica_groups=mesh['y'=4,'z'=8,'x'=4,'c'=2] {'z'}, dimensions={0} | all-to-all | bytes 196608 | tf_op jit(solution)/shard_map/all_to_all | solution.py:307
  88.2 0.6 broadcast_in_dim.13
  88.8 3.4 %all-to-all-start.3 = ((bf16[8,16,256]{2,1,0:T(8,128)(2,1)}), bf16[8,16,256]{2,1,0:T(8,128)(2,1)S(1)}, u32[]{:S(2)}, u32[]{:S(2)}) async-start(bf16[8,16,256]{2,1,0:T(8,128)(2,1)} %broadcast_in_dim.13), calls=%async_computation.3 | async-start | bytes 131072 | tf_op jit(solution)/shard_map/all_to_all | solution.py:208
  92.2 2.7 %collective-permute-start.6 = (f32[2,512]{1,0:T(2,128)S(1)}, f32[2,512]{1,0:T(2,128)S(1)}, u32[]{:S(2)}, u32[]{:S(2)}) collective-permute-start(f32[2,512]{1,0:T(2,128)S(1)} %get-tuple-element.37), channel_id=1, source_target_pairs={{0,255},{1,0},{2,1},{3,2},{4,3},{5,4},{6,5},{7,6},{8,7},{9,8},{10,... | collective-permute-start | bytes 12296 | tf_op jit(solution)/shard_map/ppermute | solution.py:202
  94.9 0.3 collective-permute-start.7
  95.2 1.1 collective-permute-start.8
  96.4 0.5 collective-permute-done.7
  96.9 0.2 collective-permute-done.8
  97.1 2.3 %all-to-all-done.3 = bf16[8,16,256]{2,1,0:T(8,128)(2,1)S(1)} async-done(((bf16[8,16,256]{2,1,0:T(8,128)(2,1)}), bf16[8,16,256]{2,1,0:T(8,128)(2,1)S(1)}, u32[]{:S(2)}, u32[]{:S(2)}) %all-to-all-start.3) | async-done | bytes 65568 | tf_op jit(solution)/shard_map/all_to_all | solution.py:208
  99.5 15.4 %all_to_all.42 = bf16[16,128,256]{2,1,0:T(8,128)(2,1)S(1)} all-to-all(bf16[16,128,256]{2,1,0:T(8,128)(2,1)S(1)} %broadcast_in_dim.14), channel_id=1, replica_groups=mesh['y'=4,'z'=8,'x'=4,'c'=2] {'y','x'}, dimensions={0} | all-to-all | bytes 2097152 | tf_op jit(solution)/shard_map/all_to_all | solution.py:208
  114.9 5.8 %collective-permute-start.9 = (bf16[2048,256]{1,0:T(8,128)(2,1)S(1)}, bf16[2048,256]{1,0:T(8,128)(2,1)S(1)}, u32[]{:S(2)}, u32[]{:S(2)}) collective-permute-start(bf16[2048,256]{1,0:T(8,128)(2,1)S(1)} %bitcast.46), channel_id=1, source_target_pairs={{0,1},{1,0},{2,3},{3,2},{4,5},{5,4},{6,7},{7,6},{8,9},{9,8},{10,11... | collective-permute-start | bytes 3145736 | tf_op jit(solution)/shard_map/ppermute | solution.py:197
  120.8 0.6 maximum_select_fusion
  121.4 0.7 fusion
  122.0 1.9 %widen_kernel.2 = (f32[512,512]{1,0:T(8,128)}, f32[512,512]{1,0:T(8,128)}, f32[512,512]{1,0:T(8,128)}, f32[512,512]{1,0:T(8,128)}) custom-call(s32[1]{0:T(128)} %bitcast.core_ref.side_ref, bf16[4,512,256]{2,1,0:T(8,128)(2,1)S(1)} %bitcast.47), custom_call_target="tpu_custom_call" | custom-call | tf_op jit(solution)/shard_map/widen_kernel/pallas_call | solution.py:181
  123.9 1.9 %widen_kernel.3 = (f32[512,512]{1,0:T(8,128)}, f32[512,512]{1,0:T(8,128)}, f32[512,512]{1,0:T(8,128)}, f32[512,512]{1,0:T(8,128)}) custom-call(s32[1]{0:T(128)} %bitcast.12.side_ref, bf16[4,512,256]{2,1,0:T(8,128)(2,1)S(1)} %bitcast.50, ...), custom_call_target="tpu_custom_call", output_to_operand_aliasing={{0}: (2, {}), {1}: (3, {}), {2}: (4, {}), {3}: (5, {})} | custom-call | tf_op jit(solution)/shard_map/widen_kernel/pallas_call | solution.py:181
  (47 shorter events, 1.1 us)
Async XLA Ops:
  0.6 0.7 copy-start
  0.7 17.9 %copy-start.5 = (s32[256]{0:T(256)S(1)}, s32[256]{0:T(256)}, u32[]{:S(2)}) copy-start(s32[256]{0:T(256)} %param.16) | copy-start | bytes 3076
  0.7 18.0 %copy-start.4 = (bf16[2,512]{1,0:T(2,128)(2,1)S(1)}, bf16[2,512]{1,0:T(2,128)(2,1)}, u32[]{:S(2)}) copy-start(bf16[2,512]{1,0:T(2,128)(2,1)} %param.17) | copy-start | bytes 6148
  0.7 26.6 %copy-start.6 = (s32[1,16]{1,0:T(1,128)S(1)}, s32[1,16]{1,0:T(1,128)}, u32[]{:S(2)}) copy-start(s32[1,16]{1,0:T(1,128)} %param.15) | copy-start | bytes 196
  0.7 42.3 %copy-start.2 = (bf16[512,512]{1,0:T(8,128)(2,1)S(1)}, bf16[512,512]{1,0:T(8,128)(2,1)}, u32[]{:S(2)}) copy-start(bf16[512,512]{1,0:T(8,128)(2,1)} %wv_ref.1) | copy-start | bytes 1572868
  0.7 42.3 %copy-start.1 = (bf16[512,512]{1,0:T(8,128)(2,1)S(1)}, bf16[512,512]{1,0:T(8,128)(2,1)}, u32[]{:S(2)}) copy-start(bf16[512,512]{1,0:T(8,128)(2,1)} %wk_ref.1) | copy-start | bytes 1572868
  0.7 42.3 %copy-start.3 = (bf16[512,512]{1,0:T(8,128)(2,1)S(1)}, bf16[512,512]{1,0:T(8,128)(2,1)}, u32[]{:S(2)}) copy-start(bf16[512,512]{1,0:T(8,128)(2,1)} %wq_ref.1) | copy-start | bytes 1572868
  2.2 33.2 %all-to-all-start = ((bf16[128,8,256]{2,1,0:T(8,128)(2,1)}), bf16[128,8,256]{2,1,0:T(8,128)(2,1)S(1)}, u32[]{:S(2)}, u32[]{:S(2)}) async-start(bf16[128,8,256]{2,1,0:T(8,128)(2,1)} %broadcast_in_dim.12), calls=%async_computation | async-start | bytes 1048576 | tf_op jit(solution)/shard_map/all_to_all | solution.py:228
  18.7 22.7 %collective-permute-start.3 = (bf16[1,128]{1,0:T(2,128)(2,1)S(1)}, bf16[1,128]{1,0:T(2,128)(2,1)S(1)}, u32[]{:S(2)}, u32[]{:S(2)}) collective-permute-start(bf16[1,128]{1,0:T(2,128)(2,1)S(1)} %slice.121), channel_id=1, source_target_pairs={{0,254},{1,255},{2,0},{3,1},{4,2},{5,3},{6,4},{7,5},{8,6},{9,7},{1... | collective-permute-start | bytes 776 | tf_op jit(solution)/shard_map/ppermute | solution.py:202
  25.6 15.9 %collective-permute-start.2 = (bf16[1,128]{1,0:T(2,128)(2,1)S(1)}, bf16[1,128]{1,0:T(2,128)(2,1)S(1)}, u32[]{:S(2)}, u32[]{:S(2)}) collective-permute-start(bf16[1,128]{1,0:T(2,128)(2,1)S(1)} %slice.121), channel_id=1, source_target_pairs={{0,2},{1,3},{2,4},{3,5},{4,6},{5,7},{6,8},{7,9},{8,10},{9,11},{10,... | collective-permute-start | bytes 776 | tf_op jit(solution)/shard_map/ppermute | solution.py:202
  25.6 3.3 %collective-permute-start.1 = (bf16[3,512]{1,0:T(4,128)(2,1)S(1)}, bf16[3,512]{1,0:T(4,128)(2,1)S(1)}, u32[]{:S(2)}, u32[]{:S(2)}) collective-permute-start(bf16[3,512]{1,0:T(4,128)(2,1)S(1)} %pad_maximum_fusion.1), channel_id=1, source_target_pairs={{0,255},{1,0},{2,1},{3,2},{4,3},{5,4},{6,5},{7,6},{8,7},{9,8},{10,... | collective-permute-start | bytes 9224 | tf_op jit(solution)/shard_map/ppermute | solution.py:202
  27.1 6.4 %collective-permute-start = (bf16[3,512]{1,0:T(4,128)(2,1)S(1)}, bf16[3,512]{1,0:T(4,128)(2,1)S(1)}, u32[]{:S(2)}, u32[]{:S(2)}) collective-permute-start(bf16[3,512]{1,0:T(4,128)(2,1)S(1)} %pad_maximum_fusion.1), channel_id=1, source_target_pairs={{0,1},{1,2},{2,3},{3,4},{4,5},{5,6},{6,7},{7,8},{8,9},{9,10},{10,1... | collective-permute-start | bytes 9224 | tf_op jit(solution)/shard_map/ppermute | solution.py:202
  35.4 7.6 %collective-permute-start.4 = (bf16[1024,256]{1,0:T(8,128)(2,1)S(1)}, bf16[1024,256]{1,0:T(8,128)(2,1)S(1)}, u32[]{:S(2)}, u32[]{:S(2)}) collective-permute-start(bf16[1024,256]{1,0:T(8,128)(2,1)S(1)} %bitcast.48), channel_id=1, source_target_pairs={{0,1},{1,0},{2,3},{3,2},{4,5},{5,4},{6,7},{7,6},{8,9},{9,8},{10,11... | collective-permute-start | bytes 1572872 | tf_op jit(solution)/shard_map/ppermute | solution.py:197
  49.0 3.5 %collective-permute-start.5 = (bf16[3072,256]{1,0:T(8,128)(2,1)S(1)}, bf16[3072,256]{1,0:T(8,128)(2,1)S(1)}, u32[]{:S(2)}, u32[]{:S(2)}) collective-permute-start(bf16[3072,256]{1,0:T(8,128)(2,1)S(1)} %get-tuple-element.24), channel_id=1, source_target_pairs={{0,1},{1,0},{2,3},{3,2},{4,5},{5,4},{6,7},{7,6},{8,9},{9,8},{10,11... | collective-permute-start | bytes 4718600 | tf_op jit(solution)/shard_map/ppermute | solution.py:197
  88.8 10.6 %all-to-all-start.3 = ((bf16[8,16,256]{2,1,0:T(8,128)(2,1)}), bf16[8,16,256]{2,1,0:T(8,128)(2,1)S(1)}, u32[]{:S(2)}, u32[]{:S(2)}) async-start(bf16[8,16,256]{2,1,0:T(8,128)(2,1)} %broadcast_in_dim.13), calls=%async_computation.3 | async-start | bytes 131072 | tf_op jit(solution)/shard_map/all_to_all | solution.py:208
  92.2 4.2 %collective-permute-start.6 = (f32[2,512]{1,0:T(2,128)S(1)}, f32[2,512]{1,0:T(2,128)S(1)}, u32[]{:S(2)}, u32[]{:S(2)}) collective-permute-start(f32[2,512]{1,0:T(2,128)S(1)} %get-tuple-element.37), channel_id=1, source_target_pairs={{0,255},{1,0},{2,1},{3,2},{4,3},{5,4},{6,5},{7,6},{8,7},{9,8},{10,... | collective-permute-start | bytes 12296 | tf_op jit(solution)/shard_map/ppermute | solution.py:202
  94.9 2.0 %collective-permute-start.7 = (f32[2,512]{1,0:T(2,128)S(1)}, f32[2,512]{1,0:T(2,128)S(1)}, u32[]{:S(2)}, u32[]{:S(2)}) collective-permute-start(f32[2,512]{1,0:T(2,128)S(1)} %get-tuple-element.38), channel_id=1, source_target_pairs={{0,1},{1,2},{2,3},{3,4},{4,5},{5,6},{6,7},{7,8},{8,9},{9,10},{10,1... | collective-permute-start | bytes 12296 | tf_op jit(solution)/shard_map/ppermute | solution.py:202
  95.2 1.9 %collective-permute-start.8 = (bf16[8,256]{1,0:T(8,128)(2,1)S(1)}, bf16[8,256]{1,0:T(8,128)(2,1)S(1)}, u32[]{:S(2)}, u32[]{:S(2)}) collective-permute-start(bf16[8,256]{1,0:T(8,128)(2,1)S(1)} %slice.126), channel_id=1, source_target_pairs={{0,1},{1,0},{2,3},{3,2},{4,5},{5,4},{6,7},{7,6},{8,9},{9,8},{10,11... | collective-permute-start | bytes 12296 | tf_op jit(solution)/shard_map/ppermute | solution.py:197
  114.9 9.0 %collective-permute-start.9 = (bf16[2048,256]{1,0:T(8,128)(2,1)S(1)}, bf16[2048,256]{1,0:T(8,128)(2,1)S(1)}, u32[]{:S(2)}, u32[]{:S(2)}) collective-permute-start(bf16[2048,256]{1,0:T(8,128)(2,1)S(1)} %bitcast.46), channel_id=1, source_target_pairs={{0,1},{1,0},{2,3},{3,2},{4,5},{5,4},{6,7},{7,6},{8,9},{9,8},{10,11... | collective-permute-start | bytes 3145736 | tf_op jit(solution)/shard_map/ppermute | solution.py:197

commit v5 on v4

--- a/solution.py
+++ b/solution.py
@@ -17,9 +17,11 @@
 SLOTS = 16
 score_cap = 30.0
 
-EVERY = ("y", "z", "x", "c")
-PLANE = ("y", "x")
-SIZES = {"y": 4, "z": 8, "x": 4, "c": 2}
+EVERY = ("y", "far", "near", "x", "c")
+TILES = ("y", "far", "near", "x")
+GROUP = ("y", "x", "near")
+SIZES = {"y": 4, "far": 4, "near": 2, "x": 4, "c": 2}
+MEMBERS = SIZES["y"] * SIZES["x"] * SIZES["near"]
 
 bf16 = jnp.bfloat16
 f32 = jnp.float32
@@ -58,9 +60,8 @@
     half = width // 2
     gauges = mine_ref.shape[0]
     pairs = width // PAIR
-    plane = SIZES["y"] * SIZES["x"]
-    gauge_chunk = gauges // plane
-    weight_chunk = 4 * width // plane
+    gauge_chunk = gauges // MEMBERS
+    weight_chunk = 4 * width // MEMBERS
     chunk = gauge_chunk + weight_chunk
 
     def store(row, value):
@@ -159,7 +160,7 @@
         + mm_cols(value_low, wv_ref[...])
     ).astype(bf16)
     places = jnp.where(gauge_ids == places_ref[...], 1.0, 0.0).astype(bf16)
-    for j in range(plane):
+    for j in range(MEMBERS):
         store(
             j * chunk + weight_chunk,
             mm(places[j * gauge_chunk : (j + 1) * gauge_chunk, :], grad_gauges),
@@ -167,28 +168,40 @@
 
 
 def widen_kernel(side_ref, part_ref, *refs):
-    for i, out_ref in enumerate(refs[-4:]):
-        out_ref[...] = part_ref[i].astype(f32)
+    out_refs, (wide_ref, sems) = refs[-6:-2], refs[-2:]
+    half = part_ref.shape[2]
+    columns = pl.ds(pl.multiple_of(side_ref[0] * half, half), half)
+    copies = []
+    for i, out_ref in enumerate(out_refs):
+        wide_ref[i] = part_ref[i].astype(f32)
+        copies.append(
+            pltpu.make_async_copy(wide_ref.at[i], out_ref.at[:, columns], sems.at[i])
+        )
+        copies[-1].start()
+    for copy in copies:
+        copy.wait()
 
 
 def widen(side, part, grads):
     half = part.shape[1]
     width = 2 * half
-    steps = 4
     given = () if grads is None else tuple(grads)
-    block_in = pl.BlockSpec((4, width // steps, half), lambda i, side: (0, i, 0))
-    block_out = pl.BlockSpec((width // steps, half), lambda i, side: (i, side[0]))
+    hbm = pl.BlockSpec(memory_space=pltpu.HBM)
     return pl.pallas_call(
         widen_kernel,
         out_shape=(jax.ShapeDtypeStruct((width, width), f32),) * 4,
-        grid_spec=pltpu.PrefetchScalarGridSpec(
-            num_scalar_prefetch=1,
-            grid=(steps,),
-            in_specs=[block_in] + [pl.BlockSpec(memory_space=pl.ANY)] * len(given),
-            out_specs=(block_out,) * 4,
-        ),
+        in_specs=[
+            pl.BlockSpec(memory_space=pltpu.SMEM),
+            pl.BlockSpec(memory_space=pltpu.VMEM),
+        ]
+        + [hbm] * len(given),
+        out_specs=(hbm,) * 4,
+        scratch_shapes=[
+            pltpu.VMEM((4, width, half), f32),
+            pltpu.SemaphoreType.DMA((4,)),
+        ],
         input_output_aliases={2 + i: i for i in range(len(given))},
-        compiler_params=pltpu.CompilerParams(vmem_limit_bytes=48 << 20),
+        compiler_params=pltpu.CompilerParams(vmem_limit_bytes=32 << 20),
         name="widen_kernel",
     )(side.reshape(1), part.reshape(4, width, half), *given)
 
@@ -202,10 +215,9 @@
     return lax.ppermute(value, EVERY, [(i, (i + steps) % count) for i in range(count)])
 
 
-def spread(value, axes, count):
+def copied(value, count):
     rows, width = value.shape
-    copies = jnp.broadcast_to(value[None], (count, rows, width)).reshape(count * rows, width)
-    return lax.all_to_all(copies, axes, 0, 0, tiled=True)
+    return jnp.broadcast_to(value[None], (count, rows, width)).reshape(count * rows, width)
 
 
 def after(value, *others):
@@ -215,17 +227,14 @@
 def per_device(cells, encoded, w_query, w_key, w_value, w_out, pattern, cell_basin, pooled_grad):
     width = cells.shape[1]
     half = width // 2
-    plane, depth = SIZES["y"] * SIZES["x"], SIZES["z"]
     core = lax.axis_index("c")
     device = lax.axis_index(EVERY)
     own = pooled_grad.shape[0]
     total = own * lax.axis_size(EVERY)
 
-    tiles = ("y", "z", "x")
     rows_own = lax.dynamic_slice_in_dim(encoded, core * half, half, 1)
-    copies = jnp.broadcast_to(rows_own[None], (plane * depth,) + rows_own.shape)
-    copies = copies.reshape(plane * depth * rows_own.shape[0], half)
-    mine = lax.all_to_all(copies, tiles, 0, 0, tiled=True)
+    copies = copied(rows_own, MEMBERS * SIZES["far"])
+    mine = lax.all_to_all(copies, TILES, 0, 0, tiled=True)
     other = swap(mine)
 
     slot = (cell_basin - device * own + own) % total
@@ -255,9 +264,11 @@
 
     block = pattern[0]
     along_x = block % SIZES["x"]
-    along_z = (block // SIZES["x"]) % depth
-    along_y = block // (SIZES["x"] * depth)
-    place = (along_y * SIZES["x"] + along_x) * depth + along_z
+    near = (block // SIZES["x"]) % SIZES["near"]
+    far_z = (block // (SIZES["x"] * SIZES["near"])) % SIZES["far"]
+    along_y = block // (SIZES["x"] * SIZES["near"] * SIZES["far"])
+    place = (along_y * SIZES["x"] + along_x) * SIZES["near"] + near
+    place = place * SIZES["far"] + far_z
     within = jnp.arange(GAUGE_ROWS, dtype=jnp.int32)[None, :]
     rows = (block[:, None] * GAUGE_ROWS + within).reshape(1, KEYS)
     places = (place[:, None] * GAUGE_ROWS + within).reshape(1, KEYS)
@@ -292,29 +303,29 @@
     )
 
     chip = (keep.astype(f32) + swap(send).astype(f32)).astype(bf16)
-    chunk = payload // plane
-    gauge_chunk = gauges // plane
+    chunk = payload // MEMBERS
+    gauge_chunk = gauges // MEMBERS
     weight_chunk = chunk - gauge_chunk
-    parts = lax.all_to_all(chip, PLANE, 0, 0, tiled=True).reshape(plane, chunk, half)
+    parts = lax.all_to_all(chip, GROUP, 0, 0, tiled=True).reshape(MEMBERS, chunk, half)
     column = jnp.sum(parts.astype(f32), axis=0).astype(bf16)
-    column = jnp.concatenate(
-        [
-            column[:weight_chunk].reshape(depth, weight_chunk // depth, half),
-            column[weight_chunk:].reshape(depth, gauge_chunk // depth, half),
-        ],
-        axis=1,
-    )
-    parts = lax.all_to_all(column, "z", 0, 0, tiled=True)
-    reduced = jnp.sum(parts.astype(f32), axis=0).astype(bf16)
-    own_weight = reduced[: weight_chunk // depth]
-    own_gauge = reduced[weight_chunk // depth :]
-
-    line = spread(own_weight, "z", depth)
-    late_sums, late_gauge = lax.optimization_barrier((sums, own_gauge))
+    count = SIZES["far"]
+    turns = [
+        lax.ppermute(column, "far", [(i, (i + s) % count) for i in range(count)])
+        for s in range(1, count)
+    ]
+    reduced = (
+        (column.astype(f32) + turns[1].astype(f32)) + (turns[0].astype(f32) + turns[2].astype(f32))
+    ).astype(bf16)
+    own_gauge = lax.dynamic_slice_in_dim(
+        reduced, weight_chunk + lax.axis_index("far") * GAUGE_ROWS, GAUGE_ROWS, 0
+    )
+
+    copies = copied(reduced[:weight_chunk], MEMBERS)
+    weights = lax.all_to_all(copies, GROUP, 0, 0, tiled=True)
+    late_sums, late_gauge = lax.optimization_barrier((sums, own_gauge, copies))[:2]
     far_gauge = swap(late_gauge)
     from_above, from_below = shifted(late_sums[low], -1), shifted(late_sums[top], 1)
-    line = after(line, far_gauge, from_above, from_below)
-    weights = spread(line, PLANE, plane)
+    weights = after(weights, far_gauge, from_above, from_below)
     pooled = ((sums[mid] + from_above + from_below) / roots[mid][:, None]).astype(bf16)
     grad_gauges = jnp.where(
         core == 0,
@@ -329,14 +340,13 @@
 
 def solution(mesh):
     grid = Mesh(mesh.devices.reshape(tuple(SIZES[a] for a in EVERY)), EVERY)
-    tiles = ("y", "z", "x")
     return jax.shard_map(
         per_device,
         mesh=grid,
         in_specs=(
-            P(EVERY, None), P(tiles, None), P(), P(), P(), P(),
+            P(EVERY, None), P(TILES, None), P(), P(), P(), P(),
             P(EVERY, None), P(EVERY), P(EVERY, None),
         ),
-        out_specs=(P(EVERY, None), P(EVERY, None), P(tiles, None), P(), P(), P(), P()),
+        out_specs=(P(EVERY, None), P(EVERY, None), P(TILES, None), P(), P(), P(), P()),
         check_vma=False,
     )

time: 126 us -> 118 us (0.937)
  blocking collectives: 50.3 us -> 25.9 us
  waiting for transfers between devices: 15.2 us -> 26.6 us
  starting transfers between devices: 44.7 us -> 49 us
    all_to_all x3 -> x1, blocking collectives: 50.3 us -> 25.9 us  [per_device(): lax.all_to_all(chip, GROUP, 0, 0, tiled=True).reshape(MEMBERS, chunk, half)]
    ppermute x0 -> x3, waiting for transfers between devices: none -> 6.84 us  [per_device(): lax.ppermute(column, 'far', [(i, (i + s) % count) for i in range(count)])]
    ppermute x6, waiting for transfers between devices: 6.58 us -> 11.4 us  [shifted(): lax.ppermute(value, EVERY, [(i, (i + steps) % count) for i in range(count)])]
    ppermute x0 -> x3, starting transfers between devices: none -> 2.44 us  [per_device(): lax.ppermute(column, 'far', [(i, (i + s) % count) for i in range(count)])]
    ppermute x6, starting transfers between devices: 11.6 us -> 13.6 us  [shifted(): lax.ppermute(value, EVERY, [(i, (i + steps) % count) for i in range(count)])]
  transfers between devices with their start and end apart: 12 -> 15, of which waited for: 9 -> 10; matrix products, arithmetic and copies ran while one was open for 2% -> 2% of each run, Pallas kernels for 1% -> 1%
where the time goes in v5:
time: 118 us; the launch traced here: 117 us
  starting transfers between devices  49 us (42%)
  waiting for transfers between devices  26.6 us (23%)
  blocking collectives  25.9 us (22%)
  Pallas kernels  9.46 us (8%)
  local copies, waits for them, and re-layouts  2.88 us (2%)
  other arithmetic  2.47 us (2%)
    all_to_all x1, blocking collectives, per_device(): lax.all_to_all(chip, GROUP, 0, 0, tiled=True).reshape(MEMBERS, chunk, half)  25.9 us
    all_to_all x1, starting transfers between devices, per_device(): mine = lax.all_to_all(copies, TILES, 0, 0, tiled=True)  16.3 us
    ppermute x6, starting transfers between devices, shifted(): lax.ppermute(value, EVERY, [(i, (i + steps) % count) for i in range(count)])  13.6 us
    ppermute x4, starting transfers between devices, swap(): return lax.ppermute(value, 'c', [(0, 1), (1, 0)])  12.6 us
    ppermute x6, waiting for transfers between devices, shifted(): lax.ppermute(value, EVERY, [(i, (i + steps) % count) for i in range(count)])  11.4 us
    ppermute x3, waiting for transfers between devices, per_device(): lax.ppermute(column, 'far', [(i, (i + s) % count) for i in range(count)])  6.84 us
    pallas_call x1, Pallas kernels, per_device(): pl.pallas_call(group_kernel, out_shape=(jax.ShapeDtypeStruct(cells.shape,...  6.69 us
    ppermute x4, waiting for transfers between devices, swap(): return lax.ppermute(value, 'c', [(0, 1), (1, 0)])  4.33 us
  transfers between devices with their start and end apart: 15, of which 10 were waited for; matrix products, arithmetic and copies ran while one was open for 2% of the time, Pallas kernels for 1%

profile of v5, /device:TPU:1, one launch (start us, length us, event | category | flops | bytes accessed | tf_op | source)
XLA Modules:
  0.0 117.3 jit_solution(5285134684211066180)
XLA Ops:
  0.7 0.6 copy-done
  1.3 0.8 broadcast_in_dim.10
  2.2 16.3 %all-to-all-start = ((bf16[128,8,256]{2,1,0:T(8,128)(2,1)}), bf16[128,8,256]{2,1,0:T(8,128)(2,1)S(1)}, u32[]{:S(2)}, u32[]{:S(2)}) async-start(bf16[128,8,256]{2,1,0:T(8,128)(2,1)} %broadcast_in_dim.10), calls=%async_computation | async-start | bytes 1048576 | tf_op jit(solution)/shard_map/all_to_all | solution.py:237
  18.7 6.8 %collective-permute-start.3 = (bf16[1,128]{1,0:T(2,128)(2,1)S(1)}, bf16[1,128]{1,0:T(2,128)(2,1)S(1)}, u32[]{:S(2)}, u32[]{:S(2)}) collective-permute-start(bf16[1,128]{1,0:T(2,128)(2,1)S(1)} %slice.109), channel_id=1, source_target_pairs={{0,254},{1,255},{2,0},{3,1},{4,2},{5,3},{6,4},{7,5},{8,6},{9,7},{1... | collective-permute-start | bytes 776 | tf_op jit(solution)/shard_map/ppermute | solution.py:215
  25.6 1.5 %collective-permute-start.1 = (bf16[3,512]{1,0:T(4,128)(2,1)S(1)}, bf16[3,512]{1,0:T(4,128)(2,1)S(1)}, u32[]{:S(2)}, u32[]{:S(2)}) collective-permute-start(bf16[3,512]{1,0:T(4,128)(2,1)S(1)} %pad_maximum_fusion), channel_id=1, source_target_pairs={{0,255},{1,0},{2,1},{3,2},{4,3},{5,4},{6,5},{7,6},{8,7},{9,8},{10,... | collective-permute-start | bytes 9224 | tf_op jit(solution)/shard_map/ppermute | solution.py:215
  27.1 0.2 collective-permute-start
  27.6 1.3 %collective-permute-done.1 = bf16[3,512]{1,0:T(4,128)(2,1)S(1)} collective-permute-done((bf16[3,512]{1,0:T(4,128)(2,1)S(1)}, bf16[3,512]{1,0:T(4,128)(2,1)S(1)}, u32[]{:S(2)}, u32[]{:S(2)}) %collective-permute-start.1) | collective-permute-done | bytes 3104 | tf_op jit(solution)/shard_map/ppermute | solution.py:215
  28.9 4.6 %collective-permute-done = bf16[3,512]{1,0:T(4,128)(2,1)S(1)} collective-permute-done((bf16[3,512]{1,0:T(4,128)(2,1)S(1)}, bf16[3,512]{1,0:T(4,128)(2,1)S(1)}, u32[]{:S(2)}, u32[]{:S(2)}) %collective-permute-start) | collective-permute-done | bytes 3104 | tf_op jit(solution)/shard_map/ppermute | solution.py:215
  33.5 1.8 %all-to-all-done = bf16[128,8,256]{2,1,0:T(8,128)(2,1)S(1)} async-done(((bf16[128,8,256]{2,1,0:T(8,128)(2,1)}), bf16[128,8,256]{2,1,0:T(8,128)(2,1)S(1)}, u32[]{:S(2)}, u32[]{:S(2)}) %all-to-all-start) | async-done | bytes 524320 | tf_op jit(solution)/shard_map/all_to_all | solution.py:237
  35.4 6.1 %collective-permute-start.4 = (bf16[1024,256]{1,0:T(8,128)(2,1)S(1)}, bf16[1024,256]{1,0:T(8,128)(2,1)S(1)}, u32[]{:S(2)}, u32[]{:S(2)}) collective-permute-start(bf16[1024,256]{1,0:T(8,128)(2,1)S(1)} %bitcast.46), channel_id=1, source_target_pairs={{0,1},{1,0},{2,3},{3,2},{4,5},{5,4},{6,7},{7,6},{8,9},{9,8},{10,11... | collective-permute-start | bytes 1572872 | tf_op jit(solution)/shard_map/ppermute | solution.py:210
  41.7 1.3 %collective-permute-done.4.other_ref = bf16[1024,256]{1,0:T(8,128)(2,1)S(1)} collective-permute-done((bf16[1024,256]{1,0:T(8,128)(2,1)S(1)}, bf16[1024,256]{1,0:T(8,128)(2,1)S(1)}, u32[]{:S(2)}, u32[]{:S(2)}) %collective-permute-start.4) | collective-permute-done | bytes 524320 | tf_op jit(solution)/shard_map/ppermute | solution.py:210
  43.0 6.7 %group_kernel.1 = (bf16[256,512]{1,0:T(8,128)(2,1)}, f32[16,512]{1,0:T(8,128)S(1)}, bf16[3072,256]{1,0:T(8,128)(2,1)S(1)}, bf16[3072,256]{1,0:T(8,128)(2,1)S(1)}) custom-call(s32[1]{0:T(128)} %bitcast.core_ref.side_ref, s32[1,128]{1,0:T(1,128)S(1)} %add.189.rows_ref, s32[1,128]{1,0:T(1,128)S(1)} %add.199.places_ref, s32[1,256]{1,0:T(1,128)S(1)} %bitcast.49, ...), custom_call_target="tpu_custom_call" | custom-call | tf_op jit(solution)/shard_map/group_kernel/pallas_call | solution.py:281
  49.7 0.5 collective-permute-start.5
  50.2 3.0 %collective-permute-done.5 = bf16[3072,256]{1,0:T(8,128)(2,1)S(1)} collective-permute-done((bf16[3072,256]{1,0:T(8,128)(2,1)S(1)}, bf16[3072,256]{1,0:T(8,128)(2,1)S(1)}, u32[]{:S(2)}, u32[]{:S(2)}) %collective-permute-start.5) | collective-permute-done | bytes 1572896 | tf_op jit(solution)/shard_map/ppermute | solution.py:210
  53.2 0.5 add_convert_fusion
  53.7 25.9 %all_to_all.26 = bf16[32,96,256]{2,1,0:T(8,128)(2,1)S(1)} all-to-all(bf16[32,96,256]{2,1,0:T(8,128)(2,1)S(1)} %bitcast.50), channel_id=1, replica_groups=mesh['y'=4,'far'=4,'near'=2,'x'=4,'c'=2] {'y','x','near'}, dimensions={0} | all-to-all | bytes 3145728 | tf_op jit(solution)/shard_map/all_to_all | solution.py:309
  79.9 2.4 %collective-permute-start.7 = (bf16[96,256]{1,0:T(8,128)(2,1)S(1)}, bf16[96,256]{1,0:T(8,128)(2,1)S(1)}, u32[]{:S(2)}, u32[]{:S(2)}) collective-permute-start(bf16[96,256]{1,0:T(8,128)(2,1)S(1)} %reduce_sum.22), channel_id=1, source_target_pairs={{0,16},{16,32},{32,48},{48,0},{1,17},{17,33},{33,49},{49,1},{2,18}... | collective-permute-start | bytes 147464 | tf_op jit(solution)/shard_map/ppermute | solution.py:313
  82.3 2.0 %collective-permute-done.8 = bf16[96,256]{1,0:T(8,128)(2,1)S(1)} collective-permute-done((bf16[96,256]{1,0:T(8,128)(2,1)S(1)}, bf16[96,256]{1,0:T(8,128)(2,1)S(1)}, u32[]{:S(2)}, u32[]{:S(2)}) %collective-permute-start.8) | collective-permute-done | bytes 49184 | tf_op jit(solution)/shard_map/ppermute | solution.py:313
  84.3 1.0 collective-permute-done.7
  85.3 3.8 %collective-permute-done.6 = bf16[96,256]{1,0:T(8,128)(2,1)S(1)} collective-permute-done((bf16[96,256]{1,0:T(8,128)(2,1)S(1)}, bf16[96,256]{1,0:T(8,128)(2,1)S(1)}, u32[]{:S(2)}, u32[]{:S(2)}) %collective-permute-start.6) | collective-permute-done | bytes 49184 | tf_op jit(solution)/shard_map/ppermute | solution.py:313
  89.1 1.1 broadcast_in_dim.11
  90.2 3.9 %all-to-all-start.2 = ((bf16[32,64,256]{2,1,0:T(8,128)(2,1)}), bf16[32,64,256]{2,1,0:T(8,128)(2,1)S(1)}, u32[]{:S(2)}, u32[]{:S(2)}) async-start(bf16[32,64,256]{2,1,0:T(8,128)(2,1)} %broadcast_in_dim.11), calls=%async_computation.2 | async-start | bytes 2097152 | tf_op jit(solution)/shard_map/all_to_all | solution.py:324
  94.2 3.6 %collective-permute-start.9 = (f32[2,512]{1,0:T(2,128)S(1)}, f32[2,512]{1,0:T(2,128)S(1)}, u32[]{:S(2)}, u32[]{:S(2)}) collective-permute-start(f32[2,512]{1,0:T(2,128)S(1)} %get-tuple-element.37), channel_id=1, source_target_pairs={{0,255},{1,0},{2,1},{3,2},{4,3},{5,4},{6,5},{7,6},{8,7},{9,8},{10,... | collective-permute-start | bytes 12296 | tf_op jit(solution)/shard_map/ppermute | solution.py:215
  97.8 1.5 %collective-permute-start.10 = (f32[2,512]{1,0:T(2,128)S(1)}, f32[2,512]{1,0:T(2,128)S(1)}, u32[]{:S(2)}, u32[]{:S(2)}) collective-permute-start(f32[2,512]{1,0:T(2,128)S(1)} %get-tuple-element.38), channel_id=1, source_target_pairs={{0,1},{1,2},{2,3},{3,4},{4,5},{5,6},{6,7},{7,8},{8,9},{9,10},{10,1... | collective-permute-start | bytes 12296 | tf_op jit(solution)/shard_map/ppermute | solution.py:215
  99.3 1.9 %collective-permute-start.11 = (bf16[8,256]{1,0:T(8,128)(2,1)S(1)}, bf16[8,256]{1,0:T(8,128)(2,1)S(1)}, u32[]{:S(2)}, u32[]{:S(2)}) collective-permute-start(bf16[8,256]{1,0:T(8,128)(2,1)S(1)} %constant_dynamic-slice_fusion), channel_id=1, source_target_pairs={{0,1},{1,0},{2,3},{3,2},{4,5},{5,4},{6,7},{7,6},{8,9},{9,8},{10,11... | collective-permute-start | bytes 12296 | tf_op jit(solution)/shard_map/ppermute | solution.py:210
  101.1 5.5 %collective-permute-done.9 = f32[2,512]{1,0:T(2,128)S(1)} collective-permute-done((f32[2,512]{1,0:T(2,128)S(1)}, f32[2,512]{1,0:T(2,128)S(1)}, u32[]{:S(2)}, u32[]{:S(2)}) %collective-permute-start.9) | collective-permute-done | bytes 4128 | tf_op jit(solution)/shard_map/ppermute | solution.py:215
  106.7 2.2 %all-to-all-done.2 = bf16[32,64,256]{2,1,0:T(8,128)(2,1)S(1)} async-done(((bf16[32,64,256]{2,1,0:T(8,128)(2,1)}), bf16[32,64,256]{2,1,0:T(8,128)(2,1)S(1)}, u32[]{:S(2)}, u32[]{:S(2)}) %all-to-all-start.2) | async-done | bytes 1048608 | tf_op jit(solution)/shard_map/all_to_all | solution.py:324
  108.9 4.2 %collective-permute-start.12 = (bf16[2048,256]{1,0:T(8,128)(2,1)S(1)}, bf16[2048,256]{1,0:T(8,128)(2,1)S(1)}, u32[]{:S(2)}, u32[]{:S(2)}) collective-permute-start(bf16[2048,256]{1,0:T(8,128)(2,1)S(1)} %bitcast.44), channel_id=1, source_target_pairs={{0,1},{1,0},{2,3},{3,2},{4,5},{5,4},{6,7},{7,6},{8,9},{9,8},{10,11... | collective-permute-start | bytes 3145736 | tf_op jit(solution)/shard_map/ppermute | solution.py:210
  113.1 0.6 maximum_select_fusion
  113.7 0.7 fusion
  114.4 1.4 %widen_kernel.2 = (f32[512,512]{1,0:T(8,128)}, f32[512,512]{1,0:T(8,128)}, f32[512,512]{1,0:T(8,128)}, f32[512,512]{1,0:T(8,128)}) custom-call(s32[1]{0:T(128)} %bitcast.core_ref.side_ref, bf16[4,512,256]{2,1,0:T(8,128)(2,1)S(1)} %bitcast.45), custom_call_target="tpu_custom_call" | custom-call | tf_op jit(solution)/shard_map/widen_kernel/pallas_call | solution.py:190
  115.8 1.4 %widen_kernel.3 = (f32[512,512]{1,0:T(8,128)}, f32[512,512]{1,0:T(8,128)}, f32[512,512]{1,0:T(8,128)}, f32[512,512]{1,0:T(8,128)}) custom-call(s32[1]{0:T(128)} %bitcast.10.side_ref, bf16[4,512,256]{2,1,0:T(8,128)(2,1)S(1)} %bitcast.48, ...), custom_call_target="tpu_custom_call", output_to_operand_aliasing={{0}: (2, {}), {1}: (3, {}), {2}: (4, {}), {3}: (5, {})} | custom-call | tf_op jit(solution)/shard_map/widen_kernel/pallas_call | solution.py:190
  (47 shorter events, 1.2 us)
Async XLA Ops:
  0.6 0.7 copy-start
  0.7 17.9 %copy-start.5 = (s32[256]{0:T(256)S(1)}, s32[256]{0:T(256)}, u32[]{:S(2)}) copy-start(s32[256]{0:T(256)} %param.16) | copy-start | bytes 3076
  0.7 18.0 %copy-start.4 = (bf16[2,512]{1,0:T(2,128)(2,1)S(1)}, bf16[2,512]{1,0:T(2,128)(2,1)}, u32[]{:S(2)}) copy-start(bf16[2,512]{1,0:T(2,128)(2,1)} %param.17) | copy-start | bytes 6148
  0.7 26.7 %copy-start.6 = (s32[1,16]{1,0:T(1,128)S(1)}, s32[1,16]{1,0:T(1,128)}, u32[]{:S(2)}) copy-start(s32[1,16]{1,0:T(1,128)} %param.15) | copy-start | bytes 196
  0.7 42.3 %copy-start.2 = (bf16[512,512]{1,0:T(8,128)(2,1)S(1)}, bf16[512,512]{1,0:T(8,128)(2,1)}, u32[]{:S(2)}) copy-start(bf16[512,512]{1,0:T(8,128)(2,1)} %wv_ref.1) | copy-start | bytes 1572868
  0.7 42.3 %copy-start.1 = (bf16[512,512]{1,0:T(8,128)(2,1)S(1)}, bf16[512,512]{1,0:T(8,128)(2,1)}, u32[]{:S(2)}) copy-start(bf16[512,512]{1,0:T(8,128)(2,1)} %wk_ref.1) | copy-start | bytes 1572868
  0.7 42.3 %copy-start.3 = (bf16[512,512]{1,0:T(8,128)(2,1)S(1)}, bf16[512,512]{1,0:T(8,128)(2,1)}, u32[]{:S(2)}) copy-start(bf16[512,512]{1,0:T(8,128)(2,1)} %wq_ref.1) | copy-start | bytes 1572868
  2.2 33.2 %all-to-all-start = ((bf16[128,8,256]{2,1,0:T(8,128)(2,1)}), bf16[128,8,256]{2,1,0:T(8,128)(2,1)S(1)}, u32[]{:S(2)}, u32[]{:S(2)}) async-start(bf16[128,8,256]{2,1,0:T(8,128)(2,1)} %broadcast_in_dim.10), calls=%async_computation | async-start | bytes 1048576 | tf_op jit(solution)/shard_map/all_to_all | solution.py:237
  18.7 22.7 %collective-permute-start.3 = (bf16[1,128]{1,0:T(2,128)(2,1)S(1)}, bf16[1,128]{1,0:T(2,128)(2,1)S(1)}, u32[]{:S(2)}, u32[]{:S(2)}) collective-permute-start(bf16[1,128]{1,0:T(2,128)(2,1)S(1)} %slice.109), channel_id=1, source_target_pairs={{0,254},{1,255},{2,0},{3,1},{4,2},{5,3},{6,4},{7,5},{8,6},{9,7},{1... | collective-permute-start | bytes 776 | tf_op jit(solution)/shard_map/ppermute | solution.py:215
  25.6 15.9 %collective-permute-start.2 = (bf16[1,128]{1,0:T(2,128)(2,1)S(1)}, bf16[1,128]{1,0:T(2,128)(2,1)S(1)}, u32[]{:S(2)}, u32[]{:S(2)}) collective-permute-start(bf16[1,128]{1,0:T(2,128)(2,1)S(1)} %slice.109), channel_id=1, source_target_pairs={{0,2},{1,3},{2,4},{3,5},{4,6},{5,7},{6,8},{7,9},{8,10},{9,11},{10,... | collective-permute-start | bytes 776 | tf_op jit(solution)/shard_map/ppermute | solution.py:215
  25.6 3.3 %collective-permute-start.1 = (bf16[3,512]{1,0:T(4,128)(2,1)S(1)}, bf16[3,512]{1,0:T(4,128)(2,1)S(1)}, u32[]{:S(2)}, u32[]{:S(2)}) collective-permute-start(bf16[3,512]{1,0:T(4,128)(2,1)S(1)} %pad_maximum_fusion), channel_id=1, source_target_pairs={{0,255},{1,0},{2,1},{3,2},{4,3},{5,4},{6,5},{7,6},{8,7},{9,8},{10,... | collective-permute-start | bytes 9224 | tf_op jit(solution)/shard_map/ppermute | solution.py:215
  27.1 6.4 %collective-permute-start = (bf16[3,512]{1,0:T(4,128)(2,1)S(1)}, bf16[3,512]{1,0:T(4,128)(2,1)S(1)}, u32[]{:S(2)}, u32[]{:S(2)}) collective-permute-start(bf16[3,512]{1,0:T(4,128)(2,1)S(1)} %pad_maximum_fusion), channel_id=1, source_target_pairs={{0,1},{1,2},{2,3},{3,4},{4,5},{5,6},{6,7},{7,8},{8,9},{9,10},{10,1... | collective-permute-start | bytes 9224 | tf_op jit(solution)/shard_map/ppermute | solution.py:215
  35.4 7.6 %collective-permute-start.4 = (bf16[1024,256]{1,0:T(8,128)(2,1)S(1)}, bf16[1024,256]{1,0:T(8,128)(2,1)S(1)}, u32[]{:S(2)}, u32[]{:S(2)}) collective-permute-start(bf16[1024,256]{1,0:T(8,128)(2,1)S(1)} %bitcast.46), channel_id=1, source_target_pairs={{0,1},{1,0},{2,3},{3,2},{4,5},{5,4},{6,7},{7,6},{8,9},{9,8},{10,11... | collective-permute-start | bytes 1572872 | tf_op jit(solution)/shard_map/ppermute | solution.py:210
  49.7 3.5 %collective-permute-start.5 = (bf16[3072,256]{1,0:T(8,128)(2,1)S(1)}, bf16[3072,256]{1,0:T(8,128)(2,1)S(1)}, u32[]{:S(2)}, u32[]{:S(2)}) collective-permute-start(bf16[3072,256]{1,0:T(8,128)(2,1)S(1)} %get-tuple-element.24), channel_id=1, source_target_pairs={{0,1},{1,0},{2,3},{3,2},{4,5},{5,4},{6,7},{7,6},{8,9},{9,8},{10,11... | collective-permute-start | bytes 4718600 | tf_op jit(solution)/shard_map/ppermute | solution.py:210
  79.8 4.4 %collective-permute-start.8 = (bf16[96,256]{1,0:T(8,128)(2,1)S(1)}, bf16[96,256]{1,0:T(8,128)(2,1)S(1)}, u32[]{:S(2)}, u32[]{:S(2)}) collective-permute-start(bf16[96,256]{1,0:T(8,128)(2,1)S(1)} %reduce_sum.22), channel_id=1, source_target_pairs={{0,48},{16,0},{32,16},{48,32},{1,49},{17,1},{33,17},{49,33},{2,50}... | collective-permute-start | bytes 147464 | tf_op jit(solution)/shard_map/ppermute | solution.py:313
  79.9 5.4 %collective-permute-start.7 = (bf16[96,256]{1,0:T(8,128)(2,1)S(1)}, bf16[96,256]{1,0:T(8,128)(2,1)S(1)}, u32[]{:S(2)}, u32[]{:S(2)}) collective-permute-start(bf16[96,256]{1,0:T(8,128)(2,1)S(1)} %reduce_sum.22), channel_id=1, source_target_pairs={{0,16},{16,32},{32,48},{48,0},{1,17},{17,33},{33,49},{49,1},{2,18}... | collective-permute-start | bytes 147464 | tf_op jit(solution)/shard_map/ppermute | solution.py:313
  82.3 6.8 %collective-permute-start.6 = (bf16[96,256]{1,0:T(8,128)(2,1)S(1)}, bf16[96,256]{1,0:T(8,128)(2,1)S(1)}, u32[]{:S(2)}, u32[]{:S(2)}) collective-permute-start(bf16[96,256]{1,0:T(8,128)(2,1)S(1)} %reduce_sum.22), channel_id=1, source_target_pairs={{0,32},{16,48},{32,0},{48,16},{1,33},{17,49},{33,1},{49,17},{2,34}... | collective-permute-start | bytes 147464 | tf_op jit(solution)/shard_map/ppermute | solution.py:313
  90.2 18.6 %all-to-all-start.2 = ((bf16[32,64,256]{2,1,0:T(8,128)(2,1)}), bf16[32,64,256]{2,1,0:T(8,128)(2,1)S(1)}, u32[]{:S(2)}, u32[]{:S(2)}) async-start(bf16[32,64,256]{2,1,0:T(8,128)(2,1)} %broadcast_in_dim.11), calls=%async_computation.2 | async-start | bytes 2097152 | tf_op jit(solution)/shard_map/all_to_all | solution.py:324
  94.2 12.4 %collective-permute-start.9 = (f32[2,512]{1,0:T(2,128)S(1)}, f32[2,512]{1,0:T(2,128)S(1)}, u32[]{:S(2)}, u32[]{:S(2)}) collective-permute-start(f32[2,512]{1,0:T(2,128)S(1)} %get-tuple-element.37), channel_id=1, source_target_pairs={{0,255},{1,0},{2,1},{3,2},{4,3},{5,4},{6,5},{7,6},{8,7},{9,8},{10,... | collective-permute-start | bytes 12296 | tf_op jit(solution)/shard_map/ppermute | solution.py:215
  97.8 8.9 %collective-permute-start.10 = (f32[2,512]{1,0:T(2,128)S(1)}, f32[2,512]{1,0:T(2,128)S(1)}, u32[]{:S(2)}, u32[]{:S(2)}) collective-permute-start(f32[2,512]{1,0:T(2,128)S(1)} %get-tuple-element.38), channel_id=1, source_target_pairs={{0,1},{1,2},{2,3},{3,4},{4,5},{5,6},{6,7},{7,8},{8,9},{9,10},{10,1... | collective-permute-start | bytes 12296 | tf_op jit(solution)/shard_map/ppermute | solution.py:215
  99.3 7.4 %collective-permute-start.11 = (bf16[8,256]{1,0:T(8,128)(2,1)S(1)}, bf16[8,256]{1,0:T(8,128)(2,1)S(1)}, u32[]{:S(2)}, u32[]{:S(2)}) collective-permute-start(bf16[8,256]{1,0:T(8,128)(2,1)S(1)} %constant_dynamic-slice_fusion), channel_id=1, source_target_pairs={{0,1},{1,0},{2,3},{3,2},{4,5},{5,4},{6,7},{7,6},{8,9},{9,8},{10,11... | collective-permute-start | bytes 12296 | tf_op jit(solution)/shard_map/ppermute | solution.py:210
  108.9 6.9 %collective-permute-start.12 = (bf16[2048,256]{1,0:T(8,128)(2,1)S(1)}, bf16[2048,256]{1,0:T(8,128)(2,1)S(1)}, u32[]{:S(2)}, u32[]{:S(2)}) collective-permute-start(bf16[2048,256]{1,0:T(8,128)(2,1)S(1)} %bitcast.44), channel_id=1, source_target_pairs={{0,1},{1,0},{2,3},{3,2},{4,5},{5,4},{6,7},{7,6},{8,9},{9,8},{10,11... | collective-permute-start | bytes 3145736 | tf_op jit(solution)/shard_map/ppermute | solution.py:210

commit v6 on v5

--- a/solution.py
+++ b/solution.py
@@ -45,17 +45,16 @@
 
 
 def group_kernel(
-    core_ref, rows_ref, places_ref, slot_ref, table_ref, mine_ref, other_ref,
-    wk_ref, wv_ref, wq_ref, cells_hbm, wo_hbm,
+    core_ref, places_ref, slot_ref, own_ref, below_ref, above_ref, below_two_ref, above_two_ref,
+    mine_ref, other_ref, wk_ref, wv_ref, wq_ref, cells_hbm, wo_hbm,
     grad_cells_ref, sums_ref, keep_ref, send_ref,
-    cells_ref, wo_ref, sems,
+    cells_ref, wo_ref, table_ref, sems,
 ):
     load_cells = pltpu.make_async_copy(cells_hbm, cells_ref, sems.at[0])
     load_wo = pltpu.make_async_copy(wo_hbm, wo_ref, sems.at[1])
     load_cells.start()
     load_wo.start()
-    core = core_ref[0]
-    first = core == 0
+    first = core_ref[0] == 0
     width = 2 * mine_ref.shape[1]
     half = width // 2
     gauges = mine_ref.shape[0]
@@ -78,92 +77,119 @@
                 value[j * weight_chunk : (j + 1) * weight_chunk, :],
             )
 
-    gauge_ids = lax.broadcasted_iota(jnp.int32, (gauges, KEYS), 0)
-    picks = jnp.where(gauge_ids == rows_ref[...], 1.0, 0.0).astype(bf16)
-    sel_mine = mm_rows(picks, mine_ref[...])
-    sel_other = mm_rows(picks, other_ref[...])
+    down = jnp.broadcast_to(places_ref[...], (KEYS, KEYS)).T
+    lanes = lax.broadcasted_iota(jnp.int32, (KEYS, KEYS), 1)
+    picks = jnp.concatenate(
+        [
+            jnp.where(lanes + j * KEYS == down, 1.0, 0.0).astype(bf16)
+            for j in range(gauges // KEYS)
+        ],
+        axis=1,
+    )
+    sel_mine = mm(picks, mine_ref[...])
+    sel_other = mm(picks, other_ref[...])
     encoded_sel = jnp.concatenate(
         [jnp.where(first, sel_mine, sel_other), jnp.where(first, sel_other, sel_mine)], axis=1
     ).astype(bf16)
     keys = mm(encoded_sel, wk_ref[...]).astype(bf16)
     values = mm(encoded_sel, wv_ref[...]).astype(bf16)
+    scale = 1.0 / math.sqrt(HEAD_DIM)
     load_cells.wait()
-    queries = mm(cells_ref[...], wq_ref[...]).astype(bf16)
+    queries = mm(cells_ref[...], wq_ref[...]).astype(bf16) * jnp.asarray(scale, bf16)
     even = lax.broadcasted_iota(jnp.int32, (KEYS, PAIR), 1) < HEAD_DIM
+    upper = lax.broadcasted_iota(jnp.int32, (PAIR, KEYS), 0) < HEAD_DIM
     zero = jnp.zeros((KEYS, PAIR), bf16)
-    scale = 1.0 / math.sqrt(HEAD_DIM)
+
+    def both(value):
+        return jnp.concatenate([jnp.where(even, value, zero), jnp.where(even, zero, value)], axis=0)
+
+    def both_across(value):
+        turned = value.T
+        return jnp.concatenate(
+            [jnp.where(upper, turned, zero), jnp.where(upper, zero, turned)], axis=1
+        )
 
     saved = []
     attended = []
     for p in range(pairs):
         columns = slice(p * PAIR, (p + 1) * PAIR)
-        key_pair, value_pair = keys[:, columns], values[:, columns]
-        key_two = jnp.concatenate(
-            [jnp.where(even, key_pair, zero), jnp.where(even, zero, key_pair)], axis=0
-        )
-        value_two = jnp.concatenate(
-            [jnp.where(even, value_pair, zero), jnp.where(even, zero, value_pair)], axis=0
-        )
+        key_two, value_two = both(keys[:, columns]), both(values[:, columns])
         query_pair = queries[:, columns]
-        scores = mm_cols(query_pair, key_two) * scale
-        tanh_val = jnp.tanh(scores / score_cap)
+        tanh_val = jnp.tanh(mm_cols(key_two, query_pair) * (1.0 / score_cap))
         exponent = jnp.exp(score_cap * tanh_val)
         parts = []
         for side in range(2):
-            part = exponent[:, side * KEYS : (side + 1) * KEYS]
-            parts.append(part / jnp.sum(part, axis=-1, keepdims=True))
-        weights = jnp.concatenate(parts, axis=1)
+            part = exponent[side * KEYS : (side + 1) * KEYS]
+            parts.append(part * (1.0 / jnp.sum(part, axis=0, keepdims=True)))
+        weights = jnp.concatenate(parts, axis=0)
         weights_bf = weights.astype(bf16)
-        attended.append(mm(weights_bf, value_two).astype(bf16))
-        saved.append((key_two, value_two, query_pair, tanh_val, weights, weights_bf))
-    attended = jnp.concatenate(attended, axis=1)
+        attended.append(mm(both_across(values[:, columns]), weights_bf).astype(bf16))
+        saved.append((value_two, query_pair, tanh_val, weights, weights_bf))
+    attended = jnp.concatenate(attended, axis=0)
     load_wo.wait()
-    cell_out = mm(attended, wo_ref[...]).astype(bf16)
+    cell_out = mm(attended.T, wo_ref[...]).astype(bf16)
     onehot = jnp.where(
         lax.broadcasted_iota(jnp.int32, (SLOTS, cell_out.shape[0]), 0) == slot_ref[...], 1.0, 0.0
     ).astype(bf16)
     sums_ref[...] = mm(onehot, cell_out)
-    out_grad = mm_rows(onehot, table_ref[...]).astype(bf16)
+
+    basins = own_ref.shape[0] - 1
+    row = lax.broadcasted_iota(jnp.int32, (SLOTS, 128), 0)
+    lane = lax.broadcasted_iota(jnp.int32, (SLOTS, 128), 1)
+    counts = jnp.zeros((SLOTS, 128), f32)
+    for offset, source in (
+        (2 * basins, below_two_ref[0:1, :]),
+        (basins, below_ref[basins : basins + 1, :128]),
+        (0, own_ref[basins : basins + 1, :128]),
+        (-basins, above_ref[basins : basins + 1, :128]),
+        (-2 * basins, above_two_ref[0:1, :]),
+    ):
+        counts = counts + jnp.where(lane == row + offset, source.astype(f32), 0.0)
+    counts = jnp.sum(counts, axis=1, keepdims=True)
+    used = lax.broadcasted_iota(jnp.int32, (SLOTS, 1), 0) < 3 * basins
+    table_ref[...] = jnp.zeros_like(table_ref)
+    for place, source in enumerate((below_ref, own_ref, above_ref)):
+        table_ref[place * basins : (place + 1) * basins, :] = source[0:basins, :].astype(f32)
+    table = (table_ref[...] / jnp.sqrt(jnp.where(used, counts, 1.0))).astype(bf16)
+    out_grad = mm_rows(onehot, table).astype(bf16)
     attended_grad = mm_cols(out_grad, wo_ref[...]).astype(bf16)
-    store_weight(3, mm_rows(attended, out_grad))
+    store_weight(3, mm(attended, out_grad))
 
     query_grad, key_grad, value_grad = [], [], []
     for p in range(pairs):
-        key_two, value_two, query_pair, tanh_val, weights, weights_bf = saved[p]
-        grad_pair = attended_grad[:, p * PAIR : (p + 1) * PAIR]
-        weight_grad = mm_cols(grad_pair, value_two)
-        two = mm_rows(weights_bf, grad_pair)
+        value_two, query_pair, tanh_val, weights, weights_bf = saved[p]
+        columns = slice(p * PAIR, (p + 1) * PAIR)
+        grad_pair = attended_grad[:, columns]
+        weight_grad = mm_cols(value_two, grad_pair)
+        two = mm(weights_bf, grad_pair)
         value_grad.append(jnp.where(even, two[:KEYS], two[KEYS:]))
         product = weights * weight_grad
         parts = []
         for side in range(2):
-            columns = slice(side * KEYS, (side + 1) * KEYS)
-            parts.append(
-                weight_grad[:, columns] - jnp.sum(product[:, columns], axis=-1, keepdims=True)
-            )
-        centred = jnp.concatenate(parts, axis=1)
-        score_grad = (weights * centred * (1.0 - tanh_val * tanh_val) * scale).astype(bf16)
-        query_grad.append(mm(score_grad, key_two).astype(bf16))
-        two = mm_rows(score_grad, query_pair)
+            rows = slice(side * KEYS, (side + 1) * KEYS)
+            parts.append(weight_grad[rows] - jnp.sum(product[rows], axis=0, keepdims=True))
+        centred = jnp.concatenate(parts, axis=0)
+        score_grad = (weights * centred * (1.0 - tanh_val * tanh_val)).astype(bf16)
+        query_grad.append((mm(both_across(keys[:, columns]), score_grad) * scale).astype(bf16))
+        two = mm(score_grad, query_pair)
         key_grad.append(jnp.where(even, two[:KEYS], two[KEYS:]))
-    query_grad = jnp.concatenate(query_grad, axis=1)
+    query_grad = jnp.concatenate(query_grad, axis=0).T
     grad_cells_ref[...] = mm_cols(query_grad, wq_ref[...]).astype(bf16)
     store_weight(0, mm_rows(cells_ref[...], query_grad))
-    key_high, key_low = two_parts(jnp.concatenate(key_grad, axis=1))
-    value_high, value_low = two_parts(jnp.concatenate(value_grad, axis=1))
-    store_weight(1, mm_rows(encoded_sel, key_high) + mm_rows(encoded_sel, key_low))
-    store_weight(2, mm_rows(encoded_sel, value_high) + mm_rows(encoded_sel, value_low))
-    grad_gauges = (
-        mm_cols(key_high, wk_ref[...])
-        + mm_cols(key_low, wk_ref[...])
-        + mm_cols(value_high, wv_ref[...])
-        + mm_cols(value_low, wv_ref[...])
+    encoded_two = jnp.concatenate([encoded_sel, encoded_sel], axis=0).T
+    key_two = jnp.concatenate(two_parts(jnp.concatenate(key_grad, axis=1)), axis=0)
+    value_two = jnp.concatenate(two_parts(jnp.concatenate(value_grad, axis=1)), axis=0)
+    store_weight(1, mm(encoded_two, key_two))
+    store_weight(2, mm(encoded_two, value_two))
+    grad_gauges = mm_cols(key_two, wk_ref[...]) + mm_cols(value_two, wv_ref[...])
+    grad_gauges = (grad_gauges[:KEYS] + grad_gauges[KEYS:]).astype(bf16)
+    places = jnp.where(
+        lax.broadcasted_iota(jnp.int32, (gauges, KEYS), 0) == places_ref[...], 1.0, 0.0
     ).astype(bf16)
-    places = jnp.where(gauge_ids == places_ref[...], 1.0, 0.0).astype(bf16)
+    spread = mm(places, grad_gauges)
     for j in range(MEMBERS):
         store(
-            j * chunk + weight_chunk,
-            mm(places[j * gauge_chunk : (j + 1) * gauge_chunk, :], grad_gauges),
+            j * chunk + weight_chunk, spread[j * gauge_chunk : (j + 1) * gauge_chunk, :]
         )
 
 
@@ -233,9 +259,8 @@
     total = own * lax.axis_size(EVERY)
 
     rows_own = lax.dynamic_slice_in_dim(encoded, core * half, half, 1)
-    copies = copied(rows_own, MEMBERS * SIZES["far"])
-    mine = lax.all_to_all(copies, TILES, 0, 0, tiled=True)
-    other = swap(mine)
+    copies = copied(rows_own, SIZES["far"])
+    line = lax.all_to_all(copies, "far", 0, 0, tiled=True)
 
     slot = (cell_basin - device * own + own) % total
     counts = jnp.sum(
@@ -246,6 +271,9 @@
     small = packet[own:, :128]
     below, above = shifted(packet, 1), shifted(packet, -1)
     below_two, above_two = shifted(small, 2), shifted(small, -2)
+    line = after(line, below, above, below_two, above_two)
+    mine = lax.all_to_all(copied(line, MEMBERS), GROUP, 0, 0, tiled=True)
+    other = swap(mine)
     own_counts = counts
     down, up = below[own, : 3 * own].astype(f32), above[own, : 3 * own].astype(f32)
     down_two, up_two = below_two[0, : 3 * own].astype(f32), above_two[0, : 3 * own].astype(f32)
@@ -258,9 +286,6 @@
         ]
     )
     roots = jnp.sqrt(all_counts)
-    table = jnp.concatenate([below[:own], pooled_grad, above[:own]], axis=0).astype(f32)
-    table = (table / roots[:, None]).astype(bf16)
-    table = jnp.pad(table, ((0, SLOTS - 3 * own), (0, 0)))
 
     block = pattern[0]
     along_x = block % SIZES["x"]
@@ -270,7 +295,6 @@
     place = (along_y * SIZES["x"] + along_x) * SIZES["near"] + near
     place = place * SIZES["far"] + far_z
     within = jnp.arange(GAUGE_ROWS, dtype=jnp.int32)[None, :]
-    rows = (block[:, None] * GAUGE_ROWS + within).reshape(1, KEYS)
     places = (place[:, None] * GAUGE_ROWS + within).reshape(1, KEYS)
 
     gauges = mine.shape[0]
@@ -286,17 +310,19 @@
             jax.ShapeDtypeStruct((payload, half), bf16),
             jax.ShapeDtypeStruct((payload, half), bf16),
         ),
-        in_specs=[smem] + [vmem] * 9 + [hbm] * 2,
+        in_specs=[smem] + [vmem] * 12 + [hbm] * 2,
         out_specs=(vmem,) * 4,
         scratch_shapes=[
             pltpu.VMEM(cells.shape, bf16),
             pltpu.VMEM(w_out.shape, bf16),
+            pltpu.VMEM((SLOTS, width), f32),
             pltpu.SemaphoreType.DMA((2,)),
         ],
         compiler_params=pltpu.CompilerParams(vmem_limit_bytes=48 << 20),
         name="group_kernel",
     )(
-        core.reshape(1), rows, places, slot[None, :], table, mine, other,
+        core.reshape(1), places, slot[None, :], packet, below, above, below_two, above_two,
+        mine, other,
         w_key, w_value, w_query,
         pltpu.with_memory_space_constraint(cells, pltpu.HBM),
         pltpu.with_memory_space_constraint(w_out, pltpu.HBM),

time: 118 us -> 124 us (1.051)
  blocking collectives: 25.9 us -> 38.7 us
  starting transfers between devices: 49 us -> 41.7 us
  other arithmetic: 2.47 us -> 3.76 us
    all_to_all x0 -> x1, blocking collectives: none -> 12.7 us  [per_device(): mine = lax.all_to_all(copied(line, MEMBERS), GROUP, 0, 0, tiled=True)]
    all_to_all x1, starting transfers between devices: 16.3 us -> 9.01 us  [per_device(): line = lax.all_to_all(copies, 'far', 0, 0, tiled=True)]
    ppermute x6, starting transfers between devices: 13.6 us -> 20 us  [shifted(): lax.ppermute(value, EVERY, [(i, (i + steps) % count) for i in range(count)])]
    ppermute x4, starting transfers between devices: 12.6 us -> 6.32 us  [swap(): return lax.ppermute(value, 'c', [(0, 1), (1, 0)])]
    all_to_all x1, waiting for transfers between devices: 1.84 us -> 0.01 us  [per_device(): line = lax.all_to_all(copies, 'far', 0, 0, tiled=True)]
    ppermute x6, waiting for transfers between devices: 11.4 us -> 13.2 us  [shifted(): lax.ppermute(value, EVERY, [(i, (i + steps) % count) for i in range(count)])]
  transfers between devices with their start and end apart: 15 -> 15, of which waited for: 10 -> 9; matrix products, arithmetic and copies ran while one was open for 2% -> 3% of each run, Pallas kernels for 1% -> 1%
where the time goes in v6:
time: 124 us
  starting transfers between devices  41.7 us (34%)
  blocking collectives  38.7 us (31%)
  waiting for transfers between devices  27.4 us (22%)
  Pallas kernels  8.55 us (7%)
  other arithmetic  3.76 us (3%)
  local copies, waits for them, and re-layouts  2.62 us (2%)
    all_to_all x1, blocking collectives, per_device(): lax.all_to_all(chip, GROUP, 0, 0, tiled=True).reshape(MEMBERS, chunk, half)  26 us
    ppermute x6, starting transfers between devices, shifted(): lax.ppermute(value, EVERY, [(i, (i + steps) % count) for i in range(count)])  20 us
    ppermute x6, waiting for transfers between devices, shifted(): lax.ppermute(value, EVERY, [(i, (i + steps) % count) for i in range(count)])  13.2 us
    all_to_all x1, blocking collectives, per_device(): mine = lax.all_to_all(copied(line, MEMBERS), GROUP, 0, 0, tiled=True)  12.7 us
    all_to_all x1, starting transfers between devices, per_device(): line = lax.all_to_all(copies, 'far', 0, 0, tiled=True)  9.01 us
    ppermute x3, waiting for transfers between devices, per_device(): lax.ppermute(column, 'far', [(i, (i + s) % count) for i in range(count)])  6.87 us
    ppermute x4, starting transfers between devices, swap(): return lax.ppermute(value, 'c', [(0, 1), (1, 0)])  6.32 us
    pallas_call x1, Pallas kernels, per_device(): pl.pallas_call(group_kernel, out_shape=(jax.ShapeDtypeStruct(cells.shape,...  5.79 us
  transfers between devices with their start and end apart: 15, of which 9 were waited for; matrix products, arithmetic and copies ran while one was open for 3% of the time, Pallas kernels for 1%

profile of v6, /device:TPU:1, one launch (start us, length us, event | category | flops | bytes accessed | tf_op | source)
XLA Modules:
  0.0 123.7 jit_solution(11006822005626608552)
XLA Ops:
  0.7 0.6 copy-done
  1.3 0.6 broadcast_in_dim.12
  1.9 9.0 %all-to-all-start = ((bf16[4,8,256]{2,1,0:T(8,128)(2,1)}), bf16[4,8,256]{2,1,0:T(8,128)(2,1)S(1)}, u32[]{:S(2)}, u32[]{:S(2)}) async-start(bf16[4,8,256]{2,1,0:T(8,128)(2,1)} %broadcast_in_dim.12), calls=%async_computation | async-start | bytes 32768 | tf_op jit(solution)/shard_map/all_to_all | solution.py:263
  11.0 0.7 and_select_fusion
  11.8 0.7 pad_maximum_fusion.own_ref
  12.5 1.0 collective-permute-start.1
  13.4 1.2 collective-permute-start
  14.6 12.8 %collective-permute-start.3 = (bf16[1,128]{1,0:T(2,128)(2,1)S(1)}, bf16[1,128]{1,0:T(2,128)(2,1)S(1)}, u32[]{:S(2)}, u32[]{:S(2)}) collective-permute-start(bf16[1,128]{1,0:T(2,128)(2,1)S(1)} %slice.99), channel_id=1, source_target_pairs={{0,254},{1,255},{2,0},{3,1},{4,2},{5,3},{6,4},{7,5},{8,6},{9,7},{1... | collective-permute-start | bytes 776 | tf_op jit(solution)/shard_map/ppermute | solution.py:241
  27.4 0.7 collective-permute-done.3.above_two_ref
  28.2 7.1 %collective-permute-done.2.below_two_ref = bf16[1,128]{1,0:T(2,128)(2,1)S(1)} collective-permute-done((bf16[1,128]{1,0:T(2,128)(2,1)S(1)}, bf16[1,128]{1,0:T(2,128)(2,1)S(1)}, u32[]{:S(2)}, u32[]{:S(2)}) %collective-permute-start.2) | collective-permute-done | bytes 288 | tf_op jit(solution)/shard_map/ppermute | solution.py:241
  35.3 12.7 %all_to_all.35 = bf16[32,32,256]{2,1,0:T(8,128)(2,1)S(1)} all-to-all(bf16[32,32,256]{2,1,0:T(8,128)(2,1)S(1)} %broadcast_in_dim.13), channel_id=1, replica_groups=mesh['y'=4,'far'=4,'near'=2,'x'=4,'c'=2] {'y','x','near'}, dimensions={0} | all-to-all | bytes 1048576 | tf_op jit(solution)/shard_map/all_to_all | solution.py:275
  48.2 1.7 %collective-permute-done.4.other_ref = bf16[1024,256]{1,0:T(8,128)(2,1)S(1)} collective-permute-done((bf16[1024,256]{1,0:T(8,128)(2,1)S(1)}, bf16[1024,256]{1,0:T(8,128)(2,1)S(1)}, u32[]{:S(2)}, u32[]{:S(2)}) %collective-permute-start.4) | collective-permute-done | bytes 524320 | tf_op jit(solution)/shard_map/ppermute | solution.py:236
  50.0 5.8 %group_kernel.1 = (bf16[256,512]{1,0:T(8,128)(2,1)}, f32[16,512]{1,0:T(8,128)S(1)}, bf16[3072,256]{1,0:T(8,128)(2,1)S(1)}, bf16[3072,256]{1,0:T(8,128)(2,1)S(1)}) custom-call(s32[1]{0:T(128)} %bitcast.core_ref.side_ref, s32[1,128]{1,0:T(1,128)S(1)} %add.170.places_ref, s32[1,256]{1,0:T(1,128)S(1)} %bitcast.49, bf16[3,512]{1,0:T(4,128)(2,1)S(1)} %pad_maximum_fusion.own_ref, ...), custom_call_target="tpu_custom_call" | custom-call | tf_op jit(solution)/shard_map/group_kernel/pallas_call | solution.py:305
  56.0 3.3 %collective-permute-done.5 = bf16[3072,256]{1,0:T(8,128)(2,1)S(1)} collective-permute-done((bf16[3072,256]{1,0:T(8,128)(2,1)S(1)}, bf16[3072,256]{1,0:T(8,128)(2,1)S(1)}, u32[]{:S(2)}, u32[]{:S(2)}) %collective-permute-start.5) | collective-permute-done | bytes 1572896 | tf_op jit(solution)/shard_map/ppermute | solution.py:236
  59.3 0.5 add_convert_fusion
  59.7 26.0 %all_to_all.36 = bf16[32,96,256]{2,1,0:T(8,128)(2,1)S(1)} all-to-all(bf16[32,96,256]{2,1,0:T(8,128)(2,1)S(1)} %bitcast.50), channel_id=1, replica_groups=mesh['y'=4,'far'=4,'near'=2,'x'=4,'c'=2] {'y','x','near'}, dimensions={0} | all-to-all | bytes 3145728 | tf_op jit(solution)/shard_map/all_to_all | solution.py:335
  86.1 2.4 %collective-permute-start.7 = (bf16[96,256]{1,0:T(8,128)(2,1)S(1)}, bf16[96,256]{1,0:T(8,128)(2,1)S(1)}, u32[]{:S(2)}, u32[]{:S(2)}) collective-permute-start(bf16[96,256]{1,0:T(8,128)(2,1)S(1)} %reduce_sum.22), channel_id=1, source_target_pairs={{0,16},{16,32},{32,48},{48,0},{1,17},{17,33},{33,49},{49,1},{2,18}... | collective-permute-start | bytes 147464 | tf_op jit(solution)/shard_map/ppermute | solution.py:339
  88.4 2.0 %collective-permute-done.8 = bf16[96,256]{1,0:T(8,128)(2,1)S(1)} collective-permute-done((bf16[96,256]{1,0:T(8,128)(2,1)S(1)}, bf16[96,256]{1,0:T(8,128)(2,1)S(1)}, u32[]{:S(2)}, u32[]{:S(2)}) %collective-permute-start.8) | collective-permute-done | bytes 49184 | tf_op jit(solution)/shard_map/ppermute | solution.py:339
  90.4 0.8 collective-permute-done.7
  91.2 4.1 %collective-permute-done.6 = bf16[96,256]{1,0:T(8,128)(2,1)S(1)} collective-permute-done((bf16[96,256]{1,0:T(8,128)(2,1)S(1)}, bf16[96,256]{1,0:T(8,128)(2,1)S(1)}, u32[]{:S(2)}, u32[]{:S(2)}) %collective-permute-start.6) | collective-permute-done | bytes 49184 | tf_op jit(solution)/shard_map/ppermute | solution.py:339
  95.4 1.1 broadcast_in_dim.14
  96.5 3.9 %all-to-all-start.3 = ((bf16[32,64,256]{2,1,0:T(8,128)(2,1)}), bf16[32,64,256]{2,1,0:T(8,128)(2,1)S(1)}, u32[]{:S(2)}, u32[]{:S(2)}) async-start(bf16[32,64,256]{2,1,0:T(8,128)(2,1)} %broadcast_in_dim.14), calls=%async_computation.3 | async-start | bytes 2097152 | tf_op jit(solution)/shard_map/all_to_all | solution.py:350
  100.4 3.5 %collective-permute-start.9 = (f32[2,512]{1,0:T(2,128)S(1)}, f32[2,512]{1,0:T(2,128)S(1)}, u32[]{:S(2)}, u32[]{:S(2)}) collective-permute-start(f32[2,512]{1,0:T(2,128)S(1)} %get-tuple-element.39), channel_id=1, source_target_pairs={{0,255},{1,0},{2,1},{3,2},{4,3},{5,4},{6,5},{7,6},{8,7},{9,8},{10,... | collective-permute-start | bytes 12296 | tf_op jit(solution)/shard_map/ppermute | solution.py:241
  104.0 1.5 %collective-permute-start.10 = (f32[2,512]{1,0:T(2,128)S(1)}, f32[2,512]{1,0:T(2,128)S(1)}, u32[]{:S(2)}, u32[]{:S(2)}) collective-permute-start(f32[2,512]{1,0:T(2,128)S(1)} %get-tuple-element.40), channel_id=1, source_target_pairs={{0,1},{1,2},{2,3},{3,4},{4,5},{5,6},{6,7},{7,8},{8,9},{9,10},{10,1... | collective-permute-start | bytes 12296 | tf_op jit(solution)/shard_map/ppermute | solution.py:241
  105.4 1.9 %collective-permute-start.11 = (bf16[8,256]{1,0:T(8,128)(2,1)S(1)}, bf16[8,256]{1,0:T(8,128)(2,1)S(1)}, u32[]{:S(2)}, u32[]{:S(2)}) collective-permute-start(bf16[8,256]{1,0:T(8,128)(2,1)S(1)} %constant_dynamic-slice_fusion), channel_id=1, source_target_pairs={{0,1},{1,0},{2,3},{3,2},{4,5},{5,4},{6,7},{7,6},{8,9},{9,8},{10,11... | collective-permute-start | bytes 12296 | tf_op jit(solution)/shard_map/ppermute | solution.py:236
  107.3 5.4 %collective-permute-done.9 = f32[2,512]{1,0:T(2,128)S(1)} collective-permute-done((f32[2,512]{1,0:T(2,128)S(1)}, f32[2,512]{1,0:T(2,128)S(1)}, u32[]{:S(2)}, u32[]{:S(2)}) %collective-permute-start.9) | collective-permute-done | bytes 4128 | tf_op jit(solution)/shard_map/ppermute | solution.py:241
  112.8 2.3 %all-to-all-done.3 = bf16[32,64,256]{2,1,0:T(8,128)(2,1)S(1)} async-done(((bf16[32,64,256]{2,1,0:T(8,128)(2,1)}), bf16[32,64,256]{2,1,0:T(8,128)(2,1)S(1)}, u32[]{:S(2)}, u32[]{:S(2)}) %all-to-all-start.3) | async-done | bytes 1048608 | tf_op jit(solution)/shard_map/all_to_all | solution.py:350
  115.1 4.2 %collective-permute-start.12 = (bf16[2048,256]{1,0:T(8,128)(2,1)S(1)}, bf16[2048,256]{1,0:T(8,128)(2,1)S(1)}, u32[]{:S(2)}, u32[]{:S(2)}) collective-permute-start(bf16[2048,256]{1,0:T(8,128)(2,1)S(1)} %bitcast.44), channel_id=1, source_target_pairs={{0,1},{1,0},{2,3},{3,2},{4,5},{5,4},{6,7},{7,6},{8,9},{9,8},{10,11... | collective-permute-start | bytes 3145736 | tf_op jit(solution)/shard_map/ppermute | solution.py:236
  119.5 0.6 maximum_select_fusion
  120.1 0.7 fusion
  120.8 1.4 %widen_kernel.2 = (f32[512,512]{1,0:T(8,128)}, f32[512,512]{1,0:T(8,128)}, f32[512,512]{1,0:T(8,128)}, f32[512,512]{1,0:T(8,128)}) custom-call(s32[1]{0:T(128)} %bitcast.core_ref.side_ref, bf16[4,512,256]{2,1,0:T(8,128)(2,1)S(1)} %bitcast.45), custom_call_target="tpu_custom_call" | custom-call | tf_op jit(solution)/shard_map/widen_kernel/pallas_call | solution.py:216
  122.2 1.4 %widen_kernel.3 = (f32[512,512]{1,0:T(8,128)}, f32[512,512]{1,0:T(8,128)}, f32[512,512]{1,0:T(8,128)}, f32[512,512]{1,0:T(8,128)}) custom-call(s32[1]{0:T(128)} %bitcast.11.side_ref, bf16[4,512,256]{2,1,0:T(8,128)(2,1)S(1)} %bitcast.48, ...), custom_call_target="tpu_custom_call", output_to_operand_aliasing={{0}: (2, {}), {1}: (3, {}), {2}: (4, {}), {3}: (5, {})} | custom-call | tf_op jit(solution)/shard_map/widen_kernel/pallas_call | solution.py:216
  (40 shorter events, 1.2 us)
Async XLA Ops:
  0.6 0.7 copy-start
  0.6 47.4 %copy-start.4 = (s32[1,16]{1,0:T(1,128)S(1)}, s32[1,16]{1,0:T(1,128)}, u32[]{:S(2)}) copy-start(s32[1,16]{1,0:T(1,128)} %param.15) | copy-start | bytes 196
  0.7 49.3 %copy-start.2 = (bf16[512,512]{1,0:T(8,128)(2,1)S(1)}, bf16[512,512]{1,0:T(8,128)(2,1)}, u32[]{:S(2)}) copy-start(bf16[512,512]{1,0:T(8,128)(2,1)} %wv_ref.1) | copy-start | bytes 1572868
  0.7 49.3 %copy-start.1 = (bf16[512,512]{1,0:T(8,128)(2,1)S(1)}, bf16[512,512]{1,0:T(8,128)(2,1)}, u32[]{:S(2)}) copy-start(bf16[512,512]{1,0:T(8,128)(2,1)} %wk_ref.1) | copy-start | bytes 1572868
  0.7 49.3 %copy-start.3 = (bf16[512,512]{1,0:T(8,128)(2,1)S(1)}, bf16[512,512]{1,0:T(8,128)(2,1)}, u32[]{:S(2)}) copy-start(bf16[512,512]{1,0:T(8,128)(2,1)} %wq_ref.1) | copy-start | bytes 1572868
  1.9 33.3 %all-to-all-start = ((bf16[4,8,256]{2,1,0:T(8,128)(2,1)}), bf16[4,8,256]{2,1,0:T(8,128)(2,1)S(1)}, u32[]{:S(2)}, u32[]{:S(2)}) async-start(bf16[4,8,256]{2,1,0:T(8,128)(2,1)} %broadcast_in_dim.12), calls=%async_computation | async-start | bytes 32768 | tf_op jit(solution)/shard_map/all_to_all | solution.py:263
  12.5 22.8 %collective-permute-start.1 = (bf16[3,512]{1,0:T(4,128)(2,1)S(1)}, bf16[3,512]{1,0:T(4,128)(2,1)S(1)}, u32[]{:S(2)}, u32[]{:S(2)}) collective-permute-start(bf16[3,512]{1,0:T(4,128)(2,1)S(1)} %pad_maximum_fusion.own_ref), channel_id=1, source_target_pairs={{0,255},{1,0},{2,1},{3,2},{4,3},{5,4},{6,5},{7,6},{8,7},{9,8},{10,... | collective-permute-start | bytes 9224 | tf_op jit(solution)/shard_map/ppermute | solution.py:241
  13.4 21.8 %collective-permute-start = (bf16[3,512]{1,0:T(4,128)(2,1)S(1)}, bf16[3,512]{1,0:T(4,128)(2,1)S(1)}, u32[]{:S(2)}, u32[]{:S(2)}) collective-permute-start(bf16[3,512]{1,0:T(4,128)(2,1)S(1)} %pad_maximum_fusion.own_ref), channel_id=1, source_target_pairs={{0,1},{1,2},{2,3},{3,4},{4,5},{5,6},{6,7},{7,8},{8,9},{9,10},{10,1... | collective-permute-start | bytes 9224 | tf_op jit(solution)/shard_map/ppermute | solution.py:241
  14.6 13.5 %collective-permute-start.3 = (bf16[1,128]{1,0:T(2,128)(2,1)S(1)}, bf16[1,128]{1,0:T(2,128)(2,1)S(1)}, u32[]{:S(2)}, u32[]{:S(2)}) collective-permute-start(bf16[1,128]{1,0:T(2,128)(2,1)S(1)} %slice.99), channel_id=1, source_target_pairs={{0,254},{1,255},{2,0},{3,1},{4,2},{5,3},{6,4},{7,5},{8,6},{9,7},{1... | collective-permute-start | bytes 776 | tf_op jit(solution)/shard_map/ppermute | solution.py:241
  27.4 7.8 %collective-permute-start.2 = (bf16[1,128]{1,0:T(2,128)(2,1)S(1)}, bf16[1,128]{1,0:T(2,128)(2,1)S(1)}, u32[]{:S(2)}, u32[]{:S(2)}) collective-permute-start(bf16[1,128]{1,0:T(2,128)(2,1)S(1)} %slice.99), channel_id=1, source_target_pairs={{0,2},{1,3},{2,4},{3,5},{4,6},{5,7},{6,8},{7,9},{8,10},{9,11},{10,... | collective-permute-start | bytes 776 | tf_op jit(solution)/shard_map/ppermute | solution.py:241
  48.1 1.9 %collective-permute-start.4 = (bf16[1024,256]{1,0:T(8,128)(2,1)S(1)}, bf16[1024,256]{1,0:T(8,128)(2,1)S(1)}, u32[]{:S(2)}, u32[]{:S(2)}) collective-permute-start(bf16[1024,256]{1,0:T(8,128)(2,1)S(1)} %bitcast.46), channel_id=1, source_target_pairs={{0,1},{1,0},{2,3},{3,2},{4,5},{5,4},{6,7},{7,6},{8,9},{9,8},{10,11... | collective-permute-start | bytes 1572872 | tf_op jit(solution)/shard_map/ppermute | solution.py:236
  55.8 3.5 %collective-permute-start.5 = (bf16[3072,256]{1,0:T(8,128)(2,1)S(1)}, bf16[3072,256]{1,0:T(8,128)(2,1)S(1)}, u32[]{:S(2)}, u32[]{:S(2)}) collective-permute-start(bf16[3072,256]{1,0:T(8,128)(2,1)S(1)} %get-tuple-element.26), channel_id=1, source_target_pairs={{0,1},{1,0},{2,3},{3,2},{4,5},{5,4},{6,7},{7,6},{8,9},{9,8},{10,11... | collective-permute-start | bytes 4718600 | tf_op jit(solution)/shard_map/ppermute | solution.py:236
  86.0 4.4 %collective-permute-start.8 = (bf16[96,256]{1,0:T(8,128)(2,1)S(1)}, bf16[96,256]{1,0:T(8,128)(2,1)S(1)}, u32[]{:S(2)}, u32[]{:S(2)}) collective-permute-start(bf16[96,256]{1,0:T(8,128)(2,1)S(1)} %reduce_sum.22), channel_id=1, source_target_pairs={{0,48},{16,0},{32,16},{48,32},{1,49},{17,1},{33,17},{49,33},{2,50}... | collective-permute-start | bytes 147464 | tf_op jit(solution)/shard_map/ppermute | solution.py:339
  86.1 5.1 %collective-permute-start.7 = (bf16[96,256]{1,0:T(8,128)(2,1)S(1)}, bf16[96,256]{1,0:T(8,128)(2,1)S(1)}, u32[]{:S(2)}, u32[]{:S(2)}) collective-permute-start(bf16[96,256]{1,0:T(8,128)(2,1)S(1)} %reduce_sum.22), channel_id=1, source_target_pairs={{0,16},{16,32},{32,48},{48,0},{1,17},{17,33},{33,49},{49,1},{2,18}... | collective-permute-start | bytes 147464 | tf_op jit(solution)/shard_map/ppermute | solution.py:339
  88.4 6.9 %collective-permute-start.6 = (bf16[96,256]{1,0:T(8,128)(2,1)S(1)}, bf16[96,256]{1,0:T(8,128)(2,1)S(1)}, u32[]{:S(2)}, u32[]{:S(2)}) collective-permute-start(bf16[96,256]{1,0:T(8,128)(2,1)S(1)} %reduce_sum.22), channel_id=1, source_target_pairs={{0,32},{16,48},{32,0},{48,16},{1,33},{17,49},{33,1},{49,17},{2,34}... | collective-permute-start | bytes 147464 | tf_op jit(solution)/shard_map/ppermute | solution.py:339
  96.5 18.6 %all-to-all-start.3 = ((bf16[32,64,256]{2,1,0:T(8,128)(2,1)}), bf16[32,64,256]{2,1,0:T(8,128)(2,1)S(1)}, u32[]{:S(2)}, u32[]{:S(2)}) async-start(bf16[32,64,256]{2,1,0:T(8,128)(2,1)} %broadcast_in_dim.14), calls=%async_computation.3 | async-start | bytes 2097152 | tf_op jit(solution)/shard_map/all_to_all | solution.py:350
  100.4 12.3 %collective-permute-start.9 = (f32[2,512]{1,0:T(2,128)S(1)}, f32[2,512]{1,0:T(2,128)S(1)}, u32[]{:S(2)}, u32[]{:S(2)}) collective-permute-start(f32[2,512]{1,0:T(2,128)S(1)} %get-tuple-element.39), channel_id=1, source_target_pairs={{0,255},{1,0},{2,1},{3,2},{4,3},{5,4},{6,5},{7,6},{8,7},{9,8},{10,... | collective-permute-start | bytes 12296 | tf_op jit(solution)/shard_map/ppermute | solution.py:241
  104.0 8.8 %collective-permute-start.10 = (f32[2,512]{1,0:T(2,128)S(1)}, f32[2,512]{1,0:T(2,128)S(1)}, u32[]{:S(2)}, u32[]{:S(2)}) collective-permute-start(f32[2,512]{1,0:T(2,128)S(1)} %get-tuple-element.40), channel_id=1, source_target_pairs={{0,1},{1,2},{2,3},{3,4},{4,5},{5,6},{6,7},{7,8},{8,9},{9,10},{10,1... | collective-permute-start | bytes 12296 | tf_op jit(solution)/shard_map/ppermute | solution.py:241
  105.4 7.3 %collective-permute-start.11 = (bf16[8,256]{1,0:T(8,128)(2,1)S(1)}, bf16[8,256]{1,0:T(8,128)(2,1)S(1)}, u32[]{:S(2)}, u32[]{:S(2)}) collective-permute-start(bf16[8,256]{1,0:T(8,128)(2,1)S(1)} %constant_dynamic-slice_fusion), channel_id=1, source_target_pairs={{0,1},{1,0},{2,3},{3,2},{4,5},{5,4},{6,7},{7,6},{8,9},{9,8},{10,11... | collective-permute-start | bytes 12296 | tf_op jit(solution)/shard_map/ppermute | solution.py:236
  115.1 7.1 %collective-permute-start.12 = (bf16[2048,256]{1,0:T(8,128)(2,1)S(1)}, bf16[2048,256]{1,0:T(8,128)(2,1)S(1)}, u32[]{:S(2)}, u32[]{:S(2)}) collective-permute-start(bf16[2048,256]{1,0:T(8,128)(2,1)S(1)} %bitcast.44), channel_id=1, source_target_pairs={{0,1},{1,0},{2,3},{3,2},{4,5},{5,4},{6,7},{7,6},{8,9},{9,8},{10,11... | collective-permute-start | bytes 3145736 | tf_op jit(solution)/shard_map/ppermute | solution.py:236

commit v7 on v6

--- a/solution.py
+++ b/solution.py
@@ -45,9 +45,9 @@
 
 
 def group_kernel(
-    core_ref, places_ref, slot_ref, own_ref, below_ref, above_ref, below_two_ref, above_two_ref,
+    core_ref, rows_ref, places_ref, slot_ref, own_ref, below_ref, above_ref, below_two_ref, above_two_ref,
     mine_ref, other_ref, wk_ref, wv_ref, wq_ref, cells_hbm, wo_hbm,
-    grad_cells_ref, sums_ref, keep_ref, send_ref,
+    grad_cells_ref, sums_ref, roots_ref, keep_ref, send_ref,
     cells_ref, wo_ref, table_ref, sems,
 ):
     load_cells = pltpu.make_async_copy(cells_hbm, cells_ref, sems.at[0])
@@ -77,7 +77,7 @@
                 value[j * weight_chunk : (j + 1) * weight_chunk, :],
             )
 
-    down = jnp.broadcast_to(places_ref[...], (KEYS, KEYS)).T
+    down = jnp.broadcast_to(rows_ref[...], (KEYS, KEYS)).T
     lanes = lax.broadcasted_iota(jnp.int32, (KEYS, KEYS), 1)
     picks = jnp.concatenate(
         [
@@ -150,7 +150,9 @@
     table_ref[...] = jnp.zeros_like(table_ref)
     for place, source in enumerate((below_ref, own_ref, above_ref)):
         table_ref[place * basins : (place + 1) * basins, :] = source[0:basins, :].astype(f32)
-    table = (table_ref[...] / jnp.sqrt(jnp.where(used, counts, 1.0))).astype(bf16)
+    roots = jnp.sqrt(jnp.where(used, counts, 1.0))
+    roots_ref[...] = jnp.broadcast_to(roots, roots_ref.shape)
+    table = (table_ref[...] / roots).astype(bf16)
     out_grad = mm_rows(onehot, table).astype(bf16)
     attended_grad = mm_cols(out_grad, wo_ref[...]).astype(bf16)
     store_weight(3, mm(attended, out_grad))
@@ -259,8 +261,8 @@
     total = own * lax.axis_size(EVERY)
 
     rows_own = lax.dynamic_slice_in_dim(encoded, core * half, half, 1)
-    copies = copied(rows_own, SIZES["far"])
-    line = lax.all_to_all(copies, "far", 0, 0, tiled=True)
+    copies = copied(rows_own, MEMBERS * SIZES["far"])
+    mine = lax.all_to_all(copies, TILES, 0, 0, tiled=True)
 
     slot = (cell_basin - device * own + own) % total
     counts = jnp.sum(
@@ -271,21 +273,9 @@
     small = packet[own:, :128]
     below, above = shifted(packet, 1), shifted(packet, -1)
     below_two, above_two = shifted(small, 2), shifted(small, -2)
-    line = after(line, below, above, below_two, above_two)
-    mine = lax.all_to_all(copied(line, MEMBERS), GROUP, 0, 0, tiled=True)
+    mine = after(mine, below, above, below_two, above_two)
     other = swap(mine)
-    own_counts = counts
-    down, up = below[own, : 3 * own].astype(f32), above[own, : 3 * own].astype(f32)
-    down_two, up_two = below_two[0, : 3 * own].astype(f32), above_two[0, : 3 * own].astype(f32)
     low, mid, top = slice(0, own), slice(own, 2 * own), slice(2 * own, 3 * own)
-    all_counts = jnp.concatenate(
-        [
-            down_two[top] + down[mid] + own_counts[low],
-            down[top] + own_counts[mid] + up[low],
-            own_counts[top] + up[mid] + up_two[low],
-        ]
-    )
-    roots = jnp.sqrt(all_counts)
 
     block = pattern[0]
     along_x = block % SIZES["x"]
@@ -295,6 +285,7 @@
     place = (along_y * SIZES["x"] + along_x) * SIZES["near"] + near
     place = place * SIZES["far"] + far_z
     within = jnp.arange(GAUGE_ROWS, dtype=jnp.int32)[None, :]
+    rows = (block[:, None] * GAUGE_ROWS + within).reshape(1, KEYS)
     places = (place[:, None] * GAUGE_ROWS + within).reshape(1, KEYS)
 
     gauges = mine.shape[0]
@@ -302,26 +293,27 @@
     vmem = pl.BlockSpec(memory_space=pltpu.VMEM)
     smem = pl.BlockSpec(memory_space=pltpu.SMEM)
     hbm = pl.BlockSpec(memory_space=pltpu.HBM)
-    grad_cells, sums, keep, send = pl.pallas_call(
+    grad_cells, sums, roots, keep, send = pl.pallas_call(
         group_kernel,
         out_shape=(
             jax.ShapeDtypeStruct(cells.shape, bf16),
             jax.ShapeDtypeStruct((SLOTS, width), f32),
+            jax.ShapeDtypeStruct((SLOTS, 128), f32),
             jax.ShapeDtypeStruct((payload, half), bf16),
             jax.ShapeDtypeStruct((payload, half), bf16),
         ),
-        in_specs=[smem] + [vmem] * 12 + [hbm] * 2,
-        out_specs=(vmem,) * 4,
+        in_specs=[smem] + [vmem] * 13 + [hbm] * 2,
+        out_specs=(vmem,) * 5,
         scratch_shapes=[
             pltpu.VMEM(cells.shape, bf16),
             pltpu.VMEM(w_out.shape, bf16),
             pltpu.VMEM((SLOTS, width), f32),
             pltpu.SemaphoreType.DMA((2,)),
         ],
-        compiler_params=pltpu.CompilerParams(vmem_limit_bytes=48 << 20),
+        compiler_params=pltpu.CompilerParams(vmem_limit_bytes=24 << 20),
         name="group_kernel",
     )(
-        core.reshape(1), places, slot[None, :], packet, below, above, below_two, above_two,
+        core.reshape(1), rows, places, slot[None, :], packet, below, above, below_two, above_two,
         mine, other,
         w_key, w_value, w_query,
         pltpu.with_memory_space_constraint(cells, pltpu.HBM),
@@ -351,13 +343,13 @@
     late_sums, late_gauge = lax.optimization_barrier((sums, own_gauge, copies))[:2]
     far_gauge = swap(late_gauge)
     from_above, from_below = shifted(late_sums[low], -1), shifted(late_sums[top], 1)
-    weights = after(weights, far_gauge, from_above, from_below)
-    pooled = ((sums[mid] + from_above + from_below) / roots[mid][:, None]).astype(bf16)
+    pooled = ((sums[mid] + from_above + from_below) / roots[mid, :1]).astype(bf16)
     grad_gauges = jnp.where(
         core == 0,
         jnp.concatenate([own_gauge, far_gauge], axis=1),
         jnp.concatenate([far_gauge, own_gauge], axis=1),
     )
+    weights = after(weights, pooled, grad_gauges)
     far = swap(weights)
     grads = widen(core, weights, None)
     grads = widen(1 - core, far, grads)

time: 124 us -> 116 us (0.935)
  blocking collectives: 38.7 us -> 26.2 us
  starting transfers between devices: 41.7 us -> 46.2 us
  other arithmetic: 3.76 us -> 2.22 us
  waiting for transfers between devices: 27.4 us -> 28.9 us
    all_to_all x1 -> x0, blocking collectives: 12.7 us -> none  [per_device(): mine = lax.all_to_all(copied(line, MEMBERS), GROUP, 0, 0, tiled=True)]
    all_to_all x1, starting transfers between devices: 9.01 us -> 16.3 us  [per_device(): mine = lax.all_to_all(copies, TILES, 0, 0, tiled=True)]
    ppermute x6, starting transfers between devices: 20 us -> 15.8 us  [shifted(): lax.ppermute(value, EVERY, [(i, (i + steps) % count) for i in range(count)])]
  transfers between devices with their start and end apart: 15 -> 15, of which waited for: 9 -> 10; matrix products, arithmetic and copies ran while one was open for 3% -> 2% of each run, Pallas kernels for 1% -> 1%
where the time goes in v7:
time: 116 us
  starting transfers between devices  46.2 us (40%)
  waiting for transfers between devices  28.9 us (25%)
  blocking collectives  26.2 us (23%)
  Pallas kernels  8.55 us (7%)
  local copies, waits for them, and re-layouts  2.9 us (2%)
  other arithmetic  2.22 us (2%)
    all_to_all x1, blocking collectives, per_device(): lax.all_to_all(chip, GROUP, 0, 0, tiled=True).reshape(MEMBERS, chunk, half)  26.2 us
    all_to_all x1, starting transfers between devices, per_device(): mine = lax.all_to_all(copies, TILES, 0, 0, tiled=True)  16.3 us
    ppermute x6, starting transfers between devices, shifted(): lax.ppermute(value, EVERY, [(i, (i + steps) % count) for i in range(count)])  15.8 us
    ppermute x6, waiting for transfers between devices, shifted(): lax.ppermute(value, EVERY, [(i, (i + steps) % count) for i in range(count)])  14.4 us
    ppermute x4, starting transfers between devices, swap(): return lax.ppermute(value, 'c', [(0, 1), (1, 0)])  7.55 us
    ppermute x3, waiting for transfers between devices, per_device(): lax.ppermute(column, 'far', [(i, (i + s) % count) for i in range(count)])  6.82 us
    ppermute x4, waiting for transfers between devices, swap(): return lax.ppermute(value, 'c', [(0, 1), (1, 0)])  5.8 us
    pallas_call x1, Pallas kernels, per_device(): pl.pallas_call(group_kernel, out_shape=(jax.ShapeDtypeStruct(cells.shape,...  5.79 us
  transfers between devices with their start and end apart: 15, of which 10 were waited for; matrix products, arithmetic and copies ran while one was open for 2% of the time, Pallas kernels for 1%

profile of v7, /device:TPU:1, one launch (start us, length us, event | category | flops | bytes accessed | tf_op | source)
XLA Modules:
  0.0 116.0 jit_solution(10684527883080613303)
XLA Ops:
  0.7 0.6 copy-done
  1.3 0.8 broadcast_in_dim.10
  2.2 16.3 %all-to-all-start = ((bf16[128,8,256]{2,1,0:T(8,128)(2,1)}), bf16[128,8,256]{2,1,0:T(8,128)(2,1)S(1)}, u32[]{:S(2)}, u32[]{:S(2)}) async-start(bf16[128,8,256]{2,1,0:T(8,128)(2,1)} %broadcast_in_dim.10), calls=%async_computation | async-start | bytes 1048576 | tf_op jit(solution)/shard_map/all_to_all | solution.py:265
  18.7 1.0 collective-permute-start.1
  19.8 0.8 collective-permute-start
  20.6 12.1 %collective-permute-start.3 = (bf16[1,128]{1,0:T(2,128)(2,1)S(1)}, bf16[1,128]{1,0:T(2,128)(2,1)S(1)}, u32[]{:S(2)}, u32[]{:S(2)}) collective-permute-start(bf16[1,128]{1,0:T(2,128)(2,1)S(1)} %slice.24), channel_id=1, source_target_pairs={{0,254},{1,255},{2,0},{3,1},{4,2},{5,3},{6,4},{7,5},{8,6},{9,7},{1... | collective-permute-start | bytes 776 | tf_op jit(solution)/shard_map/ppermute | solution.py:243
  32.7 0.7 collective-permute-done.3.above_two_ref
  33.5 7.1 %collective-permute-done.2.below_two_ref = bf16[1,128]{1,0:T(2,128)(2,1)S(1)} collective-permute-done((bf16[1,128]{1,0:T(2,128)(2,1)S(1)}, bf16[1,128]{1,0:T(2,128)(2,1)S(1)}, u32[]{:S(2)}, u32[]{:S(2)}) %collective-permute-start.2) | collective-permute-done | bytes 288 | tf_op jit(solution)/shard_map/ppermute | solution.py:243
  41.0 1.6 %collective-permute-done.4.other_ref = bf16[1024,256]{1,0:T(8,128)(2,1)S(1)} collective-permute-done((bf16[1024,256]{1,0:T(8,128)(2,1)S(1)}, bf16[1024,256]{1,0:T(8,128)(2,1)S(1)}, u32[]{:S(2)}, u32[]{:S(2)}) %collective-permute-start.4) | collective-permute-done | bytes 524320 | tf_op jit(solution)/shard_map/ppermute | solution.py:238
  42.6 5.8 %group_kernel.1 = (bf16[256,512]{1,0:T(8,128)(2,1)}, f32[16,512]{1,0:T(8,128)S(1)}, f32[16,128]{1,0:T(8,128)S(1)}, bf16[3072,256]{1,0:T(8,128)(2,1)S(1)}, bf16[3072,256]{1,0:T(8,128)(2,1)S(1)}) custom-call(s32[1]{0:T(128)} %bitcast.core_ref.side_ref, s32[1,128]{1,0:T(1,128)S(1)} %add.166.rows_ref, s32[1,128]{1,0:T(1,128)S(1)} %add.176.places_ref, ...), custom_call_target="tpu_custom_call" | custom-call | tf_op jit(solution)/shard_map/group_kernel/pallas_call | solution.py:296
  48.4 0.2 collective-permute-start.5
  48.6 3.3 %collective-permute-done.5 = bf16[3072,256]{1,0:T(8,128)(2,1)S(1)} collective-permute-done((bf16[3072,256]{1,0:T(8,128)(2,1)S(1)}, bf16[3072,256]{1,0:T(8,128)(2,1)S(1)}, u32[]{:S(2)}, u32[]{:S(2)}) %collective-permute-start.5) | collective-permute-done | bytes 1572896 | tf_op jit(solution)/shard_map/ppermute | solution.py:238
  51.9 0.5 add_convert_fusion
  52.3 26.2 %all_to_all.27 = bf16[32,96,256]{2,1,0:T(8,128)(2,1)S(1)} all-to-all(bf16[32,96,256]{2,1,0:T(8,128)(2,1)S(1)} %bitcast.35), channel_id=1, replica_groups=mesh['y'=4,'far'=4,'near'=2,'x'=4,'c'=2] {'y','x','near'}, dimensions={0} | all-to-all | bytes 3145728 | tf_op jit(solution)/shard_map/all_to_all | solution.py:327
  78.5 0.2 reduce_sum.22
  78.7 0.3 collective-permute-start.8
  79.0 2.4 %collective-permute-start.7 = (bf16[96,256]{1,0:T(8,128)(2,1)S(1)}, bf16[96,256]{1,0:T(8,128)(2,1)S(1)}, u32[]{:S(2)}, u32[]{:S(2)}) collective-permute-start(bf16[96,256]{1,0:T(8,128)(2,1)S(1)} %reduce_sum.22), channel_id=1, source_target_pairs={{0,16},{16,32},{32,48},{48,0},{1,17},{17,33},{33,49},{49,1},{2,18}... | collective-permute-start | bytes 147464 | tf_op jit(solution)/shard_map/ppermute | solution.py:331
  81.4 2.0 %collective-permute-done.8 = bf16[96,256]{1,0:T(8,128)(2,1)S(1)} collective-permute-done((bf16[96,256]{1,0:T(8,128)(2,1)S(1)}, bf16[96,256]{1,0:T(8,128)(2,1)S(1)}, u32[]{:S(2)}, u32[]{:S(2)}) %collective-permute-start.8) | collective-permute-done | bytes 49184 | tf_op jit(solution)/shard_map/ppermute | solution.py:331
  83.4 1.2 %collective-permute-done.7 = bf16[96,256]{1,0:T(8,128)(2,1)S(1)} collective-permute-done((bf16[96,256]{1,0:T(8,128)(2,1)S(1)}, bf16[96,256]{1,0:T(8,128)(2,1)S(1)}, u32[]{:S(2)}, u32[]{:S(2)}) %collective-permute-start.7) | collective-permute-done | bytes 49184 | tf_op jit(solution)/shard_map/ppermute | solution.py:331
  84.5 3.7 %collective-permute-done.6 = bf16[96,256]{1,0:T(8,128)(2,1)S(1)} collective-permute-done((bf16[96,256]{1,0:T(8,128)(2,1)S(1)}, bf16[96,256]{1,0:T(8,128)(2,1)S(1)}, u32[]{:S(2)}, u32[]{:S(2)}) %collective-permute-start.6) | collective-permute-done | bytes 49184 | tf_op jit(solution)/shard_map/ppermute | solution.py:331
  88.2 1.1 broadcast_in_dim.11
  89.3 3.9 %all-to-all-start.2 = ((bf16[32,64,256]{2,1,0:T(8,128)(2,1)}), bf16[32,64,256]{2,1,0:T(8,128)(2,1)S(1)}, u32[]{:S(2)}, u32[]{:S(2)}) async-start(bf16[32,64,256]{2,1,0:T(8,128)(2,1)} %broadcast_in_dim.11), calls=%async_computation.2 | async-start | bytes 2097152 | tf_op jit(solution)/shard_map/all_to_all | solution.py:342
  93.4 3.2 %collective-permute-start.11 = (bf16[8,256]{1,0:T(8,128)(2,1)S(1)}, bf16[8,256]{1,0:T(8,128)(2,1)S(1)}, u32[]{:S(2)}, u32[]{:S(2)}) collective-permute-start(bf16[8,256]{1,0:T(8,128)(2,1)S(1)} %constant_dynamic-slice_fusion), channel_id=1, source_target_pairs={{0,1},{1,0},{2,3},{3,2},{4,5},{5,4},{6,7},{7,6},{8,9},{9,8},{10,11... | collective-permute-start | bytes 12296 | tf_op jit(solution)/shard_map/ppermute | solution.py:238
  96.8 1.6 %collective-permute-start.10 = (f32[2,512]{1,0:T(2,128)S(1)}, f32[2,512]{1,0:T(2,128)S(1)}, u32[]{:S(2)}, u32[]{:S(2)}) collective-permute-start(f32[2,512]{1,0:T(2,128)S(1)} %get-tuple-element.42), channel_id=1, source_target_pairs={{0,1},{1,2},{2,3},{3,4},{4,5},{5,6},{6,7},{7,8},{8,9},{9,10},{10,1... | collective-permute-start | bytes 12296 | tf_op jit(solution)/shard_map/ppermute | solution.py:243
  98.4 0.6 maximum_select_fusion
  99.0 6.6 %collective-permute-done.9 = f32[2,512]{1,0:T(2,128)S(1)} collective-permute-done((f32[2,512]{1,0:T(2,128)S(1)}, f32[2,512]{1,0:T(2,128)S(1)}, u32[]{:S(2)}, u32[]{:S(2)}) %collective-permute-start.9) | collective-permute-done | bytes 4128 | tf_op jit(solution)/shard_map/ppermute | solution.py:243
  105.6 0.7 fusion
  106.3 1.9 %all-to-all-done.2 = bf16[32,64,256]{2,1,0:T(8,128)(2,1)S(1)} async-done(((bf16[32,64,256]{2,1,0:T(8,128)(2,1)}), bf16[32,64,256]{2,1,0:T(8,128)(2,1)S(1)}, u32[]{:S(2)}, u32[]{:S(2)}) %all-to-all-start.2) | async-done | bytes 1048608 | tf_op jit(solution)/shard_map/all_to_all | solution.py:342
  108.1 4.0 %collective-permute-start.12 = (bf16[2048,256]{1,0:T(8,128)(2,1)S(1)}, bf16[2048,256]{1,0:T(8,128)(2,1)S(1)}, u32[]{:S(2)}, u32[]{:S(2)}) collective-permute-start(bf16[2048,256]{1,0:T(8,128)(2,1)S(1)} %bitcast.29), channel_id=1, source_target_pairs={{0,1},{1,0},{2,3},{3,2},{4,5},{5,4},{6,7},{7,6},{8,9},{9,8},{10,11... | collective-permute-start | bytes 3145736 | tf_op jit(solution)/shard_map/ppermute | solution.py:238
  112.2 1.4 %widen_kernel.2 = (f32[512,512]{1,0:T(8,128)}, f32[512,512]{1,0:T(8,128)}, f32[512,512]{1,0:T(8,128)}, f32[512,512]{1,0:T(8,128)}) custom-call(s32[1]{0:T(128)} %bitcast.core_ref.side_ref, bf16[4,512,256]{2,1,0:T(8,128)(2,1)S(1)} %bitcast.30), custom_call_target="tpu_custom_call" | custom-call | tf_op jit(solution)/shard_map/widen_kernel/pallas_call | solution.py:218
  113.5 0.9 collective-permute-done.12
  114.4 1.4 %widen_kernel.3 = (f32[512,512]{1,0:T(8,128)}, f32[512,512]{1,0:T(8,128)}, f32[512,512]{1,0:T(8,128)}, f32[512,512]{1,0:T(8,128)}) custom-call(s32[1]{0:T(128)} %bitcast.5.side_ref, bf16[4,512,256]{2,1,0:T(8,128)(2,1)S(1)} %bitcast.33, ...), custom_call_target="tpu_custom_call", output_to_operand_aliasing={{0}: (2, {}), {1}: (3, {}), {2}: (4, {}), {3}: (5, {})} | custom-call | tf_op jit(solution)/shard_map/widen_kernel/pallas_call | solution.py:218
  (38 shorter events, 0.9 us)
Async XLA Ops:
  0.6 0.7 copy-start
  0.7 17.9 %copy-start.5 = (s32[256]{0:T(256)S(1)}, s32[256]{0:T(256)}, u32[]{:S(2)}) copy-start(s32[256]{0:T(256)} %param.16) | copy-start | bytes 3076
  0.7 18.0 %copy-start.4 = (bf16[2,512]{1,0:T(2,128)(2,1)S(1)}, bf16[2,512]{1,0:T(2,128)(2,1)}, u32[]{:S(2)}) copy-start(bf16[2,512]{1,0:T(2,128)(2,1)} %param.17) | copy-start | bytes 6148
  0.7 40.0 %copy-start.6 = (s32[1,16]{1,0:T(1,128)S(1)}, s32[1,16]{1,0:T(1,128)}, u32[]{:S(2)}) copy-start(s32[1,16]{1,0:T(1,128)} %param.15) | copy-start | bytes 196
  0.7 41.9 %copy-start.2 = (bf16[512,512]{1,0:T(8,128)(2,1)S(1)}, bf16[512,512]{1,0:T(8,128)(2,1)}, u32[]{:S(2)}) copy-start(bf16[512,512]{1,0:T(8,128)(2,1)} %wv_ref.1) | copy-start | bytes 1572868
  0.7 41.9 %copy-start.1 = (bf16[512,512]{1,0:T(8,128)(2,1)S(1)}, bf16[512,512]{1,0:T(8,128)(2,1)}, u32[]{:S(2)}) copy-start(bf16[512,512]{1,0:T(8,128)(2,1)} %wk_ref.1) | copy-start | bytes 1572868
  0.7 41.9 %copy-start.3 = (bf16[512,512]{1,0:T(8,128)(2,1)S(1)}, bf16[512,512]{1,0:T(8,128)(2,1)}, u32[]{:S(2)}) copy-start(bf16[512,512]{1,0:T(8,128)(2,1)} %wq_ref.1) | copy-start | bytes 1572868
  2.2 38.4 %all-to-all-start = ((bf16[128,8,256]{2,1,0:T(8,128)(2,1)}), bf16[128,8,256]{2,1,0:T(8,128)(2,1)S(1)}, u32[]{:S(2)}, u32[]{:S(2)}) async-start(bf16[128,8,256]{2,1,0:T(8,128)(2,1)} %broadcast_in_dim.10), calls=%async_computation | async-start | bytes 1048576 | tf_op jit(solution)/shard_map/all_to_all | solution.py:265
  18.7 21.8 %collective-permute-start.1 = (bf16[3,512]{1,0:T(4,128)(2,1)S(1)}, bf16[3,512]{1,0:T(4,128)(2,1)S(1)}, u32[]{:S(2)}, u32[]{:S(2)}) collective-permute-start(bf16[3,512]{1,0:T(4,128)(2,1)S(1)} %pad_maximum_fusion.own_ref), channel_id=1, source_target_pairs={{0,255},{1,0},{2,1},{3,2},{4,3},{5,4},{6,5},{7,6},{8,7},{9,8},{10,... | collective-permute-start | bytes 9224 | tf_op jit(solution)/shard_map/ppermute | solution.py:243
  19.8 20.8 %collective-permute-start = (bf16[3,512]{1,0:T(4,128)(2,1)S(1)}, bf16[3,512]{1,0:T(4,128)(2,1)S(1)}, u32[]{:S(2)}, u32[]{:S(2)}) collective-permute-start(bf16[3,512]{1,0:T(4,128)(2,1)S(1)} %pad_maximum_fusion.own_ref), channel_id=1, source_target_pairs={{0,1},{1,2},{2,3},{3,4},{4,5},{5,6},{6,7},{7,8},{8,9},{9,10},{10,1... | collective-permute-start | bytes 9224 | tf_op jit(solution)/shard_map/ppermute | solution.py:243
  20.6 12.9 %collective-permute-start.3 = (bf16[1,128]{1,0:T(2,128)(2,1)S(1)}, bf16[1,128]{1,0:T(2,128)(2,1)S(1)}, u32[]{:S(2)}, u32[]{:S(2)}) collective-permute-start(bf16[1,128]{1,0:T(2,128)(2,1)S(1)} %slice.24), channel_id=1, source_target_pairs={{0,254},{1,255},{2,0},{3,1},{4,2},{5,3},{6,4},{7,5},{8,6},{9,7},{1... | collective-permute-start | bytes 776 | tf_op jit(solution)/shard_map/ppermute | solution.py:243
  32.7 7.8 %collective-permute-start.2 = (bf16[1,128]{1,0:T(2,128)(2,1)S(1)}, bf16[1,128]{1,0:T(2,128)(2,1)S(1)}, u32[]{:S(2)}, u32[]{:S(2)}) collective-permute-start(bf16[1,128]{1,0:T(2,128)(2,1)S(1)} %slice.24), channel_id=1, source_target_pairs={{0,2},{1,3},{2,4},{3,5},{4,6},{5,7},{6,8},{7,9},{8,10},{9,11},{10,... | collective-permute-start | bytes 776 | tf_op jit(solution)/shard_map/ppermute | solution.py:243
  40.6 2.0 %collective-permute-start.4 = (bf16[1024,256]{1,0:T(8,128)(2,1)S(1)}, bf16[1024,256]{1,0:T(8,128)(2,1)S(1)}, u32[]{:S(2)}, u32[]{:S(2)}) collective-permute-start(bf16[1024,256]{1,0:T(8,128)(2,1)S(1)} %bitcast.31), channel_id=1, source_target_pairs={{0,1},{1,0},{2,3},{3,2},{4,5},{5,4},{6,7},{7,6},{8,9},{9,8},{10,11... | collective-permute-start | bytes 1572872 | tf_op jit(solution)/shard_map/ppermute | solution.py:238
  48.4 3.5 %collective-permute-start.5 = (bf16[3072,256]{1,0:T(8,128)(2,1)S(1)}, bf16[3072,256]{1,0:T(8,128)(2,1)S(1)}, u32[]{:S(2)}, u32[]{:S(2)}) collective-permute-start(bf16[3072,256]{1,0:T(8,128)(2,1)S(1)} %get-tuple-element.27), channel_id=1, source_target_pairs={{0,1},{1,0},{2,3},{3,2},{4,5},{5,4},{6,7},{7,6},{8,9},{9,8},{10,11... | collective-permute-start | bytes 4718600 | tf_op jit(solution)/shard_map/ppermute | solution.py:238
  78.7 4.6 %collective-permute-start.8 = (bf16[96,256]{1,0:T(8,128)(2,1)S(1)}, bf16[96,256]{1,0:T(8,128)(2,1)S(1)}, u32[]{:S(2)}, u32[]{:S(2)}) collective-permute-start(bf16[96,256]{1,0:T(8,128)(2,1)S(1)} %reduce_sum.22), channel_id=1, source_target_pairs={{0,48},{16,0},{32,16},{48,32},{1,49},{17,1},{33,17},{49,33},{2,50}... | collective-permute-start | bytes 147464 | tf_op jit(solution)/shard_map/ppermute | solution.py:331
  79.0 5.5 %collective-permute-start.7 = (bf16[96,256]{1,0:T(8,128)(2,1)S(1)}, bf16[96,256]{1,0:T(8,128)(2,1)S(1)}, u32[]{:S(2)}, u32[]{:S(2)}) collective-permute-start(bf16[96,256]{1,0:T(8,128)(2,1)S(1)} %reduce_sum.22), channel_id=1, source_target_pairs={{0,16},{16,32},{32,48},{48,0},{1,17},{17,33},{33,49},{49,1},{2,18}... | collective-permute-start | bytes 147464 | tf_op jit(solution)/shard_map/ppermute | solution.py:331
  81.4 6.8 %collective-permute-start.6 = (bf16[96,256]{1,0:T(8,128)(2,1)S(1)}, bf16[96,256]{1,0:T(8,128)(2,1)S(1)}, u32[]{:S(2)}, u32[]{:S(2)}) collective-permute-start(bf16[96,256]{1,0:T(8,128)(2,1)S(1)} %reduce_sum.22), channel_id=1, source_target_pairs={{0,32},{16,48},{32,0},{48,16},{1,33},{17,49},{33,1},{49,17},{2,34}... | collective-permute-start | bytes 147464 | tf_op jit(solution)/shard_map/ppermute | solution.py:331
  89.3 18.8 %all-to-all-start.2 = ((bf16[32,64,256]{2,1,0:T(8,128)(2,1)}), bf16[32,64,256]{2,1,0:T(8,128)(2,1)S(1)}, u32[]{:S(2)}, u32[]{:S(2)}) async-start(bf16[32,64,256]{2,1,0:T(8,128)(2,1)} %broadcast_in_dim.11), calls=%async_computation.2 | async-start | bytes 2097152 | tf_op jit(solution)/shard_map/all_to_all | solution.py:342
  93.4 5.0 %collective-permute-start.11 = (bf16[8,256]{1,0:T(8,128)(2,1)S(1)}, bf16[8,256]{1,0:T(8,128)(2,1)S(1)}, u32[]{:S(2)}, u32[]{:S(2)}) collective-permute-start(bf16[8,256]{1,0:T(8,128)(2,1)S(1)} %constant_dynamic-slice_fusion), channel_id=1, source_target_pairs={{0,1},{1,0},{2,3},{3,2},{4,5},{5,4},{6,7},{7,6},{8,9},{9,8},{10,11... | collective-permute-start | bytes 12296 | tf_op jit(solution)/shard_map/ppermute | solution.py:238
  96.7 9.0 %collective-permute-start.9 = (f32[2,512]{1,0:T(2,128)S(1)}, f32[2,512]{1,0:T(2,128)S(1)}, u32[]{:S(2)}, u32[]{:S(2)}) collective-permute-start(f32[2,512]{1,0:T(2,128)S(1)} %get-tuple-element.41), channel_id=1, source_target_pairs={{0,255},{1,0},{2,1},{3,2},{4,3},{5,4},{6,5},{7,6},{8,7},{9,8},{10,... | collective-permute-start | bytes 12296 | tf_op jit(solution)/shard_map/ppermute | solution.py:243
  96.8 8.9 %collective-permute-start.10 = (f32[2,512]{1,0:T(2,128)S(1)}, f32[2,512]{1,0:T(2,128)S(1)}, u32[]{:S(2)}, u32[]{:S(2)}) collective-permute-start(f32[2,512]{1,0:T(2,128)S(1)} %get-tuple-element.42), channel_id=1, source_target_pairs={{0,1},{1,2},{2,3},{3,4},{4,5},{5,6},{6,7},{7,8},{8,9},{9,10},{10,1... | collective-permute-start | bytes 12296 | tf_op jit(solution)/shard_map/ppermute | solution.py:243
  108.1 6.3 %collective-permute-start.12 = (bf16[2048,256]{1,0:T(8,128)(2,1)S(1)}, bf16[2048,256]{1,0:T(8,128)(2,1)S(1)}, u32[]{:S(2)}, u32[]{:S(2)}) collective-permute-start(bf16[2048,256]{1,0:T(8,128)(2,1)S(1)} %bitcast.29), channel_id=1, source_target_pairs={{0,1},{1,0},{2,3},{3,2},{4,5},{5,4},{6,7},{7,6},{8,9},{9,8},{10,11... | collective-permute-start | bytes 3145736 | tf_op jit(solution)/shard_map/ppermute | solution.py:238

commit v8 on v7

--- a/solution.py
+++ b/solution.py
@@ -47,7 +47,7 @@
 def group_kernel(
     core_ref, rows_ref, places_ref, slot_ref, own_ref, below_ref, above_ref, below_two_ref, above_two_ref,
     mine_ref, other_ref, wk_ref, wv_ref, wq_ref, cells_hbm, wo_hbm,
-    grad_cells_ref, sums_ref, roots_ref, keep_ref, send_ref,
+    grad_cells_ref, inner_ref, middle_ref, outer_ref, roots_ref, keep_ref, send_ref,
     cells_ref, wo_ref, table_ref, sems,
 ):
     load_cells = pltpu.make_async_copy(cells_hbm, cells_ref, sems.at[0])
@@ -131,9 +131,13 @@
     onehot = jnp.where(
         lax.broadcasted_iota(jnp.int32, (SLOTS, cell_out.shape[0]), 0) == slot_ref[...], 1.0, 0.0
     ).astype(bf16)
-    sums_ref[...] = mm(onehot, cell_out)
-
+    sums = mm(onehot, cell_out)
     basins = own_ref.shape[0] - 1
+    low, top = sums[:basins], sums[2 * basins : 3 * basins]
+    middle_ref[...] = sums[basins : 2 * basins]
+    inner_ref[...] = jnp.where(first, top, low)
+    outer_ref[...] = jnp.where(first, low, top)
+
     row = lax.broadcasted_iota(jnp.int32, (SLOTS, 128), 0)
     lane = lax.broadcasted_iota(jnp.int32, (SLOTS, 128), 1)
     counts = jnp.zeros((SLOTS, 128), f32)
@@ -275,8 +279,6 @@
     below_two, above_two = shifted(small, 2), shifted(small, -2)
     mine = after(mine, below, above, below_two, above_two)
     other = swap(mine)
-    low, mid, top = slice(0, own), slice(own, 2 * own), slice(2 * own, 3 * own)
-
     block = pattern[0]
     along_x = block % SIZES["x"]
     near = (block // SIZES["x"]) % SIZES["near"]
@@ -293,17 +295,19 @@
     vmem = pl.BlockSpec(memory_space=pltpu.VMEM)
     smem = pl.BlockSpec(memory_space=pltpu.SMEM)
     hbm = pl.BlockSpec(memory_space=pltpu.HBM)
-    grad_cells, sums, roots, keep, send = pl.pallas_call(
+    grad_cells, inner, middle, outer, roots, keep, send = pl.pallas_call(
         group_kernel,
         out_shape=(
             jax.ShapeDtypeStruct(cells.shape, bf16),
-            jax.ShapeDtypeStruct((SLOTS, width), f32),
+            jax.ShapeDtypeStruct((own, width), f32),
+            jax.ShapeDtypeStruct((own, width), f32),
+            jax.ShapeDtypeStruct((own, width), f32),
             jax.ShapeDtypeStruct((SLOTS, 128), f32),
             jax.ShapeDtypeStruct((payload, half), bf16),
             jax.ShapeDtypeStruct((payload, half), bf16),
         ),
         in_specs=[smem] + [vmem] * 13 + [hbm] * 2,
-        out_specs=(vmem,) * 5,
+        out_specs=(vmem,) * 7,
         scratch_shapes=[
             pltpu.VMEM(cells.shape, bf16),
             pltpu.VMEM(w_out.shape, bf16),
@@ -331,25 +335,30 @@
         lax.ppermute(column, "far", [(i, (i + s) % count) for i in range(count)])
         for s in range(1, count)
     ]
+    inner, outer = lax.optimization_barrier((inner, outer, column))[:2]
+    from_inner = swap(inner)
+    total_devices = lax.axis_size(EVERY)
+    from_outer = lax.ppermute(
+        outer,
+        EVERY,
+        [(i, (i + (1 if i % 2 else -1)) % total_devices) for i in range(total_devices)],
+    )
     reduced = (
         (column.astype(f32) + turns[1].astype(f32)) + (turns[0].astype(f32) + turns[2].astype(f32))
     ).astype(bf16)
+    reduced = after(reduced, from_inner, from_outer)
+    weights = lax.all_to_all(copied(reduced[:weight_chunk], MEMBERS), GROUP, 0, 0, tiled=True)
+
+    pooled = ((middle + from_inner + from_outer) / roots[own : 2 * own, :1]).astype(bf16)
     own_gauge = lax.dynamic_slice_in_dim(
         reduced, weight_chunk + lax.axis_index("far") * GAUGE_ROWS, GAUGE_ROWS, 0
     )
-
-    copies = copied(reduced[:weight_chunk], MEMBERS)
-    weights = lax.all_to_all(copies, GROUP, 0, 0, tiled=True)
-    late_sums, late_gauge = lax.optimization_barrier((sums, own_gauge, copies))[:2]
-    far_gauge = swap(late_gauge)
-    from_above, from_below = shifted(late_sums[low], -1), shifted(late_sums[top], 1)
-    pooled = ((sums[mid] + from_above + from_below) / roots[mid, :1]).astype(bf16)
+    far_gauge = swap(after(own_gauge, weights))
     grad_gauges = jnp.where(
         core == 0,
         jnp.concatenate([own_gauge, far_gauge], axis=1),
         jnp.concatenate([far_gauge, own_gauge], axis=1),
     )
-    weights = after(weights, pooled, grad_gauges)
     far = swap(weights)
     grads = widen(core, weights, None)
     grads = widen(1 - core, far, grads)

time: 116 us -> 116 us (level)
  blocking collectives: 26.2 us -> 44.7 us
  waiting for transfers between devices: 28.9 us -> 17.2 us
  starting transfers between devices: 46.2 us -> 39.8 us
    all_to_all x0 -> x1, blocking collectives: none -> 18.5 us  [per_device(): lax.all_to_all(copied(reduced[:weight_chunk], MEMBERS), GROUP, 0, 0, tile...]
    ppermute x6 -> x4, waiting for transfers between devices: 14.4 us -> 7.82 us  [shifted(): lax.ppermute(value, EVERY, [(i, (i + steps) % count) for i in range(count)])]
    all_to_all x1 -> x0, starting transfers between devices: 3.93 us -> none  [per_device(): weights = lax.all_to_all(copies, GROUP, 0, 0, tiled=True)]
    ppermute x3, waiting for transfers between devices: 6.82 us -> 4.43 us  [per_device(): lax.ppermute(column, 'far', [(i, (i + s) % count) for i in range(count)])]
    all_to_all x1 -> x0, waiting for transfers between devices: 1.88 us -> none  [per_device(): weights = lax.all_to_all(copies, GROUP, 0, 0, tiled=True)]
    ppermute x6 -> x4, starting transfers between devices: 15.8 us -> 14 us  [shifted(): lax.ppermute(value, EVERY, [(i, (i + steps) % count) for i in range(count)])]
    ppermute x4 -> x5, starting transfers between devices: 7.55 us -> 6.58 us  [swap(): return lax.ppermute(value, 'c', [(0, 1), (1, 0)])]
    ppermute x4 -> x5, waiting for transfers between devices: 5.8 us -> 4.92 us  [swap(): return lax.ppermute(value, 'c', [(0, 1), (1, 0)])]
  transfers between devices with their start and end apart: 15 -> 14, of which waited for: 10 -> 6; matrix products, arithmetic and copies ran while one was open for 2% -> 2% of each run, Pallas kernels for 1% -> 1%
where the time goes in v8:
time: 116 us; the launch traced here: 115 us
  blocking collectives  44.7 us (39%)
  starting transfers between devices  39.8 us (34%)
  waiting for transfers between devices  17.2 us (15%)
  Pallas kernels  8.55 us (7%)
  other arithmetic  2.17 us (2%)
  local copies, waits for them, and re-layouts  1.91 us (2%)
    all_to_all x1, blocking collectives, per_device(): lax.all_to_all(chip, GROUP, 0, 0, tiled=True).reshape(MEMBERS, chunk, half)  26.2 us
    all_to_all x1, blocking collectives, per_device(): lax.all_to_all(copied(reduced[:weight_chunk], MEMBERS), GROUP, 0, 0, tile...  18.5 us
    all_to_all x1, starting transfers between devices, per_device(): mine = lax.all_to_all(copies, TILES, 0, 0, tiled=True)  16.3 us
    ppermute x4, starting transfers between devices, shifted(): lax.ppermute(value, EVERY, [(i, (i + steps) % count) for i in range(count)])  14 us
    ppermute x4, waiting for transfers between devices, shifted(): lax.ppermute(value, EVERY, [(i, (i + steps) % count) for i in range(count)])  7.82 us
    ppermute x5, starting transfers between devices, swap(): return lax.ppermute(value, 'c', [(0, 1), (1, 0)])  6.58 us
    pallas_call x1, Pallas kernels, per_device(): pl.pallas_call(group_kernel, out_shape=(jax.ShapeDtypeStruct(cells.shape,...  5.79 us
    ppermute x5, waiting for transfers between devices, swap(): return lax.ppermute(value, 'c', [(0, 1), (1, 0)])  4.92 us
  transfers between devices with their start and end apart: 14, of which 6 were waited for; matrix products, arithmetic and copies ran while one was open for 2% of the time, Pallas kernels for 1%

profile of v8, /device:TPU:1, one launch (start us, length us, event | category | flops | bytes accessed | tf_op | source)
XLA Modules:
  0.0 115.3 jit_solution(14838945685977391827)
XLA Ops:
  0.7 0.6 copy-done
  1.3 0.8 broadcast_in_dim.10
  2.2 16.3 %all-to-all-start = ((bf16[128,8,256]{2,1,0:T(8,128)(2,1)}), bf16[128,8,256]{2,1,0:T(8,128)(2,1)S(1)}, u32[]{:S(2)}, u32[]{:S(2)}) async-start(bf16[128,8,256]{2,1,0:T(8,128)(2,1)} %broadcast_in_dim.10), calls=%async_computation | async-start | bytes 1048576 | tf_op jit(solution)/shard_map/all_to_all | solution.py:269
  18.6 0.1 convert_reduce_fusion
  18.7 1.0 collective-permute-start.1
  19.8 0.8 collective-permute-start
  20.6 12.1 %collective-permute-start.3 = (bf16[1,128]{1,0:T(2,128)(2,1)S(1)}, bf16[1,128]{1,0:T(2,128)(2,1)S(1)}, u32[]{:S(2)}, u32[]{:S(2)}) collective-permute-start(bf16[1,128]{1,0:T(2,128)(2,1)S(1)} %slice.12), channel_id=1, source_target_pairs={{0,254},{1,255},{2,0},{3,1},{4,2},{5,3},{6,4},{7,5},{8,6},{9,7},{1... | collective-permute-start | bytes 776 | tf_op jit(solution)/shard_map/ppermute | solution.py:247
  32.7 0.7 collective-permute-done.3.above_two_ref
  33.5 7.1 %collective-permute-done.2.below_two_ref = bf16[1,128]{1,0:T(2,128)(2,1)S(1)} collective-permute-done((bf16[1,128]{1,0:T(2,128)(2,1)S(1)}, bf16[1,128]{1,0:T(2,128)(2,1)S(1)}, u32[]{:S(2)}, u32[]{:S(2)}) %collective-permute-start.2) | collective-permute-done | bytes 288 | tf_op jit(solution)/shard_map/ppermute | solution.py:247
  40.6 0.1 collective-permute-start.4
  41.0 1.6 %collective-permute-done.4.other_ref = bf16[1024,256]{1,0:T(8,128)(2,1)S(1)} collective-permute-done((bf16[1024,256]{1,0:T(8,128)(2,1)S(1)}, bf16[1024,256]{1,0:T(8,128)(2,1)S(1)}, u32[]{:S(2)}, u32[]{:S(2)}) %collective-permute-start.4) | collective-permute-done | bytes 524320 | tf_op jit(solution)/shard_map/ppermute | solution.py:242
  42.6 5.8 %group_kernel.1 = (bf16[256,512]{1,0:T(8,128)(2,1)}, f32[2,512]{1,0:T(2,128)S(1)}, f32[2,512]{1,0:T(2,128)S(1)}, f32[2,512]{1,0:T(2,128)S(1)}, f32[16,128]{1,0:T...) custom-call(s32[1]{0:T(128)} %bitcast.core_ref.side_ref, s32[1,128]{1,0:T(1,128)S(1)} %add.166.rows_ref, ...), custom_call_target="tpu_custom_call" | custom-call | tf_op jit(solution)/shard_map/group_kernel/pallas_call | solution.py:298
  48.4 0.2 collective-permute-start.5
  48.6 3.3 %collective-permute-done.5 = bf16[3072,256]{1,0:T(8,128)(2,1)S(1)} collective-permute-done((bf16[3072,256]{1,0:T(8,128)(2,1)S(1)}, bf16[3072,256]{1,0:T(8,128)(2,1)S(1)}, u32[]{:S(2)}, u32[]{:S(2)}) %collective-permute-start.5) | collective-permute-done | bytes 1572896 | tf_op jit(solution)/shard_map/ppermute | solution.py:242
  51.9 0.4 add_convert_fusion
  52.3 26.2 %all_to_all.27 = bf16[32,96,256]{2,1,0:T(8,128)(2,1)S(1)} all-to-all(bf16[32,96,256]{2,1,0:T(8,128)(2,1)S(1)} %bitcast.35), channel_id=1, replica_groups=mesh['y'=4,'far'=4,'near'=2,'x'=4,'c'=2] {'y','x','near'}, dimensions={0} | all-to-all | bytes 3145728 | tf_op jit(solution)/shard_map/all_to_all | solution.py:331
  78.5 0.2 reduce_sum.22
  78.7 0.3 collective-permute-start.10
  79.0 2.4 %collective-permute-start.9 = (bf16[96,256]{1,0:T(8,128)(2,1)S(1)}, bf16[96,256]{1,0:T(8,128)(2,1)S(1)}, u32[]{:S(2)}, u32[]{:S(2)}) collective-permute-start(bf16[96,256]{1,0:T(8,128)(2,1)S(1)} %reduce_sum.22), channel_id=1, source_target_pairs={{0,16},{16,32},{32,48},{48,0},{1,17},{17,33},{33,49},{49,1},{2,18}... | collective-permute-start | bytes 147464 | tf_op jit(solution)/shard_map/ppermute | solution.py:335
  81.3 2.2 %collective-permute-start.6 = (f32[2,512]{1,0:T(2,128)S(1)}, f32[2,512]{1,0:T(2,128)S(1)}, u32[]{:S(2)}, u32[]{:S(2)}) collective-permute-start(f32[2,512]{1,0:T(2,128)S(1)} %get-tuple-element.33), channel_id=1, source_target_pairs={{0,1},{1,0},{2,3},{3,2},{4,5},{5,4},{6,7},{7,6},{8,9},{9,8},{10,11... | collective-permute-start | bytes 12296 | tf_op jit(solution)/shard_map/ppermute | solution.py:242
  83.5 0.2 collective-permute-start.7
  83.7 0.8 collective-permute-done.9
  84.5 3.7 %collective-permute-done.8 = bf16[96,256]{1,0:T(8,128)(2,1)S(1)} collective-permute-done((bf16[96,256]{1,0:T(8,128)(2,1)S(1)}, bf16[96,256]{1,0:T(8,128)(2,1)S(1)}, u32[]{:S(2)}, u32[]{:S(2)}) %collective-permute-start.8) | collective-permute-done | bytes 49184 | tf_op jit(solution)/shard_map/ppermute | solution.py:335
  88.2 0.1 broadcast_in_dim.11
  88.3 18.5 %all_to_all.28 = bf16[32,64,256]{2,1,0:T(8,128)(2,1)S(1)} all-to-all(bf16[32,64,256]{2,1,0:T(8,128)(2,1)S(1)} %broadcast_in_dim.11), channel_id=1, replica_groups=mesh['y'=4,'far'=4,'near'=2,'x'=4,'c'=2] {'y','x','near'}, dimensions={0} | all-to-all | bytes 2097152 | tf_op jit(solution)/shard_map/all_to_all | solution.py:350
  106.8 4.0 %collective-permute-start.12 = (bf16[2048,256]{1,0:T(8,128)(2,1)S(1)}, bf16[2048,256]{1,0:T(8,128)(2,1)S(1)}, u32[]{:S(2)}, u32[]{:S(2)}) collective-permute-start(bf16[2048,256]{1,0:T(8,128)(2,1)S(1)} %bitcast.29), channel_id=1, source_target_pairs={{0,1},{1,0},{2,3},{3,2},{4,5},{5,4},{6,7},{7,6},{8,9},{9,8},{10,11... | collective-permute-start | bytes 3145736 | tf_op jit(solution)/shard_map/ppermute | solution.py:242
  110.9 0.1 slice_reduce_fusion
  111.0 0.1 collective-permute-start.11
  111.1 0.7 fusion
  111.8 1.4 %widen_kernel.2 = (f32[512,512]{1,0:T(8,128)}, f32[512,512]{1,0:T(8,128)}, f32[512,512]{1,0:T(8,128)}, f32[512,512]{1,0:T(8,128)}) custom-call(s32[1]{0:T(128)} %bitcast.core_ref.side_ref, bf16[4,512,256]{2,1,0:T(8,128)(2,1)S(1)} %bitcast.30), custom_call_target="tpu_custom_call" | custom-call | tf_op jit(solution)/shard_map/widen_kernel/pallas_call | solution.py:222
  113.2 0.6 maximum_select_fusion
  113.8 1.4 %widen_kernel.3 = (f32[512,512]{1,0:T(8,128)}, f32[512,512]{1,0:T(8,128)}, f32[512,512]{1,0:T(8,128)}, f32[512,512]{1,0:T(8,128)}) custom-call(s32[1]{0:T(128)} %bitcast.6.side_ref, bf16[4,512,256]{2,1,0:T(8,128)(2,1)S(1)} %bitcast.33, ...), custom_call_target="tpu_custom_call", output_to_operand_aliasing={{0}: (2, {}), {1}: (3, {}), {2}: (4, {}), {3}: (5, {})} | custom-call | tf_op jit(solution)/shard_map/widen_kernel/pallas_call | solution.py:222
  (36 shorter events, 0.5 us)
Async XLA Ops:
  0.6 0.7 copy-start
  0.7 17.9 %copy-start.5 = (s32[256]{0:T(256)S(1)}, s32[256]{0:T(256)}, u32[]{:S(2)}) copy-start(s32[256]{0:T(256)} %param.16) | copy-start | bytes 3076
  0.7 18.0 %copy-start.4 = (bf16[2,512]{1,0:T(2,128)(2,1)S(1)}, bf16[2,512]{1,0:T(2,128)(2,1)}, u32[]{:S(2)}) copy-start(bf16[2,512]{1,0:T(2,128)(2,1)} %param.17) | copy-start | bytes 6148
  0.7 40.0 %copy-start.6 = (s32[1,16]{1,0:T(1,128)S(1)}, s32[1,16]{1,0:T(1,128)}, u32[]{:S(2)}) copy-start(s32[1,16]{1,0:T(1,128)} %param.15) | copy-start | bytes 196
  0.7 41.9 %copy-start.2 = (bf16[512,512]{1,0:T(8,128)(2,1)S(1)}, bf16[512,512]{1,0:T(8,128)(2,1)}, u32[]{:S(2)}) copy-start(bf16[512,512]{1,0:T(8,128)(2,1)} %wv_ref.1) | copy-start | bytes 1572868
  0.7 41.9 %copy-start.1 = (bf16[512,512]{1,0:T(8,128)(2,1)S(1)}, bf16[512,512]{1,0:T(8,128)(2,1)}, u32[]{:S(2)}) copy-start(bf16[512,512]{1,0:T(8,128)(2,1)} %wk_ref.1) | copy-start | bytes 1572868
  0.7 41.9 %copy-start.3 = (bf16[512,512]{1,0:T(8,128)(2,1)S(1)}, bf16[512,512]{1,0:T(8,128)(2,1)}, u32[]{:S(2)}) copy-start(bf16[512,512]{1,0:T(8,128)(2,1)} %wq_ref.1) | copy-start | bytes 1572868
  2.2 38.4 %all-to-all-start = ((bf16[128,8,256]{2,1,0:T(8,128)(2,1)}), bf16[128,8,256]{2,1,0:T(8,128)(2,1)S(1)}, u32[]{:S(2)}, u32[]{:S(2)}) async-start(bf16[128,8,256]{2,1,0:T(8,128)(2,1)} %broadcast_in_dim.10), calls=%async_computation | async-start | bytes 1048576 | tf_op jit(solution)/shard_map/all_to_all | solution.py:269
  18.7 21.8 %collective-permute-start.1 = (bf16[3,512]{1,0:T(4,128)(2,1)S(1)}, bf16[3,512]{1,0:T(4,128)(2,1)S(1)}, u32[]{:S(2)}, u32[]{:S(2)}) collective-permute-start(bf16[3,512]{1,0:T(4,128)(2,1)S(1)} %pad_maximum_fusion.own_ref), channel_id=1, source_target_pairs={{0,255},{1,0},{2,1},{3,2},{4,3},{5,4},{6,5},{7,6},{8,7},{9,8},{10,... | collective-permute-start | bytes 9224 | tf_op jit(solution)/shard_map/ppermute | solution.py:247
  19.8 20.8 %collective-permute-start = (bf16[3,512]{1,0:T(4,128)(2,1)S(1)}, bf16[3,512]{1,0:T(4,128)(2,1)S(1)}, u32[]{:S(2)}, u32[]{:S(2)}) collective-permute-start(bf16[3,512]{1,0:T(4,128)(2,1)S(1)} %pad_maximum_fusion.own_ref), channel_id=1, source_target_pairs={{0,1},{1,2},{2,3},{3,4},{4,5},{5,6},{6,7},{7,8},{8,9},{9,10},{10,1... | collective-permute-start | bytes 9224 | tf_op jit(solution)/shard_map/ppermute | solution.py:247
  20.6 12.9 %collective-permute-start.3 = (bf16[1,128]{1,0:T(2,128)(2,1)S(1)}, bf16[1,128]{1,0:T(2,128)(2,1)S(1)}, u32[]{:S(2)}, u32[]{:S(2)}) collective-permute-start(bf16[1,128]{1,0:T(2,128)(2,1)S(1)} %slice.12), channel_id=1, source_target_pairs={{0,254},{1,255},{2,0},{3,1},{4,2},{5,3},{6,4},{7,5},{8,6},{9,7},{1... | collective-permute-start | bytes 776 | tf_op jit(solution)/shard_map/ppermute | solution.py:247
  32.7 7.8 %collective-permute-start.2 = (bf16[1,128]{1,0:T(2,128)(2,1)S(1)}, bf16[1,128]{1,0:T(2,128)(2,1)S(1)}, u32[]{:S(2)}, u32[]{:S(2)}) collective-permute-start(bf16[1,128]{1,0:T(2,128)(2,1)S(1)} %slice.12), channel_id=1, source_target_pairs={{0,2},{1,3},{2,4},{3,5},{4,6},{5,7},{6,8},{7,9},{8,10},{9,11},{10,... | collective-permute-start | bytes 776 | tf_op jit(solution)/shard_map/ppermute | solution.py:247
  40.6 2.0 %collective-permute-start.4 = (bf16[1024,256]{1,0:T(8,128)(2,1)S(1)}, bf16[1024,256]{1,0:T(8,128)(2,1)S(1)}, u32[]{:S(2)}, u32[]{:S(2)}) collective-permute-start(bf16[1024,256]{1,0:T(8,128)(2,1)S(1)} %bitcast.31), channel_id=1, source_target_pairs={{0,1},{1,0},{2,3},{3,2},{4,5},{5,4},{6,7},{7,6},{8,9},{9,8},{10,11... | collective-permute-start | bytes 1572872 | tf_op jit(solution)/shard_map/ppermute | solution.py:242
  48.4 3.5 %collective-permute-start.5 = (bf16[3072,256]{1,0:T(8,128)(2,1)S(1)}, bf16[3072,256]{1,0:T(8,128)(2,1)S(1)}, u32[]{:S(2)}, u32[]{:S(2)}) collective-permute-start(bf16[3072,256]{1,0:T(8,128)(2,1)S(1)} %get-tuple-element.32), channel_id=1, source_target_pairs={{0,1},{1,0},{2,3},{3,2},{4,5},{5,4},{6,7},{7,6},{8,9},{9,8},{10,11... | collective-permute-start | bytes 4718600 | tf_op jit(solution)/shard_map/ppermute | solution.py:242
  78.7 5.0 %collective-permute-start.10 = (bf16[96,256]{1,0:T(8,128)(2,1)S(1)}, bf16[96,256]{1,0:T(8,128)(2,1)S(1)}, u32[]{:S(2)}, u32[]{:S(2)}) collective-permute-start(bf16[96,256]{1,0:T(8,128)(2,1)S(1)} %reduce_sum.22), channel_id=1, source_target_pairs={{0,48},{16,0},{32,16},{48,32},{1,49},{17,1},{33,17},{49,33},{2,50}... | collective-permute-start | bytes 147464 | tf_op jit(solution)/shard_map/ppermute | solution.py:335
  79.0 5.5 %collective-permute-start.9 = (bf16[96,256]{1,0:T(8,128)(2,1)S(1)}, bf16[96,256]{1,0:T(8,128)(2,1)S(1)}, u32[]{:S(2)}, u32[]{:S(2)}) collective-permute-start(bf16[96,256]{1,0:T(8,128)(2,1)S(1)} %reduce_sum.22), channel_id=1, source_target_pairs={{0,16},{16,32},{32,48},{48,0},{1,17},{17,33},{33,49},{49,1},{2,18}... | collective-permute-start | bytes 147464 | tf_op jit(solution)/shard_map/ppermute | solution.py:335
  81.3 6.8 %collective-permute-start.8 = (bf16[96,256]{1,0:T(8,128)(2,1)S(1)}, bf16[96,256]{1,0:T(8,128)(2,1)S(1)}, u32[]{:S(2)}, u32[]{:S(2)}) collective-permute-start(bf16[96,256]{1,0:T(8,128)(2,1)S(1)} %reduce_sum.22), channel_id=1, source_target_pairs={{0,32},{16,48},{32,0},{48,16},{1,33},{17,49},{33,1},{49,17},{2,34}... | collective-permute-start | bytes 147464 | tf_op jit(solution)/shard_map/ppermute | solution.py:335
  81.3 6.9 %collective-permute-start.6 = (f32[2,512]{1,0:T(2,128)S(1)}, f32[2,512]{1,0:T(2,128)S(1)}, u32[]{:S(2)}, u32[]{:S(2)}) collective-permute-start(f32[2,512]{1,0:T(2,128)S(1)} %get-tuple-element.33), channel_id=1, source_target_pairs={{0,1},{1,0},{2,3},{3,2},{4,5},{5,4},{6,7},{7,6},{8,9},{9,8},{10,11... | collective-permute-start | bytes 12296 | tf_op jit(solution)/shard_map/ppermute | solution.py:242
  83.5 4.7 %collective-permute-start.7 = (f32[2,512]{1,0:T(2,128)S(1)}, f32[2,512]{1,0:T(2,128)S(1)}, u32[]{:S(2)}, u32[]{:S(2)}) collective-permute-start(f32[2,512]{1,0:T(2,128)S(1)} %get-tuple-element.34), channel_id=1, source_target_pairs={{0,255},{1,2},{2,1},{3,4},{4,3},{5,6},{6,5},{7,8},{8,7},{9,10},{10... | collective-permute-start | bytes 12296 | tf_op jit(solution)/shard_map/ppermute | solution.py:341
  106.8 6.9 %collective-permute-start.12 = (bf16[2048,256]{1,0:T(8,128)(2,1)S(1)}, bf16[2048,256]{1,0:T(8,128)(2,1)S(1)}, u32[]{:S(2)}, u32[]{:S(2)}) collective-permute-start(bf16[2048,256]{1,0:T(8,128)(2,1)S(1)} %bitcast.29), channel_id=1, source_target_pairs={{0,1},{1,0},{2,3},{3,2},{4,5},{5,4},{6,7},{7,6},{8,9},{9,8},{10,11... | collective-permute-start | bytes 3145736 | tf_op jit(solution)/shard_map/ppermute | solution.py:242
  111.0 2.2 %collective-permute-start.11 = (bf16[8,256]{1,0:T(8,128)(2,1)S(1)}, bf16[8,256]{1,0:T(8,128)(2,1)S(1)}, u32[]{:S(2)}, u32[]{:S(2)}) collective-permute-start(bf16[8,256]{1,0:T(8,128)(2,1)S(1)} %constant_dynamic-slice_fusion), channel_id=1, source_target_pairs={{0,1},{1,0},{2,3},{3,2},{4,5},{5,4},{6,7},{7,6},{8,9},{9,8},{10,11... | collective-permute-start | bytes 12296 | tf_op jit(solution)/shard_map/ppermute | solution.py:242

commit v9 on v8

--- a/solution.py
+++ b/solution.py
@@ -324,7 +324,16 @@
         pltpu.with_memory_space_constraint(w_out, pltpu.HBM),
     )
 
-    chip = (keep.astype(f32) + swap(send).astype(f32)).astype(bf16)
+    from_core = swap(send)
+    from_inner = swap(inner)
+    total_devices = lax.axis_size(EVERY)
+    from_outer = lax.ppermute(
+        outer,
+        EVERY,
+        [(i, (i + (1 if i % 2 else -1)) % total_devices) for i in range(total_devices)],
+    )
+    from_core = after(from_core, from_inner, from_outer)
+    chip = (keep.astype(f32) + from_core.astype(f32)).astype(bf16)
     chunk = payload // MEMBERS
     gauge_chunk = gauges // MEMBERS
     weight_chunk = chunk - gauge_chunk
@@ -335,21 +344,13 @@
         lax.ppermute(column, "far", [(i, (i + s) % count) for i in range(count)])
         for s in range(1, count)
     ]
-    inner, outer = lax.optimization_barrier((inner, outer, column))[:2]
-    from_inner = swap(inner)
-    total_devices = lax.axis_size(EVERY)
-    from_outer = lax.ppermute(
-        outer,
-        EVERY,
-        [(i, (i + (1 if i % 2 else -1)) % total_devices) for i in range(total_devices)],
-    )
     reduced = (
         (column.astype(f32) + turns[1].astype(f32)) + (turns[0].astype(f32) + turns[2].astype(f32))
     ).astype(bf16)
-    reduced = after(reduced, from_inner, from_outer)
+    pooled = ((middle + from_inner + from_outer) / roots[own : 2 * own, :1]).astype(bf16)
+    reduced = after(reduced, pooled)
     weights = lax.all_to_all(copied(reduced[:weight_chunk], MEMBERS), GROUP, 0, 0, tiled=True)
 
-    pooled = ((middle + from_inner + from_outer) / roots[own : 2 * own, :1]).astype(bf16)
     own_gauge = lax.dynamic_slice_in_dim(
         reduced, weight_chunk + lax.axis_index("far") * GAUGE_ROWS, GAUGE_ROWS, 0
     )

time: 116 us -> 118 us (1.017)
  blocking collectives: 44.7 us -> 17.4 us
  waiting for transfers between devices: 17.2 us -> 36.7 us
  starting transfers between devices: 39.8 us -> 49.1 us
  other arithmetic: 2.17 us -> 3.42 us
    all_to_all x1 -> x0, blocking collectives: 26.2 us -> none  [per_device(): lax.all_to_all(chip, GROUP, 0, 0, tiled=True).reshape(MEMBERS, chunk, half)]
    all_to_all x0 -> x1, waiting for transfers between devices: none -> 19.1 us  [per_device(): lax.all_to_all(chip, GROUP, 0, 0, tiled=True).reshape(MEMBERS, chunk, half)]
    ppermute x3, starting transfers between devices: 2.65 us -> 9.41 us  [per_device(): lax.ppermute(column, 'far', [(i, (i + s) % count) for i in range(count)])]
    all_to_all x0 -> x1, starting transfers between devices: none -> 4.15 us  [per_device(): lax.all_to_all(chip, GROUP, 0, 0, tiled=True).reshape(MEMBERS, chunk, half)]
    ppermute x5, starting transfers between devices: 6.58 us -> 5.16 us  [swap(): return lax.ppermute(value, 'c', [(0, 1), (1, 0)])]
    convert_element_type x1, other arithmetic: 0.43 us -> 1.68 us  [per_device(): chip = (keep.astype(f32) + from_core.astype(f32)).astype(bf16)]
  transfers between devices with their start and end apart: 14 -> 15, of which waited for: 6 -> 9; matrix products, arithmetic and copies ran while one was open for 2% -> 2% of each run, Pallas kernels for 1% -> 1%
where the time goes in v9:
time: 118 us
  starting transfers between devices  49.1 us (42%)
  waiting for transfers between devices  36.7 us (31%)
  blocking collectives  17.4 us (15%)
  Pallas kernels  8.55 us (7%)
  other arithmetic  3.42 us (3%)
  local copies, waits for them, and re-layouts  1.91 us (2%)
    all_to_all x1, waiting for transfers between devices, per_device(): lax.all_to_all(chip, GROUP, 0, 0, tiled=True).reshape(MEMBERS, chunk, half)  19.1 us
    all_to_all x1, blocking collectives, per_device(): lax.all_to_all(copied(reduced[:weight_chunk], MEMBERS), GROUP, 0, 0, tile...  17.4 us
    all_to_all x1, starting transfers between devices, per_device(): mine = lax.all_to_all(copies, TILES, 0, 0, tiled=True)  16.3 us
    ppermute x4, starting transfers between devices, shifted(): lax.ppermute(value, EVERY, [(i, (i + steps) % count) for i in range(count)])  14 us
    ppermute x3, starting transfers between devices, per_device(): lax.ppermute(column, 'far', [(i, (i + s) % count) for i in range(count)])  9.41 us
    ppermute x4, waiting for transfers between devices, shifted(): lax.ppermute(value, EVERY, [(i, (i + steps) % count) for i in range(count)])  7.82 us
    pallas_call x1, Pallas kernels, per_device(): pl.pallas_call(group_kernel, out_shape=(jax.ShapeDtypeStruct(cells.shape,...  5.79 us
    ppermute x5, waiting for transfers between devices, swap(): return lax.ppermute(value, 'c', [(0, 1), (1, 0)])  5.41 us
  transfers between devices with their start and end apart: 15, of which 9 were waited for; matrix products, arithmetic and copies ran while one was open for 2% of the time, Pallas kernels for 1%

profile of v9, /device:TPU:1, one launch (start us, length us, event | category | flops | bytes accessed | tf_op | source)
XLA Modules:
  0.0 118.0 jit_solution(11277408519795056835)
XLA Ops:
  0.7 0.6 copy-done
  1.3 0.8 broadcast_in_dim.10
  2.2 16.3 %all-to-all-start = ((bf16[128,8,256]{2,1,0:T(8,128)(2,1)}), bf16[128,8,256]{2,1,0:T(8,128)(2,1)S(1)}, u32[]{:S(2)}, u32[]{:S(2)}) async-start(bf16[128,8,256]{2,1,0:T(8,128)(2,1)} %broadcast_in_dim.10), calls=%async_computation | async-start | bytes 1048576 | tf_op jit(solution)/shard_map/all_to_all | solution.py:269
  18.6 0.1 convert_reduce_fusion
  18.7 1.0 collective-permute-start.1
  19.8 0.8 collective-permute-start
  20.6 12.1 %collective-permute-start.3 = (bf16[1,128]{1,0:T(2,128)(2,1)S(1)}, bf16[1,128]{1,0:T(2,128)(2,1)S(1)}, u32[]{:S(2)}, u32[]{:S(2)}) collective-permute-start(bf16[1,128]{1,0:T(2,128)(2,1)S(1)} %slice.12), channel_id=1, source_target_pairs={{0,254},{1,255},{2,0},{3,1},{4,2},{5,3},{6,4},{7,5},{8,6},{9,7},{1... | collective-permute-start | bytes 776 | tf_op jit(solution)/shard_map/ppermute | solution.py:247
  32.7 0.7 collective-permute-done.3.above_two_ref
  33.5 7.1 %collective-permute-done.2.below_two_ref = bf16[1,128]{1,0:T(2,128)(2,1)S(1)} collective-permute-done((bf16[1,128]{1,0:T(2,128)(2,1)S(1)}, bf16[1,128]{1,0:T(2,128)(2,1)S(1)}, u32[]{:S(2)}, u32[]{:S(2)}) %collective-permute-start.2) | collective-permute-done | bytes 288 | tf_op jit(solution)/shard_map/ppermute | solution.py:247
  41.0 1.6 %collective-permute-done.4.other_ref = bf16[1024,256]{1,0:T(8,128)(2,1)S(1)} collective-permute-done((bf16[1024,256]{1,0:T(8,128)(2,1)S(1)}, bf16[1024,256]{1,0:T(8,128)(2,1)S(1)}, u32[]{:S(2)}, u32[]{:S(2)}) %collective-permute-start.4) | collective-permute-done | bytes 524320 | tf_op jit(solution)/shard_map/ppermute | solution.py:242
  42.6 5.8 %group_kernel.1 = (bf16[256,512]{1,0:T(8,128)(2,1)}, f32[2,512]{1,0:T(2,128)S(1)}, f32[2,512]{1,0:T(2,128)S(1)}, f32[2,512]{1,0:T(2,128)S(1)}, f32[16,128]{1,0:T...) custom-call(s32[1]{0:T(128)} %bitcast.core_ref.side_ref, s32[1,128]{1,0:T(1,128)S(1)} %add.166.rows_ref, ...), custom_call_target="tpu_custom_call" | custom-call | tf_op jit(solution)/shard_map/group_kernel/pallas_call | solution.py:298
  48.4 0.2 collective-permute-start.7
  48.6 0.4 collective-permute-start.5
  49.0 2.9 %collective-permute-done.5 = f32[2,512]{1,0:T(2,128)S(1)} collective-permute-done((f32[2,512]{1,0:T(2,128)S(1)}, f32[2,512]{1,0:T(2,128)S(1)}, u32[]{:S(2)}, u32[]{:S(2)}) %collective-permute-start.5) | collective-permute-done | bytes 4128 | tf_op jit(solution)/shard_map/ppermute | solution.py:242
  51.9 0.1 collective-permute-done.6
  52.0 1.7 %add_convert_fusion = bf16[3072,256]{1,0:T(8,128)(2,1)} fusion(bf16[3072,256]{1,0:T(8,128)(2,1)S(1)} %collective-permute-done.7, bf16[3072,256]{1,0:T(8,128)(2,1)S(1)} %get-tuple-element.32), kind=kLoop, calls=%fused_computation | loop fusion | flops 3145728 | bytes 4718592 | tf_op jit(solution)/shard_map/convert_element_type | solution.py:336
  53.7 4.2 %all-to-all-start.1 = ((bf16[32,96,256]{2,1,0:T(8,128)(2,1)}), bf16[32,96,256]{2,1,0:T(8,128)(2,1)S(1)}, u32[]{:S(2)}, u32[]{:S(2)}) async-start(bf16[32,96,256]{2,1,0:T(8,128)(2,1)} %bitcast.35), calls=%async_computation.1 | async-start | bytes 3145728 | tf_op jit(solution)/shard_map/all_to_all | solution.py:340
  57.8 0.1 slice_reduce_fusion
  58.0 19.1 %all-to-all-done.1 = bf16[32,96,256]{2,1,0:T(8,128)(2,1)S(1)} async-done(((bf16[32,96,256]{2,1,0:T(8,128)(2,1)}), bf16[32,96,256]{2,1,0:T(8,128)(2,1)S(1)}, u32[]{:S(2)}, u32[]{:S(2)}) %all-to-all-start.1) | async-done | bytes 1572896 | tf_op jit(solution)/shard_map/all_to_all | solution.py:340
  77.1 0.2 reduce_sum.22
  77.3 7.2 %collective-permute-start.10 = (bf16[96,256]{1,0:T(8,128)(2,1)S(1)}, bf16[96,256]{1,0:T(8,128)(2,1)S(1)}, u32[]{:S(2)}, u32[]{:S(2)}) collective-permute-start(bf16[96,256]{1,0:T(8,128)(2,1)S(1)} %reduce_sum.22), channel_id=1, source_target_pairs={{0,48},{16,0},{32,16},{48,32},{1,49},{17,1},{33,17},{49,33},{2,50}... | collective-permute-start | bytes 147464 | tf_op jit(solution)/shard_map/ppermute | solution.py:344
  84.5 2.2 %collective-permute-start.8 = (bf16[96,256]{1,0:T(8,128)(2,1)S(1)}, bf16[96,256]{1,0:T(8,128)(2,1)S(1)}, u32[]{:S(2)}, u32[]{:S(2)}) collective-permute-start(bf16[96,256]{1,0:T(8,128)(2,1)S(1)} %reduce_sum.22), channel_id=1, source_target_pairs={{0,32},{16,48},{32,0},{48,16},{1,33},{17,49},{33,1},{49,17},{2,34}... | collective-permute-start | bytes 147464 | tf_op jit(solution)/shard_map/ppermute | solution.py:344
  86.7 0.7 fusion
  87.4 3.1 %collective-permute-done.9 = bf16[96,256]{1,0:T(8,128)(2,1)S(1)} collective-permute-done((bf16[96,256]{1,0:T(8,128)(2,1)S(1)}, bf16[96,256]{1,0:T(8,128)(2,1)S(1)}, u32[]{:S(2)}, u32[]{:S(2)}) %collective-permute-start.9) | collective-permute-done | bytes 49184 | tf_op jit(solution)/shard_map/ppermute | solution.py:344
  90.4 1.1 collective-permute-done.8
  91.6 0.1 broadcast_in_dim.11
  91.7 17.4 %all_to_all.27 = bf16[32,64,256]{2,1,0:T(8,128)(2,1)S(1)} all-to-all(bf16[32,64,256]{2,1,0:T(8,128)(2,1)S(1)} %broadcast_in_dim.11), channel_id=1, replica_groups=mesh['y'=4,'far'=4,'near'=2,'x'=4,'c'=2] {'y','x','near'}, dimensions={0} | all-to-all | bytes 2097152 | tf_op jit(solution)/shard_map/all_to_all | solution.py:352
  109.1 4.5 %collective-permute-start.12 = (bf16[2048,256]{1,0:T(8,128)(2,1)S(1)}, bf16[2048,256]{1,0:T(8,128)(2,1)S(1)}, u32[]{:S(2)}, u32[]{:S(2)}) collective-permute-start(bf16[2048,256]{1,0:T(8,128)(2,1)S(1)} %bitcast.29), channel_id=1, source_target_pairs={{0,1},{1,0},{2,3},{3,2},{4,5},{5,4},{6,7},{7,6},{8,9},{9,8},{10,11... | collective-permute-start | bytes 3145736 | tf_op jit(solution)/shard_map/ppermute | solution.py:242
  113.6 1.4 %widen_kernel.2 = (f32[512,512]{1,0:T(8,128)}, f32[512,512]{1,0:T(8,128)}, f32[512,512]{1,0:T(8,128)}, f32[512,512]{1,0:T(8,128)}) custom-call(s32[1]{0:T(128)} %bitcast.core_ref.side_ref, bf16[4,512,256]{2,1,0:T(8,128)(2,1)S(1)} %bitcast.30), custom_call_target="tpu_custom_call" | custom-call | tf_op jit(solution)/shard_map/widen_kernel/pallas_call | solution.py:222
  115.0 0.9 collective-permute-done.11
  115.9 0.6 maximum_select_fusion
  116.5 1.4 %widen_kernel.3 = (f32[512,512]{1,0:T(8,128)}, f32[512,512]{1,0:T(8,128)}, f32[512,512]{1,0:T(8,128)}, f32[512,512]{1,0:T(8,128)}) custom-call(s32[1]{0:T(128)} %bitcast.6.side_ref, bf16[4,512,256]{2,1,0:T(8,128)(2,1)S(1)} %bitcast.33, ...), custom_call_target="tpu_custom_call", output_to_operand_aliasing={{0}: (2, {}), {1}: (3, {}), {2}: (4, {}), {3}: (5, {})} | custom-call | tf_op jit(solution)/shard_map/widen_kernel/pallas_call | solution.py:222
  (37 shorter events, 0.5 us)
Async XLA Ops:
  0.6 0.7 copy-start
  0.7 17.9 %copy-start.5 = (s32[256]{0:T(256)S(1)}, s32[256]{0:T(256)}, u32[]{:S(2)}) copy-start(s32[256]{0:T(256)} %param.16) | copy-start | bytes 3076
  0.7 18.0 %copy-start.4 = (bf16[2,512]{1,0:T(2,128)(2,1)S(1)}, bf16[2,512]{1,0:T(2,128)(2,1)}, u32[]{:S(2)}) copy-start(bf16[2,512]{1,0:T(2,128)(2,1)} %param.17) | copy-start | bytes 6148
  0.7 40.0 %copy-start.6 = (s32[1,16]{1,0:T(1,128)S(1)}, s32[1,16]{1,0:T(1,128)}, u32[]{:S(2)}) copy-start(s32[1,16]{1,0:T(1,128)} %param.15) | copy-start | bytes 196
  0.7 41.9 %copy-start.2 = (bf16[512,512]{1,0:T(8,128)(2,1)S(1)}, bf16[512,512]{1,0:T(8,128)(2,1)}, u32[]{:S(2)}) copy-start(bf16[512,512]{1,0:T(8,128)(2,1)} %wv_ref.1) | copy-start | bytes 1572868
  0.7 41.9 %copy-start.1 = (bf16[512,512]{1,0:T(8,128)(2,1)S(1)}, bf16[512,512]{1,0:T(8,128)(2,1)}, u32[]{:S(2)}) copy-start(bf16[512,512]{1,0:T(8,128)(2,1)} %wk_ref.1) | copy-start | bytes 1572868
  0.7 41.9 %copy-start.3 = (bf16[512,512]{1,0:T(8,128)(2,1)S(1)}, bf16[512,512]{1,0:T(8,128)(2,1)}, u32[]{:S(2)}) copy-start(bf16[512,512]{1,0:T(8,128)(2,1)} %wq_ref.1) | copy-start | bytes 1572868
  2.2 38.4 %all-to-all-start = ((bf16[128,8,256]{2,1,0:T(8,128)(2,1)}), bf16[128,8,256]{2,1,0:T(8,128)(2,1)S(1)}, u32[]{:S(2)}, u32[]{:S(2)}) async-start(bf16[128,8,256]{2,1,0:T(8,128)(2,1)} %broadcast_in_dim.10), calls=%async_computation | async-start | bytes 1048576 | tf_op jit(solution)/shard_map/all_to_all | solution.py:269
  18.7 21.8 %collective-permute-start.1 = (bf16[3,512]{1,0:T(4,128)(2,1)S(1)}, bf16[3,512]{1,0:T(4,128)(2,1)S(1)}, u32[]{:S(2)}, u32[]{:S(2)}) collective-permute-start(bf16[3,512]{1,0:T(4,128)(2,1)S(1)} %pad_maximum_fusion.own_ref), channel_id=1, source_target_pairs={{0,255},{1,0},{2,1},{3,2},{4,3},{5,4},{6,5},{7,6},{8,7},{9,8},{10,... | collective-permute-start | bytes 9224 | tf_op jit(solution)/shard_map/ppermute | solution.py:247
  19.8 20.8 %collective-permute-start = (bf16[3,512]{1,0:T(4,128)(2,1)S(1)}, bf16[3,512]{1,0:T(4,128)(2,1)S(1)}, u32[]{:S(2)}, u32[]{:S(2)}) collective-permute-start(bf16[3,512]{1,0:T(4,128)(2,1)S(1)} %pad_maximum_fusion.own_ref), channel_id=1, source_target_pairs={{0,1},{1,2},{2,3},{3,4},{4,5},{5,6},{6,7},{7,8},{8,9},{9,10},{10,1... | collective-permute-start | bytes 9224 | tf_op jit(solution)/shard_map/ppermute | solution.py:247
  20.6 12.9 %collective-permute-start.3 = (bf16[1,128]{1,0:T(2,128)(2,1)S(1)}, bf16[1,128]{1,0:T(2,128)(2,1)S(1)}, u32[]{:S(2)}, u32[]{:S(2)}) collective-permute-start(bf16[1,128]{1,0:T(2,128)(2,1)S(1)} %slice.12), channel_id=1, source_target_pairs={{0,254},{1,255},{2,0},{3,1},{4,2},{5,3},{6,4},{7,5},{8,6},{9,7},{1... | collective-permute-start | bytes 776 | tf_op jit(solution)/shard_map/ppermute | solution.py:247
  32.7 7.8 %collective-permute-start.2 = (bf16[1,128]{1,0:T(2,128)(2,1)S(1)}, bf16[1,128]{1,0:T(2,128)(2,1)S(1)}, u32[]{:S(2)}, u32[]{:S(2)}) collective-permute-start(bf16[1,128]{1,0:T(2,128)(2,1)S(1)} %slice.12), channel_id=1, source_target_pairs={{0,2},{1,3},{2,4},{3,5},{4,6},{5,7},{6,8},{7,9},{8,10},{9,11},{10,... | collective-permute-start | bytes 776 | tf_op jit(solution)/shard_map/ppermute | solution.py:247
  40.6 2.0 %collective-permute-start.4 = (bf16[1024,256]{1,0:T(8,128)(2,1)S(1)}, bf16[1024,256]{1,0:T(8,128)(2,1)S(1)}, u32[]{:S(2)}, u32[]{:S(2)}) collective-permute-start(bf16[1024,256]{1,0:T(8,128)(2,1)S(1)} %bitcast.31), channel_id=1, source_target_pairs={{0,1},{1,0},{2,3},{3,2},{4,5},{5,4},{6,7},{7,6},{8,9},{9,8},{10,11... | collective-permute-start | bytes 1572872 | tf_op jit(solution)/shard_map/ppermute | solution.py:242
  48.4 3.6 %collective-permute-start.7 = (bf16[3072,256]{1,0:T(8,128)(2,1)S(1)}, bf16[3072,256]{1,0:T(8,128)(2,1)S(1)}, u32[]{:S(2)}, u32[]{:S(2)}) collective-permute-start(bf16[3072,256]{1,0:T(8,128)(2,1)S(1)} %get-tuple-element.33), channel_id=1, source_target_pairs={{0,1},{1,0},{2,3},{3,2},{4,5},{5,4},{6,7},{7,6},{8,9},{9,8},{10,11... | collective-permute-start | bytes 4718600 | tf_op jit(solution)/shard_map/ppermute | solution.py:242
  48.6 3.3 %collective-permute-start.5 = (f32[2,512]{1,0:T(2,128)S(1)}, f32[2,512]{1,0:T(2,128)S(1)}, u32[]{:S(2)}, u32[]{:S(2)}) collective-permute-start(f32[2,512]{1,0:T(2,128)S(1)} %get-tuple-element.28), channel_id=1, source_target_pairs={{0,1},{1,0},{2,3},{3,2},{4,5},{5,4},{6,7},{7,6},{8,9},{9,8},{10,11... | collective-permute-start | bytes 12296 | tf_op jit(solution)/shard_map/ppermute | solution.py:242
  49.0 3.0 %collective-permute-start.6 = (f32[2,512]{1,0:T(2,128)S(1)}, f32[2,512]{1,0:T(2,128)S(1)}, u32[]{:S(2)}, u32[]{:S(2)}) collective-permute-start(f32[2,512]{1,0:T(2,128)S(1)} %get-tuple-element.29), channel_id=1, source_target_pairs={{0,255},{1,2},{2,1},{3,4},{4,3},{5,6},{6,5},{7,8},{8,7},{9,10},{10... | collective-permute-start | bytes 12296 | tf_op jit(solution)/shard_map/ppermute | solution.py:330
  53.7 23.4 %all-to-all-start.1 = ((bf16[32,96,256]{2,1,0:T(8,128)(2,1)}), bf16[32,96,256]{2,1,0:T(8,128)(2,1)S(1)}, u32[]{:S(2)}, u32[]{:S(2)}) async-start(bf16[32,96,256]{2,1,0:T(8,128)(2,1)} %bitcast.35), calls=%async_computation.1 | async-start | bytes 3145728 | tf_op jit(solution)/shard_map/all_to_all | solution.py:340
  77.3 10.1 %collective-permute-start.10 = (bf16[96,256]{1,0:T(8,128)(2,1)S(1)}, bf16[96,256]{1,0:T(8,128)(2,1)S(1)}, u32[]{:S(2)}, u32[]{:S(2)}) collective-permute-start(bf16[96,256]{1,0:T(8,128)(2,1)S(1)} %reduce_sum.22), channel_id=1, source_target_pairs={{0,48},{16,0},{32,16},{48,32},{1,49},{17,1},{33,17},{49,33},{2,50}... | collective-permute-start | bytes 147464 | tf_op jit(solution)/shard_map/ppermute | solution.py:344
  84.5 5.9 %collective-permute-start.9 = (bf16[96,256]{1,0:T(8,128)(2,1)S(1)}, bf16[96,256]{1,0:T(8,128)(2,1)S(1)}, u32[]{:S(2)}, u32[]{:S(2)}) collective-permute-start(bf16[96,256]{1,0:T(8,128)(2,1)S(1)} %reduce_sum.22), channel_id=1, source_target_pairs={{0,16},{16,32},{32,48},{48,0},{1,17},{17,33},{33,49},{49,1},{2,18}... | collective-permute-start | bytes 147464 | tf_op jit(solution)/shard_map/ppermute | solution.py:344
  84.5 7.0 %collective-permute-start.8 = (bf16[96,256]{1,0:T(8,128)(2,1)S(1)}, bf16[96,256]{1,0:T(8,128)(2,1)S(1)}, u32[]{:S(2)}, u32[]{:S(2)}) collective-permute-start(bf16[96,256]{1,0:T(8,128)(2,1)S(1)} %reduce_sum.22), channel_id=1, source_target_pairs={{0,32},{16,48},{32,0},{48,16},{1,33},{17,49},{33,1},{49,17},{2,34}... | collective-permute-start | bytes 147464 | tf_op jit(solution)/shard_map/ppermute | solution.py:344
  109.1 7.4 %collective-permute-start.12 = (bf16[2048,256]{1,0:T(8,128)(2,1)S(1)}, bf16[2048,256]{1,0:T(8,128)(2,1)S(1)}, u32[]{:S(2)}, u32[]{:S(2)}) collective-permute-start(bf16[2048,256]{1,0:T(8,128)(2,1)S(1)} %bitcast.29), channel_id=1, source_target_pairs={{0,1},{1,0},{2,3},{3,2},{4,5},{5,4},{6,7},{7,6},{8,9},{9,8},{10,11... | collective-permute-start | bytes 3145736 | tf_op jit(solution)/shard_map/ppermute | solution.py:242
  113.6 2.3 %collective-permute-start.11 = (bf16[8,256]{1,0:T(8,128)(2,1)S(1)}, bf16[8,256]{1,0:T(8,128)(2,1)S(1)}, u32[]{:S(2)}, u32[]{:S(2)}) collective-permute-start(bf16[8,256]{1,0:T(8,128)(2,1)S(1)} %constant_dynamic-slice_fusion), channel_id=1, source_target_pairs={{0,1},{1,0},{2,3},{3,2},{4,5},{5,4},{6,7},{7,6},{8,9},{9,8},{10,11... | collective-permute-start | bytes 12296 | tf_op jit(solution)/shard_map/ppermute | solution.py:242

commit v10 on v9

--- a/solution.py
+++ b/solution.py
@@ -155,7 +155,7 @@
     for place, source in enumerate((below_ref, own_ref, above_ref)):
         table_ref[place * basins : (place + 1) * basins, :] = source[0:basins, :].astype(f32)
     roots = jnp.sqrt(jnp.where(used, counts, 1.0))
-    roots_ref[...] = jnp.broadcast_to(roots, roots_ref.shape)
+    roots_ref[...] = jnp.broadcast_to(roots[basins : 2 * basins], roots_ref.shape)
     table = (table_ref[...] / roots).astype(bf16)
     out_grad = mm_rows(onehot, table).astype(bf16)
     attended_grad = mm_cols(out_grad, wo_ref[...]).astype(bf16)
@@ -199,8 +199,7 @@
         )
 
 
-def widen_kernel(side_ref, part_ref, *refs):
-    out_refs, (wide_ref, sems) = refs[-6:-2], refs[-2:]
+def write_half(side_ref, part_ref, out_refs, wide_ref, sems):
     half = part_ref.shape[2]
     columns = pl.ds(pl.multiple_of(side_ref[0] * half, half), half)
     copies = []
@@ -210,32 +209,48 @@
             pltpu.make_async_copy(wide_ref.at[i], out_ref.at[:, columns], sems.at[i])
         )
         copies[-1].start()
+    return copies
+
+
+def widen_kernel(side_ref, part_ref, *refs):
+    for copy in write_half(side_ref, part_ref, refs[:4], *refs[4:]):
+        copy.wait()
+
+
+def finish_kernel(side_ref, part_ref, own_ref, far_ref, *refs):
+    gauge_ref = refs[8]
+    copies = write_half(side_ref, part_ref, refs[4:8], *refs[9:])
+    half = own_ref.shape[1]
+    first = side_ref[0] == 1
+    own, far = own_ref[...], far_ref[...]
+    gauge_ref[:, :half] = jnp.where(first, own, far)
+    gauge_ref[:, half:] = jnp.where(first, far, own)
     for copy in copies:
         copy.wait()
 
 
-def widen(side, part, grads):
+def widen(side, part, *rest):
     half = part.shape[1]
     width = 2 * half
-    given = () if grads is None else tuple(grads)
+    smem = pl.BlockSpec(memory_space=pltpu.SMEM)
+    vmem = pl.BlockSpec(memory_space=pltpu.VMEM)
     hbm = pl.BlockSpec(memory_space=pltpu.HBM)
+    shapes = (jax.ShapeDtypeStruct((width, width), f32),) * 4
+    if rest:
+        shapes += (jax.ShapeDtypeStruct((rest[0].shape[0], width), bf16),)
     return pl.pallas_call(
-        widen_kernel,
-        out_shape=(jax.ShapeDtypeStruct((width, width), f32),) * 4,
-        in_specs=[
-            pl.BlockSpec(memory_space=pltpu.SMEM),
-            pl.BlockSpec(memory_space=pltpu.VMEM),
-        ]
-        + [hbm] * len(given),
-        out_specs=(hbm,) * 4,
+        finish_kernel if rest else widen_kernel,
+        out_shape=shapes,
+        in_specs=[smem, vmem] + ([vmem] * 2 + [hbm] * 4 if rest else []),
+        out_specs=(hbm,) * 4 + ((vmem,) if rest else ()),
         scratch_shapes=[
             pltpu.VMEM((4, width, half), f32),
             pltpu.SemaphoreType.DMA((4,)),
         ],
-        input_output_aliases={2 + i: i for i in range(len(given))},
+        input_output_aliases={4 + i: i for i in range(4)} if rest else {},
         compiler_params=pltpu.CompilerParams(vmem_limit_bytes=32 << 20),
-        name="widen_kernel",
-    )(side.reshape(1), part.reshape(4, width, half), *given)
+        name="finish_kernel" if rest else "widen_kernel",
+    )(side.reshape(1), part.reshape(4, width, half), *rest)
 
 
 def swap(value):
@@ -302,7 +317,7 @@
             jax.ShapeDtypeStruct((own, width), f32),
             jax.ShapeDtypeStruct((own, width), f32),
             jax.ShapeDtypeStruct((own, width), f32),
-            jax.ShapeDtypeStruct((SLOTS, 128), f32),
+            jax.ShapeDtypeStruct((own, width), f32),
             jax.ShapeDtypeStruct((payload, half), bf16),
             jax.ShapeDtypeStruct((payload, half), bf16),
         ),
@@ -347,7 +362,8 @@
     reduced = (
         (column.astype(f32) + turns[1].astype(f32)) + (turns[0].astype(f32) + turns[2].astype(f32))
     ).astype(bf16)
-    pooled = ((middle + from_inner + from_outer) / roots[own : 2 * own, :1]).astype(bf16)
+    middle = after(middle, column)
+    pooled = ((middle + from_inner + from_outer) / roots).astype(bf16)
     reduced = after(reduced, pooled)
     weights = lax.all_to_all(copied(reduced[:weight_chunk], MEMBERS), GROUP, 0, 0, tiled=True)
 
@@ -355,14 +371,9 @@
         reduced, weight_chunk + lax.axis_index("far") * GAUGE_ROWS, GAUGE_ROWS, 0
     )
     far_gauge = swap(after(own_gauge, weights))
-    grad_gauges = jnp.where(
-        core == 0,
-        jnp.concatenate([own_gauge, far_gauge], axis=1),
-        jnp.concatenate([far_gauge, own_gauge], axis=1),
-    )
     far = swap(weights)
-    grads = widen(core, weights, None)
-    grads = widen(1 - core, far, grads)
+    grads = widen(core, weights)
+    *grads, grad_gauges = widen(1 - core, far, own_gauge, far_gauge, *grads)
     return (pooled, grad_cells, grad_gauges, grads[0], grads[1], grads[2], grads[3])
 
 

time: 118 us -> 117 us (level)
  blocking collectives: 17.4 us -> 42 us
  waiting for transfers between devices: 36.7 us -> 16.4 us
  starting transfers between devices: 49.1 us -> 45.1 us
  other arithmetic: 3.42 us -> 1.55 us
    all_to_all x0 -> x1, blocking collectives: none -> 22.4 us  [per_device(): lax.all_to_all(chip, GROUP, 0, 0, tiled=True).reshape(MEMBERS, chunk, half)]
    all_to_all x1 -> x0, waiting for transfers between devices: 19.1 us -> none  [per_device(): lax.all_to_all(chip, GROUP, 0, 0, tiled=True).reshape(MEMBERS, chunk, half)]
    all_to_all x1 -> x0, starting transfers between devices: 4.15 us -> none  [per_device(): lax.all_to_all(chip, GROUP, 0, 0, tiled=True).reshape(MEMBERS, chunk, half)]
    all_to_all x1, blocking collectives: 17.4 us -> 19.5 us  [per_device(): lax.all_to_all(copied(reduced[:weight_chunk], MEMBERS), GROUP, 0, 0, tile...]
    ppermute x3, starting transfers between devices: 9.41 us -> 10.7 us  [per_device(): lax.ppermute(column, 'far', [(i, (i + s) % count) for i in range(count)])]
    convert_element_type x1, other arithmetic: 1.68 us -> 0.48 us  [per_device(): chip = (keep.astype(f32) + from_core.astype(f32)).astype(bf16)]
  transfers between devices with their start and end apart: 15 -> 14, of which waited for: 9 -> 8; matrix products, arithmetic and copies ran while one was open for 2% -> 1% of each run, Pallas kernels for 1% -> 1%
where the time goes in v10:
time: 117 us
  starting transfers between devices  45.1 us (39%)
  blocking collectives  42 us (36%)
  waiting for transfers between devices  16.4 us (14%)
  Pallas kernels  9.14 us (8%)
  local copies, waits for them, and re-layouts  1.8 us (2%)
  other arithmetic  1.55 us (1%)
    all_to_all x1, blocking collectives, per_device(): lax.all_to_all(chip, GROUP, 0, 0, tiled=True).reshape(MEMBERS, chunk, half)  22.4 us
    all_to_all x1, blocking collectives, per_device(): lax.all_to_all(copied(reduced[:weight_chunk], MEMBERS), GROUP, 0, 0, tile...  19.5 us
    all_to_all x1, starting transfers between devices, per_device(): mine = lax.all_to_all(copies, TILES, 0, 0, tiled=True)  16.3 us
    ppermute x4, starting transfers between devices, shifted(): lax.ppermute(value, EVERY, [(i, (i + steps) % count) for i in range(count)])  14 us
    ppermute x3, starting transfers between devices, per_device(): lax.ppermute(column, 'far', [(i, (i + s) % count) for i in range(count)])  10.7 us
    ppermute x4, waiting for transfers between devices, shifted(): lax.ppermute(value, EVERY, [(i, (i + steps) % count) for i in range(count)])  7.82 us
    pallas_call x1, Pallas kernels, per_device(): pl.pallas_call(group_kernel, out_shape=(jax.ShapeDtypeStruct(cells.shape,...  5.79 us
    ppermute x5, waiting for transfers between devices, swap(): return lax.ppermute(value, 'c', [(0, 1), (1, 0)])  5.41 us
  transfers between devices with their start and end apart: 14, of which 8 were waited for; matrix products, arithmetic and copies ran while one was open for 1% of the time, Pallas kernels for 1%

profile of v10, /device:TPU:1, one launch (start us, length us, event | category | flops | bytes accessed | tf_op | source)
XLA Modules:
  0.0 117.0 jit_solution(14227399603733440770)
XLA Ops:
  0.7 0.6 copy-done
  1.3 0.8 broadcast_in_dim.10
  2.2 16.3 %all-to-all-start = ((bf16[128,8,256]{2,1,0:T(8,128)(2,1)}), bf16[128,8,256]{2,1,0:T(8,128)(2,1)S(1)}, u32[]{:S(2)}, u32[]{:S(2)}) async-start(bf16[128,8,256]{2,1,0:T(8,128)(2,1)} %broadcast_in_dim.10), calls=%async_computation | async-start | bytes 1048576 | tf_op jit(solution)/shard_map/all_to_all | solution.py:284
  18.6 0.1 convert_reduce_fusion
  18.7 1.0 collective-permute-start.1
  19.8 0.8 collective-permute-start
  20.6 12.1 %collective-permute-start.3 = (bf16[1,128]{1,0:T(2,128)(2,1)S(1)}, bf16[1,128]{1,0:T(2,128)(2,1)S(1)}, u32[]{:S(2)}, u32[]{:S(2)}) collective-permute-start(bf16[1,128]{1,0:T(2,128)(2,1)S(1)} %slice.8), channel_id=1, source_target_pairs={{0,254},{1,255},{2,0},{3,1},{4,2},{5,3},{6,4},{7,5},{8,6},{9,7},{1... | collective-permute-start | bytes 776 | tf_op jit(solution)/shard_map/ppermute | solution.py:262
  32.7 0.7 collective-permute-done.3.above_two_ref
  33.5 7.1 %collective-permute-done.2.below_two_ref = bf16[1,128]{1,0:T(2,128)(2,1)S(1)} collective-permute-done((bf16[1,128]{1,0:T(2,128)(2,1)S(1)}, bf16[1,128]{1,0:T(2,128)(2,1)S(1)}, u32[]{:S(2)}, u32[]{:S(2)}) %collective-permute-start.2) | collective-permute-done | bytes 288 | tf_op jit(solution)/shard_map/ppermute | solution.py:262
  40.6 0.1 collective-permute-start.4
  40.9 0.1 add.166.rows_ref
  41.0 1.6 %collective-permute-done.4.other_ref = bf16[1024,256]{1,0:T(8,128)(2,1)S(1)} collective-permute-done((bf16[1024,256]{1,0:T(8,128)(2,1)S(1)}, bf16[1024,256]{1,0:T(8,128)(2,1)S(1)}, u32[]{:S(2)}, u32[]{:S(2)}) %collective-permute-start.4) | collective-permute-done | bytes 524320 | tf_op jit(solution)/shard_map/ppermute | solution.py:257
  42.6 5.8 %group_kernel.1 = (bf16[256,512]{1,0:T(8,128)(2,1)}, f32[2,512]{1,0:T(2,128)S(1)}, f32[2,512]{1,0:T(2,128)S(1)}, f32[2,512]{1,0:T(2,128)S(1)}, f32[2,512]{1,0:T(...) custom-call(s32[1]{0:T(128)} %bitcast.core_ref.side_ref, s32[1,128]{1,0:T(1,128)S(1)} %add.166.rows_ref, ...), custom_call_target="tpu_custom_call" | custom-call | tf_op jit(solution)/shard_map/group_kernel/pallas_call | solution.py:313
  48.4 0.2 collective-permute-start.5
  48.6 0.4 collective-permute-start.6
  49.0 2.9 %collective-permute-done.6 = f32[2,512]{1,0:T(2,128)S(1)} collective-permute-done((f32[2,512]{1,0:T(2,128)S(1)}, f32[2,512]{1,0:T(2,128)S(1)}, u32[]{:S(2)}, u32[]{:S(2)}) %collective-permute-start.6) | collective-permute-done | bytes 4128 | tf_op jit(solution)/shard_map/ppermute | solution.py:257
  51.9 0.1 collective-permute-done.7
  52.0 0.5 add_convert_fusion
  52.5 22.4 %all_to_all.27 = bf16[32,96,256]{2,1,0:T(8,128)(2,1)S(1)} all-to-all(bf16[32,96,256]{2,1,0:T(8,128)(2,1)S(1)} %bitcast.35), channel_id=1, replica_groups=mesh['y'=4,'far'=4,'near'=2,'x'=4,'c'=2] {'y','x','near'}, dimensions={0} | all-to-all | bytes 3145728 | tf_op jit(solution)/shard_map/all_to_all | solution.py:355
  74.9 0.2 reduce_sum.22
  75.1 7.1 %collective-permute-start.10 = (bf16[96,256]{1,0:T(8,128)(2,1)S(1)}, bf16[96,256]{1,0:T(8,128)(2,1)S(1)}, u32[]{:S(2)}, u32[]{:S(2)}) collective-permute-start(bf16[96,256]{1,0:T(8,128)(2,1)S(1)} %reduce_sum.22), channel_id=1, source_target_pairs={{0,48},{16,0},{32,16},{48,32},{1,49},{17,1},{33,17},{49,33},{2,50}... | collective-permute-start | bytes 147464 | tf_op jit(solution)/shard_map/ppermute | solution.py:359
  82.2 0.4 collective-permute-start.9
  82.7 3.2 %collective-permute-start.8 = (bf16[96,256]{1,0:T(8,128)(2,1)S(1)}, bf16[96,256]{1,0:T(8,128)(2,1)S(1)}, u32[]{:S(2)}, u32[]{:S(2)}) collective-permute-start(bf16[96,256]{1,0:T(8,128)(2,1)S(1)} %reduce_sum.22), channel_id=1, source_target_pairs={{0,32},{16,48},{32,0},{48,16},{1,33},{17,49},{33,1},{49,17},{2,34}... | collective-permute-start | bytes 147464 | tf_op jit(solution)/shard_map/ppermute | solution.py:359
  85.9 0.6 fusion
  86.5 1.0 collective-permute-done.9
  87.4 2.1 %collective-permute-done.8 = bf16[96,256]{1,0:T(8,128)(2,1)S(1)} collective-permute-done((bf16[96,256]{1,0:T(8,128)(2,1)S(1)}, bf16[96,256]{1,0:T(8,128)(2,1)S(1)}, u32[]{:S(2)}, u32[]{:S(2)}) %collective-permute-start.8) | collective-permute-done | bytes 49184 | tf_op jit(solution)/shard_map/ppermute | solution.py:359
  89.5 0.1 broadcast_in_dim.11
  89.7 19.5 %all_to_all.28 = bf16[32,64,256]{2,1,0:T(8,128)(2,1)S(1)} all-to-all(bf16[32,64,256]{2,1,0:T(8,128)(2,1)S(1)} %broadcast_in_dim.11), channel_id=1, replica_groups=mesh['y'=4,'far'=4,'near'=2,'x'=4,'c'=2] {'y','x','near'}, dimensions={0} | all-to-all | bytes 2097152 | tf_op jit(solution)/shard_map/all_to_all | solution.py:368
  109.2 3.3 %collective-permute-start.11 = (bf16[2048,256]{1,0:T(8,128)(2,1)S(1)}, bf16[2048,256]{1,0:T(8,128)(2,1)S(1)}, u32[]{:S(2)}, u32[]{:S(2)}) collective-permute-start(bf16[2048,256]{1,0:T(8,128)(2,1)S(1)} %bitcast.29), channel_id=1, source_target_pairs={{0,1},{1,0},{2,3},{3,2},{4,5},{5,4},{6,7},{7,6},{8,9},{9,8},{10,11... | collective-permute-start | bytes 3145736 | tf_op jit(solution)/shard_map/ppermute | solution.py:257
  112.5 1.4 %widen_kernel.1 = (f32[512,512]{1,0:T(8,128)}, f32[512,512]{1,0:T(8,128)}, f32[512,512]{1,0:T(8,128)}, f32[512,512]{1,0:T(8,128)}) custom-call(s32[1]{0:T(128)} %bitcast.core_ref.side_ref, bf16[4,512,256]{2,1,0:T(8,128)(2,1)S(1)} %bitcast.30), custom_call_target="tpu_custom_call" | custom-call | tf_op jit(solution)/shard_map/widen_kernel/pallas_call | solution.py:241
  113.9 0.9 collective-permute-done.12.far_ref
  114.8 2.0 %finish_kernel.1 = (f32[512,512]{1,0:T(8,128)}, f32[512,512]{1,0:T(8,128)}, f32[512,512]{1,0:T(8,128)}, f32[512,512]{1,0:T(8,128)}, bf16[8,512]{1,0:T(8,128)(2,1)}) custom-call(s32[1]{0:T(128)} %bitcast.5.side_ref, bf16[4,512,256]{2,1,0:T(8,128)(2,1)S(1)} %bitcast.33, ...), custom_call_target="tpu_custom_call", output_to_operand_aliasing={{0}: (4, {}), {1}: (5, {}), {2}: (6, {}), {3}: (7, {})} | custom-call | tf_op jit(solution)/shard_map/finish_kernel/pallas_call | solution.py:241
  (34 shorter events, 0.3 us)
Async XLA Ops:
  0.6 0.7 copy-start
  0.7 17.9 %copy-start.5 = (s32[256]{0:T(256)S(1)}, s32[256]{0:T(256)}, u32[]{:S(2)}) copy-start(s32[256]{0:T(256)} %param.16) | copy-start | bytes 3076
  0.7 18.0 %copy-start.4 = (bf16[2,512]{1,0:T(2,128)(2,1)S(1)}, bf16[2,512]{1,0:T(2,128)(2,1)}, u32[]{:S(2)}) copy-start(bf16[2,512]{1,0:T(2,128)(2,1)} %param.17) | copy-start | bytes 6148
  0.7 40.0 %copy-start.6 = (s32[1,16]{1,0:T(1,128)S(1)}, s32[1,16]{1,0:T(1,128)}, u32[]{:S(2)}) copy-start(s32[1,16]{1,0:T(1,128)} %param.15) | copy-start | bytes 196
  0.7 41.9 %copy-start.2 = (bf16[512,512]{1,0:T(8,128)(2,1)S(1)}, bf16[512,512]{1,0:T(8,128)(2,1)}, u32[]{:S(2)}) copy-start(bf16[512,512]{1,0:T(8,128)(2,1)} %wv_ref.1) | copy-start | bytes 1572868
  0.7 41.9 %copy-start.1 = (bf16[512,512]{1,0:T(8,128)(2,1)S(1)}, bf16[512,512]{1,0:T(8,128)(2,1)}, u32[]{:S(2)}) copy-start(bf16[512,512]{1,0:T(8,128)(2,1)} %wk_ref.1) | copy-start | bytes 1572868
  0.7 41.9 %copy-start.3 = (bf16[512,512]{1,0:T(8,128)(2,1)S(1)}, bf16[512,512]{1,0:T(8,128)(2,1)}, u32[]{:S(2)}) copy-start(bf16[512,512]{1,0:T(8,128)(2,1)} %wq_ref.1) | copy-start | bytes 1572868
  2.2 38.4 %all-to-all-start = ((bf16[128,8,256]{2,1,0:T(8,128)(2,1)}), bf16[128,8,256]{2,1,0:T(8,128)(2,1)S(1)}, u32[]{:S(2)}, u32[]{:S(2)}) async-start(bf16[128,8,256]{2,1,0:T(8,128)(2,1)} %broadcast_in_dim.10), calls=%async_computation | async-start | bytes 1048576 | tf_op jit(solution)/shard_map/all_to_all | solution.py:284
  18.7 21.8 %collective-permute-start.1 = (bf16[3,512]{1,0:T(4,128)(2,1)S(1)}, bf16[3,512]{1,0:T(4,128)(2,1)S(1)}, u32[]{:S(2)}, u32[]{:S(2)}) collective-permute-start(bf16[3,512]{1,0:T(4,128)(2,1)S(1)} %pad_maximum_fusion.own_ref), channel_id=1, source_target_pairs={{0,255},{1,0},{2,1},{3,2},{4,3},{5,4},{6,5},{7,6},{8,7},{9,8},{10,... | collective-permute-start | bytes 9224 | tf_op jit(solution)/shard_map/ppermute | solution.py:262
  19.8 20.8 %collective-permute-start = (bf16[3,512]{1,0:T(4,128)(2,1)S(1)}, bf16[3,512]{1,0:T(4,128)(2,1)S(1)}, u32[]{:S(2)}, u32[]{:S(2)}) collective-permute-start(bf16[3,512]{1,0:T(4,128)(2,1)S(1)} %pad_maximum_fusion.own_ref), channel_id=1, source_target_pairs={{0,1},{1,2},{2,3},{3,4},{4,5},{5,6},{6,7},{7,8},{8,9},{9,10},{10,1... | collective-permute-start | bytes 9224 | tf_op jit(solution)/shard_map/ppermute | solution.py:262
  20.6 12.9 %collective-permute-start.3 = (bf16[1,128]{1,0:T(2,128)(2,1)S(1)}, bf16[1,128]{1,0:T(2,128)(2,1)S(1)}, u32[]{:S(2)}, u32[]{:S(2)}) collective-permute-start(bf16[1,128]{1,0:T(2,128)(2,1)S(1)} %slice.8), channel_id=1, source_target_pairs={{0,254},{1,255},{2,0},{3,1},{4,2},{5,3},{6,4},{7,5},{8,6},{9,7},{1... | collective-permute-start | bytes 776 | tf_op jit(solution)/shard_map/ppermute | solution.py:262
  32.7 7.8 %collective-permute-start.2 = (bf16[1,128]{1,0:T(2,128)(2,1)S(1)}, bf16[1,128]{1,0:T(2,128)(2,1)S(1)}, u32[]{:S(2)}, u32[]{:S(2)}) collective-permute-start(bf16[1,128]{1,0:T(2,128)(2,1)S(1)} %slice.8), channel_id=1, source_target_pairs={{0,2},{1,3},{2,4},{3,5},{4,6},{5,7},{6,8},{7,9},{8,10},{9,11},{10,... | collective-permute-start | bytes 776 | tf_op jit(solution)/shard_map/ppermute | solution.py:262
  40.6 2.0 %collective-permute-start.4 = (bf16[1024,256]{1,0:T(8,128)(2,1)S(1)}, bf16[1024,256]{1,0:T(8,128)(2,1)S(1)}, u32[]{:S(2)}, u32[]{:S(2)}) collective-permute-start(bf16[1024,256]{1,0:T(8,128)(2,1)S(1)} %bitcast.31), channel_id=1, source_target_pairs={{0,1},{1,0},{2,3},{3,2},{4,5},{5,4},{6,7},{7,6},{8,9},{9,8},{10,11... | collective-permute-start | bytes 1572872 | tf_op jit(solution)/shard_map/ppermute | solution.py:257
  48.4 3.6 %collective-permute-start.5 = (bf16[3072,256]{1,0:T(8,128)(2,1)S(1)}, bf16[3072,256]{1,0:T(8,128)(2,1)S(1)}, u32[]{:S(2)}, u32[]{:S(2)}) collective-permute-start(bf16[3072,256]{1,0:T(8,128)(2,1)S(1)} %get-tuple-element.31), channel_id=1, source_target_pairs={{0,1},{1,0},{2,3},{3,2},{4,5},{5,4},{6,7},{7,6},{8,9},{9,8},{10,11... | collective-permute-start | bytes 4718600 | tf_op jit(solution)/shard_map/ppermute | solution.py:257
  48.6 3.3 %collective-permute-start.6 = (f32[2,512]{1,0:T(2,128)S(1)}, f32[2,512]{1,0:T(2,128)S(1)}, u32[]{:S(2)}, u32[]{:S(2)}) collective-permute-start(f32[2,512]{1,0:T(2,128)S(1)} %get-tuple-element.32), channel_id=1, source_target_pairs={{0,1},{1,0},{2,3},{3,2},{4,5},{5,4},{6,7},{7,6},{8,9},{9,8},{10,11... | collective-permute-start | bytes 12296 | tf_op jit(solution)/shard_map/ppermute | solution.py:257
  49.0 3.0 %collective-permute-start.7 = (f32[2,512]{1,0:T(2,128)S(1)}, f32[2,512]{1,0:T(2,128)S(1)}, u32[]{:S(2)}, u32[]{:S(2)}) collective-permute-start(f32[2,512]{1,0:T(2,128)S(1)} %get-tuple-element.33), channel_id=1, source_target_pairs={{0,255},{1,2},{2,1},{3,4},{4,3},{5,6},{6,5},{7,8},{8,7},{9,10},{10... | collective-permute-start | bytes 12296 | tf_op jit(solution)/shard_map/ppermute | solution.py:345
  75.1 11.3 %collective-permute-start.10 = (bf16[96,256]{1,0:T(8,128)(2,1)S(1)}, bf16[96,256]{1,0:T(8,128)(2,1)S(1)}, u32[]{:S(2)}, u32[]{:S(2)}) collective-permute-start(bf16[96,256]{1,0:T(8,128)(2,1)S(1)} %reduce_sum.22), channel_id=1, source_target_pairs={{0,48},{16,0},{32,16},{48,32},{1,49},{17,1},{33,17},{49,33},{2,50}... | collective-permute-start | bytes 147464 | tf_op jit(solution)/shard_map/ppermute | solution.py:359
  82.2 5.2 %collective-permute-start.9 = (bf16[96,256]{1,0:T(8,128)(2,1)S(1)}, bf16[96,256]{1,0:T(8,128)(2,1)S(1)}, u32[]{:S(2)}, u32[]{:S(2)}) collective-permute-start(bf16[96,256]{1,0:T(8,128)(2,1)S(1)} %reduce_sum.22), channel_id=1, source_target_pairs={{0,16},{16,32},{32,48},{48,0},{1,17},{17,33},{33,49},{49,1},{2,18}... | collective-permute-start | bytes 147464 | tf_op jit(solution)/shard_map/ppermute | solution.py:359
  82.7 6.8 %collective-permute-start.8 = (bf16[96,256]{1,0:T(8,128)(2,1)S(1)}, bf16[96,256]{1,0:T(8,128)(2,1)S(1)}, u32[]{:S(2)}, u32[]{:S(2)}) collective-permute-start(bf16[96,256]{1,0:T(8,128)(2,1)S(1)} %reduce_sum.22), channel_id=1, source_target_pairs={{0,32},{16,48},{32,0},{48,16},{1,33},{17,49},{33,1},{49,17},{2,34}... | collective-permute-start | bytes 147464 | tf_op jit(solution)/shard_map/ppermute | solution.py:359
  109.2 5.6 %collective-permute-start.11 = (bf16[2048,256]{1,0:T(8,128)(2,1)S(1)}, bf16[2048,256]{1,0:T(8,128)(2,1)S(1)}, u32[]{:S(2)}, u32[]{:S(2)}) collective-permute-start(bf16[2048,256]{1,0:T(8,128)(2,1)S(1)} %bitcast.29), channel_id=1, source_target_pairs={{0,1},{1,0},{2,3},{3,2},{4,5},{5,4},{6,7},{7,6},{8,9},{9,8},{10,11... | collective-permute-start | bytes 3145736 | tf_op jit(solution)/shard_map/ppermute | solution.py:257
  112.5 2.3 %collective-permute-start.12 = (bf16[8,256]{1,0:T(8,128)(2,1)S(1)}, bf16[8,256]{1,0:T(8,128)(2,1)S(1)}, u32[]{:S(2)}, u32[]{:S(2)}) collective-permute-start(bf16[8,256]{1,0:T(8,128)(2,1)S(1)} %constant_dynamic-slice_fusion.own_ref), channel_id=1, source_target_pairs={{0,1},{1,0},{2,3},{3,2},{4,5},{5,4},{6,7},{7,6},{8,9},{9,8},{10,11... | collective-permute-start | bytes 12296 | tf_op jit(solution)/shard_map/ppermute | solution.py:257

commit v11 on v8

--- a/solution.py
+++ b/solution.py
@@ -335,7 +335,15 @@
         lax.ppermute(column, "far", [(i, (i + s) % count) for i in range(count)])
         for s in range(1, count)
     ]
-    inner, outer = lax.optimization_barrier((inner, outer, column))[:2]
+    reduced = (
+        (column.astype(f32) + turns[1].astype(f32)) + (turns[0].astype(f32) + turns[2].astype(f32))
+    ).astype(bf16)
+    copies = copied(reduced[:weight_chunk], MEMBERS)
+    weights = lax.all_to_all(copies, GROUP, 0, 0, tiled=True)
+    own_gauge = lax.dynamic_slice_in_dim(
+        reduced, weight_chunk + lax.axis_index("far") * GAUGE_ROWS, GAUGE_ROWS, 0
+    )
+    inner, outer, late_gauge = lax.optimization_barrier((inner, outer, own_gauge, copies))[:3]
     from_inner = swap(inner)
     total_devices = lax.axis_size(EVERY)
     from_outer = lax.ppermute(
@@ -343,22 +351,14 @@
         EVERY,
         [(i, (i + (1 if i % 2 else -1)) % total_devices) for i in range(total_devices)],
     )
-    reduced = (
-        (column.astype(f32) + turns[1].astype(f32)) + (turns[0].astype(f32) + turns[2].astype(f32))
-    ).astype(bf16)
-    reduced = after(reduced, from_inner, from_outer)
-    weights = lax.all_to_all(copied(reduced[:weight_chunk], MEMBERS), GROUP, 0, 0, tiled=True)
-
+    far_gauge = swap(late_gauge)
     pooled = ((middle + from_inner + from_outer) / roots[own : 2 * own, :1]).astype(bf16)
-    own_gauge = lax.dynamic_slice_in_dim(
-        reduced, weight_chunk + lax.axis_index("far") * GAUGE_ROWS, GAUGE_ROWS, 0
-    )
-    far_gauge = swap(after(own_gauge, weights))
     grad_gauges = jnp.where(
         core == 0,
         jnp.concatenate([own_gauge, far_gauge], axis=1),
         jnp.concatenate([far_gauge, own_gauge], axis=1),
     )
+    weights = after(weights, pooled, grad_gauges)
     far = swap(weights)
     grads = widen(core, weights, None)
     grads = widen(1 - core, far, grads)

time: 116 us -> 116 us (level)
  blocking collectives: 44.7 us -> 26.2 us
  waiting for transfers between devices: 17.2 us -> 28.7 us
  starting transfers between devices: 39.8 us -> 46.5 us
    all_to_all x1 -> x0, blocking collectives: 18.5 us -> none  [per_device(): lax.all_to_all(copied(reduced[:weight_chunk], MEMBERS), GROUP, 0, 0, tile...]
    ppermute x1, waiting for transfers between devices: 0.01 us -> 6.36 us  [per_device(): lax.ppermute(outer, EVERY, [(i, (i + (1 if i % 2 else -1)) % total_device...]
    all_to_all x0 -> x1, starting transfers between devices: none -> 3.93 us  [per_device(): weights = lax.all_to_all(copies, GROUP, 0, 0, tiled=True)]
    ppermute x3, waiting for transfers between devices: 4.43 us -> 6.82 us  [per_device(): lax.ppermute(column, 'far', [(i, (i + s) % count) for i in range(count)])]
    all_to_all x0 -> x1, waiting for transfers between devices: none -> 1.88 us  [per_device(): weights = lax.all_to_all(copies, GROUP, 0, 0, tiled=True)]
    ppermute x1, starting transfers between devices: 0.23 us -> 1.89 us  [per_device(): lax.ppermute(outer, EVERY, [(i, (i + (1 if i % 2 else -1)) % total_device...]
  transfers between devices with their start and end apart: 14 -> 15, of which waited for: 6 -> 10; matrix products, arithmetic and copies ran while one was open for 2% -> 2% of each run, Pallas kernels for 1% -> 1%
where the time goes in v11:
time: 116 us
  starting transfers between devices  46.5 us (40%)
  waiting for transfers between devices  28.7 us (25%)
  blocking collectives  26.2 us (23%)
  Pallas kernels  8.54 us (7%)
  local copies, waits for them, and re-layouts  2.9 us (2%)
  other arithmetic  2.17 us (2%)
    all_to_all x1, blocking collectives, per_device(): lax.all_to_all(chip, GROUP, 0, 0, tiled=True).reshape(MEMBERS, chunk, half)  26.2 us
    all_to_all x1, starting transfers between devices, per_device(): mine = lax.all_to_all(copies, TILES, 0, 0, tiled=True)  16.3 us
    ppermute x4, starting transfers between devices, shifted(): lax.ppermute(value, EVERY, [(i, (i + steps) % count) for i in range(count)])  14 us
    ppermute x4, waiting for transfers between devices, shifted(): lax.ppermute(value, EVERY, [(i, (i + steps) % count) for i in range(count)])  7.82 us
    ppermute x5, starting transfers between devices, swap(): return lax.ppermute(value, 'c', [(0, 1), (1, 0)])  7.65 us
    ppermute x3, waiting for transfers between devices, per_device(): lax.ppermute(column, 'far', [(i, (i + s) % count) for i in range(count)])  6.82 us
    ppermute x1, waiting for transfers between devices, per_device(): lax.ppermute(outer, EVERY, [(i, (i + (1 if i % 2 else -1)) % total_device...  6.36 us
    ppermute x5, waiting for transfers between devices, swap(): return lax.ppermute(value, 'c', [(0, 1), (1, 0)])  5.8 us
  transfers between devices with their start and end apart: 15, of which 10 were waited for; matrix products, arithmetic and copies ran while one was open for 2% of the time, Pallas kernels for 1%

profile of v11, /device:TPU:1, one launch (start us, length us, event | category | flops | bytes accessed | tf_op | source)
XLA Modules:
  0.0 115.9 jit_solution(9174726273695128988)
XLA Ops:
  0.7 0.6 copy-done
  1.3 0.8 broadcast_in_dim.10
  2.2 16.3 %all-to-all-start = ((bf16[128,8,256]{2,1,0:T(8,128)(2,1)}), bf16[128,8,256]{2,1,0:T(8,128)(2,1)S(1)}, u32[]{:S(2)}, u32[]{:S(2)}) async-start(bf16[128,8,256]{2,1,0:T(8,128)(2,1)} %broadcast_in_dim.10), calls=%async_computation | async-start | bytes 1048576 | tf_op jit(solution)/shard_map/all_to_all | solution.py:269
  18.7 1.0 collective-permute-start.1
  19.8 0.8 collective-permute-start
  20.6 12.1 %collective-permute-start.3 = (bf16[1,128]{1,0:T(2,128)(2,1)S(1)}, bf16[1,128]{1,0:T(2,128)(2,1)S(1)}, u32[]{:S(2)}, u32[]{:S(2)}) collective-permute-start(bf16[1,128]{1,0:T(2,128)(2,1)S(1)} %slice.12), channel_id=1, source_target_pairs={{0,254},{1,255},{2,0},{3,1},{4,2},{5,3},{6,4},{7,5},{8,6},{9,7},{1... | collective-permute-start | bytes 776 | tf_op jit(solution)/shard_map/ppermute | solution.py:247
  32.7 0.7 collective-permute-done.3.above_two_ref
  33.5 7.1 %collective-permute-done.2.below_two_ref = bf16[1,128]{1,0:T(2,128)(2,1)S(1)} collective-permute-done((bf16[1,128]{1,0:T(2,128)(2,1)S(1)}, bf16[1,128]{1,0:T(2,128)(2,1)S(1)}, u32[]{:S(2)}, u32[]{:S(2)}) %collective-permute-start.2) | collective-permute-done | bytes 288 | tf_op jit(solution)/shard_map/ppermute | solution.py:247
  41.0 1.6 %collective-permute-done.4.other_ref = bf16[1024,256]{1,0:T(8,128)(2,1)S(1)} collective-permute-done((bf16[1024,256]{1,0:T(8,128)(2,1)S(1)}, bf16[1024,256]{1,0:T(8,128)(2,1)S(1)}, u32[]{:S(2)}, u32[]{:S(2)}) %collective-permute-start.4) | collective-permute-done | bytes 524320 | tf_op jit(solution)/shard_map/ppermute | solution.py:242
  42.6 5.8 %group_kernel.1 = (bf16[256,512]{1,0:T(8,128)(2,1)}, f32[2,512]{1,0:T(2,128)S(1)}, f32[2,512]{1,0:T(2,128)S(1)}, f32[2,512]{1,0:T(2,128)S(1)}, f32[16,128]{1,0:T...) custom-call(s32[1]{0:T(128)} %bitcast.core_ref.side_ref, s32[1,128]{1,0:T(1,128)S(1)} %add.166.rows_ref, ...), custom_call_target="tpu_custom_call" | custom-call | tf_op jit(solution)/shard_map/group_kernel/pallas_call | solution.py:298
  48.4 0.2 collective-permute-start.5
  48.6 3.3 %collective-permute-done.5 = bf16[3072,256]{1,0:T(8,128)(2,1)S(1)} collective-permute-done((bf16[3072,256]{1,0:T(8,128)(2,1)S(1)}, bf16[3072,256]{1,0:T(8,128)(2,1)S(1)}, u32[]{:S(2)}, u32[]{:S(2)}) %collective-permute-start.5) | collective-permute-done | bytes 1572896 | tf_op jit(solution)/shard_map/ppermute | solution.py:242
  51.9 0.4 add_convert_fusion
  52.3 26.2 %all_to_all.27 = bf16[32,96,256]{2,1,0:T(8,128)(2,1)S(1)} all-to-all(bf16[32,96,256]{2,1,0:T(8,128)(2,1)S(1)} %bitcast.35), channel_id=1, replica_groups=mesh['y'=4,'far'=4,'near'=2,'x'=4,'c'=2] {'y','x','near'}, dimensions={0} | all-to-all | bytes 3145728 | tf_op jit(solution)/shard_map/all_to_all | solution.py:331
  78.5 0.2 reduce_sum.22
  78.7 0.3 collective-permute-start.8
  79.0 2.4 %collective-permute-start.7 = (bf16[96,256]{1,0:T(8,128)(2,1)S(1)}, bf16[96,256]{1,0:T(8,128)(2,1)S(1)}, u32[]{:S(2)}, u32[]{:S(2)}) collective-permute-start(bf16[96,256]{1,0:T(8,128)(2,1)S(1)} %reduce_sum.22), channel_id=1, source_target_pairs={{0,16},{16,32},{32,48},{48,0},{1,17},{17,33},{33,49},{49,1},{2,18}... | collective-permute-start | bytes 147464 | tf_op jit(solution)/shard_map/ppermute | solution.py:335
  81.3 2.0 %collective-permute-done.8 = bf16[96,256]{1,0:T(8,128)(2,1)S(1)} collective-permute-done((bf16[96,256]{1,0:T(8,128)(2,1)S(1)}, bf16[96,256]{1,0:T(8,128)(2,1)S(1)}, u32[]{:S(2)}, u32[]{:S(2)}) %collective-permute-start.8) | collective-permute-done | bytes 49184 | tf_op jit(solution)/shard_map/ppermute | solution.py:335
  83.3 1.2 %collective-permute-done.7 = bf16[96,256]{1,0:T(8,128)(2,1)S(1)} collective-permute-done((bf16[96,256]{1,0:T(8,128)(2,1)S(1)}, bf16[96,256]{1,0:T(8,128)(2,1)S(1)}, u32[]{:S(2)}, u32[]{:S(2)}) %collective-permute-start.7) | collective-permute-done | bytes 49184 | tf_op jit(solution)/shard_map/ppermute | solution.py:335
  84.5 3.7 %collective-permute-done.6 = bf16[96,256]{1,0:T(8,128)(2,1)S(1)} collective-permute-done((bf16[96,256]{1,0:T(8,128)(2,1)S(1)}, bf16[96,256]{1,0:T(8,128)(2,1)S(1)}, u32[]{:S(2)}, u32[]{:S(2)}) %collective-permute-start.6) | collective-permute-done | bytes 49184 | tf_op jit(solution)/shard_map/ppermute | solution.py:335
  88.2 1.1 broadcast_in_dim.11
  89.3 3.9 %all-to-all-start.2 = ((bf16[32,64,256]{2,1,0:T(8,128)(2,1)}), bf16[32,64,256]{2,1,0:T(8,128)(2,1)S(1)}, u32[]{:S(2)}, u32[]{:S(2)}) async-start(bf16[32,64,256]{2,1,0:T(8,128)(2,1)} %broadcast_in_dim.11), calls=%async_computation.2 | async-start | bytes 2097152 | tf_op jit(solution)/shard_map/all_to_all | solution.py:342
  93.2 3.2 %collective-permute-start.11 = (bf16[8,256]{1,0:T(8,128)(2,1)S(1)}, bf16[8,256]{1,0:T(8,128)(2,1)S(1)}, u32[]{:S(2)}, u32[]{:S(2)}) collective-permute-start(bf16[8,256]{1,0:T(8,128)(2,1)S(1)} %constant_dynamic-slice_fusion), channel_id=1, source_target_pairs={{0,1},{1,0},{2,3},{3,2},{4,5},{5,4},{6,7},{7,6},{8,9},{9,8},{10,11... | collective-permute-start | bytes 12296 | tf_op jit(solution)/shard_map/ppermute | solution.py:242
  96.7 1.9 %collective-permute-start.10 = (f32[2,512]{1,0:T(2,128)S(1)}, f32[2,512]{1,0:T(2,128)S(1)}, u32[]{:S(2)}, u32[]{:S(2)}) collective-permute-start(f32[2,512]{1,0:T(2,128)S(1)} %get-tuple-element.34), channel_id=1, source_target_pairs={{0,255},{1,2},{2,1},{3,4},{4,3},{5,6},{6,5},{7,8},{8,7},{9,10},{10... | collective-permute-start | bytes 12296 | tf_op jit(solution)/shard_map/ppermute | solution.py:349
  98.6 0.6 maximum_select_fusion
  99.2 6.4 %collective-permute-done.10 = f32[2,512]{1,0:T(2,128)S(1)} collective-permute-done((f32[2,512]{1,0:T(2,128)S(1)}, f32[2,512]{1,0:T(2,128)S(1)}, u32[]{:S(2)}, u32[]{:S(2)}) %collective-permute-start.10) | collective-permute-done | bytes 4128 | tf_op jit(solution)/shard_map/ppermute | solution.py:349
  105.6 0.7 fusion
  106.2 1.9 %all-to-all-done.2 = bf16[32,64,256]{2,1,0:T(8,128)(2,1)S(1)} async-done(((bf16[32,64,256]{2,1,0:T(8,128)(2,1)}), bf16[32,64,256]{2,1,0:T(8,128)(2,1)S(1)}, u32[]{:S(2)}, u32[]{:S(2)}) %all-to-all-start.2) | async-done | bytes 1048608 | tf_op jit(solution)/shard_map/all_to_all | solution.py:342
  108.1 4.0 %collective-permute-start.12 = (bf16[2048,256]{1,0:T(8,128)(2,1)S(1)}, bf16[2048,256]{1,0:T(8,128)(2,1)S(1)}, u32[]{:S(2)}, u32[]{:S(2)}) collective-permute-start(bf16[2048,256]{1,0:T(8,128)(2,1)S(1)} %bitcast.29), channel_id=1, source_target_pairs={{0,1},{1,0},{2,3},{3,2},{4,5},{5,4},{6,7},{7,6},{8,9},{9,8},{10,11... | collective-permute-start | bytes 3145736 | tf_op jit(solution)/shard_map/ppermute | solution.py:242
  112.1 1.4 %widen_kernel.2 = (f32[512,512]{1,0:T(8,128)}, f32[512,512]{1,0:T(8,128)}, f32[512,512]{1,0:T(8,128)}, f32[512,512]{1,0:T(8,128)}) custom-call(s32[1]{0:T(128)} %bitcast.core_ref.side_ref, bf16[4,512,256]{2,1,0:T(8,128)(2,1)S(1)} %bitcast.30), custom_call_target="tpu_custom_call" | custom-call | tf_op jit(solution)/shard_map/widen_kernel/pallas_call | solution.py:222
  113.5 0.9 collective-permute-done.12
  114.4 1.4 %widen_kernel.3 = (f32[512,512]{1,0:T(8,128)}, f32[512,512]{1,0:T(8,128)}, f32[512,512]{1,0:T(8,128)}, f32[512,512]{1,0:T(8,128)}) custom-call(s32[1]{0:T(128)} %bitcast.5.side_ref, bf16[4,512,256]{2,1,0:T(8,128)(2,1)S(1)} %bitcast.33, ...), custom_call_target="tpu_custom_call", output_to_operand_aliasing={{0}: (2, {}), {1}: (3, {}), {2}: (4, {}), {3}: (5, {})} | custom-call | tf_op jit(solution)/shard_map/widen_kernel/pallas_call | solution.py:222
  (37 shorter events, 0.9 us)
Async XLA Ops:
  0.6 0.7 copy-start
  0.7 17.9 %copy-start.5 = (s32[256]{0:T(256)S(1)}, s32[256]{0:T(256)}, u32[]{:S(2)}) copy-start(s32[256]{0:T(256)} %param.16) | copy-start | bytes 3076
  0.7 18.0 %copy-start.4 = (bf16[2,512]{1,0:T(2,128)(2,1)S(1)}, bf16[2,512]{1,0:T(2,128)(2,1)}, u32[]{:S(2)}) copy-start(bf16[2,512]{1,0:T(2,128)(2,1)} %param.17) | copy-start | bytes 6148
  0.7 40.0 %copy-start.6 = (s32[1,16]{1,0:T(1,128)S(1)}, s32[1,16]{1,0:T(1,128)}, u32[]{:S(2)}) copy-start(s32[1,16]{1,0:T(1,128)} %param.15) | copy-start | bytes 196
  0.7 41.9 %copy-start.2 = (bf16[512,512]{1,0:T(8,128)(2,1)S(1)}, bf16[512,512]{1,0:T(8,128)(2,1)}, u32[]{:S(2)}) copy-start(bf16[512,512]{1,0:T(8,128)(2,1)} %wv_ref.1) | copy-start | bytes 1572868
  0.7 41.9 %copy-start.1 = (bf16[512,512]{1,0:T(8,128)(2,1)S(1)}, bf16[512,512]{1,0:T(8,128)(2,1)}, u32[]{:S(2)}) copy-start(bf16[512,512]{1,0:T(8,128)(2,1)} %wk_ref.1) | copy-start | bytes 1572868
  0.7 41.9 %copy-start.3 = (bf16[512,512]{1,0:T(8,128)(2,1)S(1)}, bf16[512,512]{1,0:T(8,128)(2,1)}, u32[]{:S(2)}) copy-start(bf16[512,512]{1,0:T(8,128)(2,1)} %wq_ref.1) | copy-start | bytes 1572868
  2.2 38.4 %all-to-all-start = ((bf16[128,8,256]{2,1,0:T(8,128)(2,1)}), bf16[128,8,256]{2,1,0:T(8,128)(2,1)S(1)}, u32[]{:S(2)}, u32[]{:S(2)}) async-start(bf16[128,8,256]{2,1,0:T(8,128)(2,1)} %broadcast_in_dim.10), calls=%async_computation | async-start | bytes 1048576 | tf_op jit(solution)/shard_map/all_to_all | solution.py:269
  18.7 21.8 %collective-permute-start.1 = (bf16[3,512]{1,0:T(4,128)(2,1)S(1)}, bf16[3,512]{1,0:T(4,128)(2,1)S(1)}, u32[]{:S(2)}, u32[]{:S(2)}) collective-permute-start(bf16[3,512]{1,0:T(4,128)(2,1)S(1)} %pad_maximum_fusion.own_ref), channel_id=1, source_target_pairs={{0,255},{1,0},{2,1},{3,2},{4,3},{5,4},{6,5},{7,6},{8,7},{9,8},{10,... | collective-permute-start | bytes 9224 | tf_op jit(solution)/shard_map/ppermute | solution.py:247
  19.8 20.8 %collective-permute-start = (bf16[3,512]{1,0:T(4,128)(2,1)S(1)}, bf16[3,512]{1,0:T(4,128)(2,1)S(1)}, u32[]{:S(2)}, u32[]{:S(2)}) collective-permute-start(bf16[3,512]{1,0:T(4,128)(2,1)S(1)} %pad_maximum_fusion.own_ref), channel_id=1, source_target_pairs={{0,1},{1,2},{2,3},{3,4},{4,5},{5,6},{6,7},{7,8},{8,9},{9,10},{10,1... | collective-permute-start | bytes 9224 | tf_op jit(solution)/shard_map/ppermute | solution.py:247
  20.6 12.9 %collective-permute-start.3 = (bf16[1,128]{1,0:T(2,128)(2,1)S(1)}, bf16[1,128]{1,0:T(2,128)(2,1)S(1)}, u32[]{:S(2)}, u32[]{:S(2)}) collective-permute-start(bf16[1,128]{1,0:T(2,128)(2,1)S(1)} %slice.12), channel_id=1, source_target_pairs={{0,254},{1,255},{2,0},{3,1},{4,2},{5,3},{6,4},{7,5},{8,6},{9,7},{1... | collective-permute-start | bytes 776 | tf_op jit(solution)/shard_map/ppermute | solution.py:247
  32.7 7.8 %collective-permute-start.2 = (bf16[1,128]{1,0:T(2,128)(2,1)S(1)}, bf16[1,128]{1,0:T(2,128)(2,1)S(1)}, u32[]{:S(2)}, u32[]{:S(2)}) collective-permute-start(bf16[1,128]{1,0:T(2,128)(2,1)S(1)} %slice.12), channel_id=1, source_target_pairs={{0,2},{1,3},{2,4},{3,5},{4,6},{5,7},{6,8},{7,9},{8,10},{9,11},{10,... | collective-permute-start | bytes 776 | tf_op jit(solution)/shard_map/ppermute | solution.py:247
  40.6 2.0 %collective-permute-start.4 = (bf16[1024,256]{1,0:T(8,128)(2,1)S(1)}, bf16[1024,256]{1,0:T(8,128)(2,1)S(1)}, u32[]{:S(2)}, u32[]{:S(2)}) collective-permute-start(bf16[1024,256]{1,0:T(8,128)(2,1)S(1)} %bitcast.31), channel_id=1, source_target_pairs={{0,1},{1,0},{2,3},{3,2},{4,5},{5,4},{6,7},{7,6},{8,9},{9,8},{10,11... | collective-permute-start | bytes 1572872 | tf_op jit(solution)/shard_map/ppermute | solution.py:242
  48.4 3.5 %collective-permute-start.5 = (bf16[3072,256]{1,0:T(8,128)(2,1)S(1)}, bf16[3072,256]{1,0:T(8,128)(2,1)S(1)}, u32[]{:S(2)}, u32[]{:S(2)}) collective-permute-start(bf16[3072,256]{1,0:T(8,128)(2,1)S(1)} %get-tuple-element.32), channel_id=1, source_target_pairs={{0,1},{1,0},{2,3},{3,2},{4,5},{5,4},{6,7},{7,6},{8,9},{9,8},{10,11... | collective-permute-start | bytes 4718600 | tf_op jit(solution)/shard_map/ppermute | solution.py:242
  78.7 4.6 %collective-permute-start.8 = (bf16[96,256]{1,0:T(8,128)(2,1)S(1)}, bf16[96,256]{1,0:T(8,128)(2,1)S(1)}, u32[]{:S(2)}, u32[]{:S(2)}) collective-permute-start(bf16[96,256]{1,0:T(8,128)(2,1)S(1)} %reduce_sum.22), channel_id=1, source_target_pairs={{0,48},{16,0},{32,16},{48,32},{1,49},{17,1},{33,17},{49,33},{2,50}... | collective-permute-start | bytes 147464 | tf_op jit(solution)/shard_map/ppermute | solution.py:335
  79.0 5.5 %collective-permute-start.7 = (bf16[96,256]{1,0:T(8,128)(2,1)S(1)}, bf16[96,256]{1,0:T(8,128)(2,1)S(1)}, u32[]{:S(2)}, u32[]{:S(2)}) collective-permute-start(bf16[96,256]{1,0:T(8,128)(2,1)S(1)} %reduce_sum.22), channel_id=1, source_target_pairs={{0,16},{16,32},{32,48},{48,0},{1,17},{17,33},{33,49},{49,1},{2,18}... | collective-permute-start | bytes 147464 | tf_op jit(solution)/shard_map/ppermute | solution.py:335
  81.3 6.8 %collective-permute-start.6 = (bf16[96,256]{1,0:T(8,128)(2,1)S(1)}, bf16[96,256]{1,0:T(8,128)(2,1)S(1)}, u32[]{:S(2)}, u32[]{:S(2)}) collective-permute-start(bf16[96,256]{1,0:T(8,128)(2,1)S(1)} %reduce_sum.22), channel_id=1, source_target_pairs={{0,32},{16,48},{32,0},{48,16},{1,33},{17,49},{33,1},{49,17},{2,34}... | collective-permute-start | bytes 147464 | tf_op jit(solution)/shard_map/ppermute | solution.py:335
  89.3 18.8 %all-to-all-start.2 = ((bf16[32,64,256]{2,1,0:T(8,128)(2,1)}), bf16[32,64,256]{2,1,0:T(8,128)(2,1)S(1)}, u32[]{:S(2)}, u32[]{:S(2)}) async-start(bf16[32,64,256]{2,1,0:T(8,128)(2,1)} %broadcast_in_dim.11), calls=%async_computation.2 | async-start | bytes 2097152 | tf_op jit(solution)/shard_map/all_to_all | solution.py:342
  93.2 5.3 %collective-permute-start.11 = (bf16[8,256]{1,0:T(8,128)(2,1)S(1)}, bf16[8,256]{1,0:T(8,128)(2,1)S(1)}, u32[]{:S(2)}, u32[]{:S(2)}) collective-permute-start(bf16[8,256]{1,0:T(8,128)(2,1)S(1)} %constant_dynamic-slice_fusion), channel_id=1, source_target_pairs={{0,1},{1,0},{2,3},{3,2},{4,5},{5,4},{6,7},{7,6},{8,9},{9,8},{10,11... | collective-permute-start | bytes 12296 | tf_op jit(solution)/shard_map/ppermute | solution.py:242
  96.6 2.6 %collective-permute-start.9 = (f32[2,512]{1,0:T(2,128)S(1)}, f32[2,512]{1,0:T(2,128)S(1)}, u32[]{:S(2)}, u32[]{:S(2)}) collective-permute-start(f32[2,512]{1,0:T(2,128)S(1)} %get-tuple-element.33), channel_id=1, source_target_pairs={{0,1},{1,0},{2,3},{3,2},{4,5},{5,4},{6,7},{7,6},{8,9},{9,8},{10,11... | collective-permute-start | bytes 12296 | tf_op jit(solution)/shard_map/ppermute | solution.py:242
  96.7 8.9 %collective-permute-start.10 = (f32[2,512]{1,0:T(2,128)S(1)}, f32[2,512]{1,0:T(2,128)S(1)}, u32[]{:S(2)}, u32[]{:S(2)}) collective-permute-start(f32[2,512]{1,0:T(2,128)S(1)} %get-tuple-element.34), channel_id=1, source_target_pairs={{0,255},{1,2},{2,1},{3,4},{4,3},{5,6},{6,5},{7,8},{8,7},{9,10},{10... | collective-permute-start | bytes 12296 | tf_op jit(solution)/shard_map/ppermute | solution.py:349
  108.1 6.3 %collective-permute-start.12 = (bf16[2048,256]{1,0:T(8,128)(2,1)S(1)}, bf16[2048,256]{1,0:T(8,128)(2,1)S(1)}, u32[]{:S(2)}, u32[]{:S(2)}) collective-permute-start(bf16[2048,256]{1,0:T(8,128)(2,1)S(1)} %bitcast.29), channel_id=1, source_target_pairs={{0,1},{1,0},{2,3},{3,2},{4,5},{5,4},{6,7},{7,6},{8,9},{9,8},{10,11... | collective-permute-start | bytes 3145736 | tf_op jit(solution)/shard_map/ppermute | solution.py:242

commit v12 on v8

--- a/solution.py
+++ b/solution.py
@@ -45,7 +45,7 @@
 
 
 def group_kernel(
-    core_ref, rows_ref, places_ref, slot_ref, own_ref, below_ref, above_ref, below_two_ref, above_two_ref,
+    core_ref, rows_ref, places_ref, slot_ref, own_ref, mate_ref, side_ref, before_ref, behind_ref,
     mine_ref, other_ref, wk_ref, wv_ref, wq_ref, cells_hbm, wo_hbm,
     grad_cells_ref, inner_ref, middle_ref, outer_ref, roots_ref, keep_ref, send_ref,
     cells_ref, wo_ref, table_ref, sems,
@@ -138,22 +138,24 @@
     inner_ref[...] = jnp.where(first, top, low)
     outer_ref[...] = jnp.where(first, low, top)
 
+    below = jnp.where(first, side_ref[...], mate_ref[...])
+    above = jnp.where(first, mate_ref[...], side_ref[...])
     row = lax.broadcasted_iota(jnp.int32, (SLOTS, 128), 0)
     lane = lax.broadcasted_iota(jnp.int32, (SLOTS, 128), 1)
     counts = jnp.zeros((SLOTS, 128), f32)
     for offset, source in (
-        (2 * basins, below_two_ref[0:1, :]),
-        (basins, below_ref[basins : basins + 1, :128]),
+        (2 * basins, before_ref[basins : basins + 1, :128]),
+        (basins, below[basins : basins + 1, :128]),
         (0, own_ref[basins : basins + 1, :128]),
-        (-basins, above_ref[basins : basins + 1, :128]),
-        (-2 * basins, above_two_ref[0:1, :]),
+        (-basins, above[basins : basins + 1, :128]),
+        (-2 * basins, behind_ref[basins : basins + 1, :128]),
     ):
         counts = counts + jnp.where(lane == row + offset, source.astype(f32), 0.0)
     counts = jnp.sum(counts, axis=1, keepdims=True)
     used = lax.broadcasted_iota(jnp.int32, (SLOTS, 1), 0) < 3 * basins
     table_ref[...] = jnp.zeros_like(table_ref)
-    for place, source in enumerate((below_ref, own_ref, above_ref)):
-        table_ref[place * basins : (place + 1) * basins, :] = source[0:basins, :].astype(f32)
+    for place, source in enumerate((below, own_ref[...], above)):
+        table_ref[place * basins : (place + 1) * basins, :] = source[:basins, :].astype(f32)
     roots = jnp.sqrt(jnp.where(used, counts, 1.0))
     roots_ref[...] = jnp.broadcast_to(roots, roots_ref.shape)
     table = (table_ref[...] / roots).astype(bf16)
@@ -242,9 +244,9 @@
     return lax.ppermute(value, "c", [(0, 1), (1, 0)])
 
 
-def shifted(value, steps):
-    count = lax.axis_size(EVERY)
-    return lax.ppermute(value, EVERY, [(i, (i + steps) % count) for i in range(count)])
+def chips_over(value, steps):
+    count = lax.axis_size(TILES)
+    return lax.ppermute(value, TILES, [(i, (i + steps) % count) for i in range(count)])
 
 
 def copied(value, count):
@@ -266,7 +268,6 @@
 
     rows_own = lax.dynamic_slice_in_dim(encoded, core * half, half, 1)
     copies = copied(rows_own, MEMBERS * SIZES["far"])
-    mine = lax.all_to_all(copies, TILES, 0, 0, tiled=True)
 
     slot = (cell_basin - device * own + own) % total
     counts = jnp.sum(
@@ -274,11 +275,13 @@
     )
     count_row = jnp.pad(counts.astype(bf16), (0, width - 3 * own))[None, :]
     packet = after(jnp.concatenate([pooled_grad, count_row], axis=0), copies)
-    small = packet[own:, :128]
-    below, above = shifted(packet, 1), shifted(packet, -1)
-    below_two, above_two = shifted(small, 2), shifted(small, -2)
-    mine = after(mine, below, above, below_two, above_two)
+    before, behind = chips_over(packet, 1), chips_over(packet, -1)
+    mate = swap(packet)
+    mine = lax.all_to_all(copies, TILES, 0, 0, tiled=True)
+    before, behind, mate, mine = lax.optimization_barrier((before, behind, mate, mine))
     other = swap(mine)
+    side = swap(jnp.where(core == 0, behind, before))
+
     block = pattern[0]
     along_x = block % SIZES["x"]
     near = (block // SIZES["x"]) % SIZES["near"]
@@ -317,7 +320,7 @@
         compiler_params=pltpu.CompilerParams(vmem_limit_bytes=24 << 20),
         name="group_kernel",
     )(
-        core.reshape(1), rows, places, slot[None, :], packet, below, above, below_two, above_two,
+        core.reshape(1), rows, places, slot[None, :], packet, mate, side, before, behind,
         mine, other,
         w_key, w_value, w_query,
         pltpu.with_memory_space_constraint(cells, pltpu.HBM),

time: 116 us -> 116 us (level)
  blocking collectives: 44.7 us -> 47 us
  starting transfers between devices: 39.8 us -> 38.5 us
    ppermute x4 -> x2, starting transfers between devices: 14 us -> 7.05 us  [chips_over(): lax.ppermute(value, TILES, [(i, (i + steps) % count) for i in range(count)])]
    ppermute x5 -> x7, starting transfers between devices: 6.58 us -> 11.2 us  [swap(): return lax.ppermute(value, 'c', [(0, 1), (1, 0)])]
    all_to_all x1, blocking collectives: 18.5 us -> 19.8 us  [per_device(): lax.all_to_all(copied(reduced[:weight_chunk], MEMBERS), GROUP, 0, 0, tile...]
    ppermute x4 -> x2, waiting for transfers between devices: 7.82 us -> 8.59 us  [chips_over(): lax.ppermute(value, TILES, [(i, (i + steps) % count) for i in range(count)])]
    ppermute x5 -> x7, waiting for transfers between devices: 4.92 us -> 4.21 us  [swap(): return lax.ppermute(value, 'c', [(0, 1), (1, 0)])]
  transfers between devices with their start and end apart: 14 -> 14, of which waited for: 6 -> 5; matrix products, arithmetic and copies ran while one was open for 2% -> 2% of each run, Pallas kernels for 1% -> 1%
where the time goes in v12:
time: 116 us; the launch traced here: 115 us
  blocking collectives  47 us (41%)
  starting transfers between devices  38.5 us (33%)
  waiting for transfers between devices  16.1 us (14%)
  Pallas kernels  8.56 us (7%)
  other arithmetic  2.18 us (2%)
  local copies, waits for them, and re-layouts  1.91 us (2%)
    all_to_all x1, blocking collectives, per_device(): lax.all_to_all(chip, GROUP, 0, 0, tiled=True).reshape(MEMBERS, chunk, half)  27.2 us
    all_to_all x1, blocking collectives, per_device(): lax.all_to_all(copied(reduced[:weight_chunk], MEMBERS), GROUP, 0, 0, tile...  19.8 us
    all_to_all x1, starting transfers between devices, per_device(): mine = lax.all_to_all(copies, TILES, 0, 0, tiled=True)  16.3 us
    ppermute x7, starting transfers between devices, swap(): return lax.ppermute(value, 'c', [(0, 1), (1, 0)])  11.2 us
    ppermute x2, waiting for transfers between devices, chips_over(): lax.ppermute(value, TILES, [(i, (i + steps) % count) for i in range(count)])  8.59 us
    ppermute x2, starting transfers between devices, chips_over(): lax.ppermute(value, TILES, [(i, (i + steps) % count) for i in range(count)])  7.05 us
    pallas_call x1, Pallas kernels, per_device(): pl.pallas_call(group_kernel, out_shape=(jax.ShapeDtypeStruct(cells.shape,...  5.8 us
    ppermute x7, waiting for transfers between devices, swap(): return lax.ppermute(value, 'c', [(0, 1), (1, 0)])  4.21 us
  transfers between devices with their start and end apart: 14, of which 5 were waited for; matrix products, arithmetic and copies ran while one was open for 2% of the time, Pallas kernels for 1%

profile of v12, /device:TPU:1, one launch (start us, length us, event | category | flops | bytes accessed | tf_op | source)
XLA Modules:
  0.0 115.2 jit_solution(7947716020997264374)
XLA Ops:
  0.7 0.6 copy-done
  1.3 0.8 broadcast_in_dim.10
  2.2 16.3 %all-to-all-start = ((bf16[128,8,256]{2,1,0:T(8,128)(2,1)}), bf16[128,8,256]{2,1,0:T(8,128)(2,1)S(1)}, u32[]{:S(2)}, u32[]{:S(2)}) async-start(bf16[128,8,256]{2,1,0:T(8,128)(2,1)} %broadcast_in_dim.10), calls=%async_computation | async-start | bytes 1048576 | tf_op jit(solution)/shard_map/all_to_all | solution.py:280
  18.6 0.1 convert_reduce_fusion
  18.7 1.0 collective-permute-start.2
  19.8 7.0 %collective-permute-start.1 = (bf16[3,512]{1,0:T(4,128)(2,1)S(1)}, bf16[3,512]{1,0:T(4,128)(2,1)S(1)}, u32[]{:S(2)}, u32[]{:S(2)}) collective-permute-start(bf16[3,512]{1,0:T(4,128)(2,1)S(1)} %pad_maximum_fusion.own_ref), channel_id=1, source_target_pairs={{0,254},{2,0},{4,2},{6,4},{8,6},{10,8},{12,10},{14,12},{16,14},{18... | collective-permute-start | bytes 9224 | tf_op jit(solution)/shard_map/ppermute | solution.py:249
  26.8 1.1 collective-permute-done.1.behind_ref
  27.9 7.5 %collective-permute-done.before_ref = bf16[3,512]{1,0:T(4,128)(2,1)S(1)} collective-permute-done((bf16[3,512]{1,0:T(4,128)(2,1)S(1)}, bf16[3,512]{1,0:T(4,128)(2,1)S(1)}, u32[]{:S(2)}, u32[]{:S(2)}) %collective-permute-start) | collective-permute-done | bytes 3104 | tf_op jit(solution)/shard_map/ppermute | solution.py:249
  35.4 3.4 %collective-permute-start.4 = (bf16[1024,256]{1,0:T(8,128)(2,1)S(1)}, bf16[1024,256]{1,0:T(8,128)(2,1)S(1)}, u32[]{:S(2)}, u32[]{:S(2)}) collective-permute-start(bf16[1024,256]{1,0:T(8,128)(2,1)S(1)} %bitcast.31), channel_id=1, source_target_pairs={{0,1},{1,0},{2,3},{3,2},{4,5},{5,4},{6,7},{7,6},{8,9},{9,8},{10,11... | collective-permute-start | bytes 1572872 | tf_op jit(solution)/shard_map/ppermute | solution.py:244
  38.8 0.1 collective-permute-start.3
  39.2 1.1 collective-permute-done.3.side_ref
  40.4 5.8 %group_kernel.1 = (bf16[256,512]{1,0:T(8,128)(2,1)}, f32[2,512]{1,0:T(2,128)S(1)}, f32[2,512]{1,0:T(2,128)S(1)}, f32[2,512]{1,0:T(2,128)S(1)}, f32[16,128]{1,0:T...) custom-call(s32[1]{0:T(128)} %bitcast.core_ref.side_ref, s32[1,128]{1,0:T(1,128)S(1)} %add.166.rows_ref, ...), custom_call_target="tpu_custom_call" | custom-call | tf_op jit(solution)/shard_map/group_kernel/pallas_call | solution.py:301
  46.2 0.5 collective-permute-start.5
  46.6 3.0 %collective-permute-done.5 = bf16[3072,256]{1,0:T(8,128)(2,1)S(1)} collective-permute-done((bf16[3072,256]{1,0:T(8,128)(2,1)S(1)}, bf16[3072,256]{1,0:T(8,128)(2,1)S(1)}, u32[]{:S(2)}, u32[]{:S(2)}) %collective-permute-start.5) | collective-permute-done | bytes 1572896 | tf_op jit(solution)/shard_map/ppermute | solution.py:244
  49.7 0.4 add_convert_fusion
  50.1 27.2 %all_to_all.27 = bf16[32,96,256]{2,1,0:T(8,128)(2,1)S(1)} all-to-all(bf16[32,96,256]{2,1,0:T(8,128)(2,1)S(1)} %bitcast.35), channel_id=1, replica_groups=mesh['y'=4,'far'=4,'near'=2,'x'=4,'c'=2] {'y','x','near'}, dimensions={0} | all-to-all | bytes 3145728 | tf_op jit(solution)/shard_map/all_to_all | solution.py:334
  77.3 0.2 reduce_sum.22
  77.6 0.4 collective-permute-start.10
  77.9 2.1 %collective-permute-start.9 = (bf16[96,256]{1,0:T(8,128)(2,1)S(1)}, bf16[96,256]{1,0:T(8,128)(2,1)S(1)}, u32[]{:S(2)}, u32[]{:S(2)}) collective-permute-start(bf16[96,256]{1,0:T(8,128)(2,1)S(1)} %reduce_sum.22), channel_id=1, source_target_pairs={{0,16},{16,32},{32,48},{48,0},{1,17},{17,33},{33,49},{49,1},{2,18}... | collective-permute-start | bytes 147464 | tf_op jit(solution)/shard_map/ppermute | solution.py:338
  80.0 1.2 %collective-permute-start.8 = (bf16[96,256]{1,0:T(8,128)(2,1)S(1)}, bf16[96,256]{1,0:T(8,128)(2,1)S(1)}, u32[]{:S(2)}, u32[]{:S(2)}) collective-permute-start(bf16[96,256]{1,0:T(8,128)(2,1)S(1)} %reduce_sum.22), channel_id=1, source_target_pairs={{0,32},{16,48},{32,0},{48,16},{1,33},{17,49},{33,1},{49,17},{2,34}... | collective-permute-start | bytes 147464 | tf_op jit(solution)/shard_map/ppermute | solution.py:338
  81.2 2.2 %collective-permute-start.6 = (f32[2,512]{1,0:T(2,128)S(1)}, f32[2,512]{1,0:T(2,128)S(1)}, u32[]{:S(2)}, u32[]{:S(2)}) collective-permute-start(f32[2,512]{1,0:T(2,128)S(1)} %get-tuple-element.39), channel_id=1, source_target_pairs={{0,1},{1,0},{2,3},{3,2},{4,5},{5,4},{6,7},{7,6},{8,9},{9,8},{10,11... | collective-permute-start | bytes 12296 | tf_op jit(solution)/shard_map/ppermute | solution.py:244
  83.3 0.2 collective-permute-start.7
  83.6 3.3 %collective-permute-done.8 = bf16[96,256]{1,0:T(8,128)(2,1)S(1)} collective-permute-done((bf16[96,256]{1,0:T(8,128)(2,1)S(1)}, bf16[96,256]{1,0:T(8,128)(2,1)S(1)}, u32[]{:S(2)}, u32[]{:S(2)}) %collective-permute-start.8) | collective-permute-done | bytes 49184 | tf_op jit(solution)/shard_map/ppermute | solution.py:338
  86.9 0.1 broadcast_in_dim.11
  87.0 19.8 %all_to_all.28 = bf16[32,64,256]{2,1,0:T(8,128)(2,1)S(1)} all-to-all(bf16[32,64,256]{2,1,0:T(8,128)(2,1)S(1)} %broadcast_in_dim.11), channel_id=1, replica_groups=mesh['y'=4,'far'=4,'near'=2,'x'=4,'c'=2] {'y','x','near'}, dimensions={0} | all-to-all | bytes 2097152 | tf_op jit(solution)/shard_map/all_to_all | solution.py:353
  106.8 4.0 %collective-permute-start.12 = (bf16[2048,256]{1,0:T(8,128)(2,1)S(1)}, bf16[2048,256]{1,0:T(8,128)(2,1)S(1)}, u32[]{:S(2)}, u32[]{:S(2)}) collective-permute-start(bf16[2048,256]{1,0:T(8,128)(2,1)S(1)} %bitcast.29), channel_id=1, source_target_pairs={{0,1},{1,0},{2,3},{3,2},{4,5},{5,4},{6,7},{7,6},{8,9},{9,8},{10,11... | collective-permute-start | bytes 3145736 | tf_op jit(solution)/shard_map/ppermute | solution.py:244
  110.8 0.1 slice_reduce_fusion
  110.9 0.1 collective-permute-start.11
  111.0 0.7 fusion
  111.7 1.4 %widen_kernel.2 = (f32[512,512]{1,0:T(8,128)}, f32[512,512]{1,0:T(8,128)}, f32[512,512]{1,0:T(8,128)}, f32[512,512]{1,0:T(8,128)}) custom-call(s32[1]{0:T(128)} %bitcast.core_ref.side_ref, bf16[4,512,256]{2,1,0:T(8,128)(2,1)S(1)} %bitcast.30), custom_call_target="tpu_custom_call" | custom-call | tf_op jit(solution)/shard_map/widen_kernel/pallas_call | solution.py:224
  113.1 0.6 maximum_select_fusion
  113.7 1.4 %widen_kernel.3 = (f32[512,512]{1,0:T(8,128)}, f32[512,512]{1,0:T(8,128)}, f32[512,512]{1,0:T(8,128)}, f32[512,512]{1,0:T(8,128)}) custom-call(s32[1]{0:T(128)} %bitcast.6.side_ref, bf16[4,512,256]{2,1,0:T(8,128)(2,1)S(1)} %bitcast.33, ...), custom_call_target="tpu_custom_call", output_to_operand_aliasing={{0}: (2, {}), {1}: (3, {}), {2}: (4, {}), {3}: (5, {})} | custom-call | tf_op jit(solution)/shard_map/widen_kernel/pallas_call | solution.py:224
  (36 shorter events, 0.4 us)
Async XLA Ops:
  0.6 0.7 copy-start
  0.7 17.9 %copy-start.5 = (s32[256]{0:T(256)S(1)}, s32[256]{0:T(256)}, u32[]{:S(2)}) copy-start(s32[256]{0:T(256)} %param.16) | copy-start | bytes 3076
  0.7 18.0 %copy-start.4 = (bf16[2,512]{1,0:T(2,128)(2,1)S(1)}, bf16[2,512]{1,0:T(2,128)(2,1)}, u32[]{:S(2)}) copy-start(bf16[2,512]{1,0:T(2,128)(2,1)} %param.17) | copy-start | bytes 6148
  0.7 38.1 %copy-start.6 = (s32[1,16]{1,0:T(1,128)S(1)}, s32[1,16]{1,0:T(1,128)}, u32[]{:S(2)}) copy-start(s32[1,16]{1,0:T(1,128)} %param.15) | copy-start | bytes 196
  0.7 39.7 %copy-start.2 = (bf16[512,512]{1,0:T(8,128)(2,1)S(1)}, bf16[512,512]{1,0:T(8,128)(2,1)}, u32[]{:S(2)}) copy-start(bf16[512,512]{1,0:T(8,128)(2,1)} %wv_ref.1) | copy-start | bytes 1572868
  0.7 39.7 %copy-start.1 = (bf16[512,512]{1,0:T(8,128)(2,1)S(1)}, bf16[512,512]{1,0:T(8,128)(2,1)}, u32[]{:S(2)}) copy-start(bf16[512,512]{1,0:T(8,128)(2,1)} %wk_ref.1) | copy-start | bytes 1572868
  0.7 39.6 %copy-start.3 = (bf16[512,512]{1,0:T(8,128)(2,1)S(1)}, bf16[512,512]{1,0:T(8,128)(2,1)}, u32[]{:S(2)}) copy-start(bf16[512,512]{1,0:T(8,128)(2,1)} %wq_ref.1) | copy-start | bytes 1572868
  2.2 33.2 %all-to-all-start = ((bf16[128,8,256]{2,1,0:T(8,128)(2,1)}), bf16[128,8,256]{2,1,0:T(8,128)(2,1)S(1)}, u32[]{:S(2)}, u32[]{:S(2)}) async-start(bf16[128,8,256]{2,1,0:T(8,128)(2,1)} %broadcast_in_dim.10), calls=%async_computation | async-start | bytes 1048576 | tf_op jit(solution)/shard_map/all_to_all | solution.py:280
  18.7 8.1 %collective-permute-start.2 = (bf16[3,512]{1,0:T(4,128)(2,1)S(1)}, bf16[3,512]{1,0:T(4,128)(2,1)S(1)}, u32[]{:S(2)}, u32[]{:S(2)}) collective-permute-start(bf16[3,512]{1,0:T(4,128)(2,1)S(1)} %pad_maximum_fusion.own_ref), channel_id=1, source_target_pairs={{0,1},{1,0},{2,3},{3,2},{4,5},{5,4},{6,7},{7,6},{8,9},{9,8},{10,11... | collective-permute-start | bytes 9224 | tf_op jit(solution)/shard_map/ppermute | solution.py:244
  19.8 8.2 %collective-permute-start.1 = (bf16[3,512]{1,0:T(4,128)(2,1)S(1)}, bf16[3,512]{1,0:T(4,128)(2,1)S(1)}, u32[]{:S(2)}, u32[]{:S(2)}) collective-permute-start(bf16[3,512]{1,0:T(4,128)(2,1)S(1)} %pad_maximum_fusion.own_ref), channel_id=1, source_target_pairs={{0,254},{2,0},{4,2},{6,4},{8,6},{10,8},{12,10},{14,12},{16,14},{18... | collective-permute-start | bytes 9224 | tf_op jit(solution)/shard_map/ppermute | solution.py:249
  26.8 8.6 %collective-permute-start = (bf16[3,512]{1,0:T(4,128)(2,1)S(1)}, bf16[3,512]{1,0:T(4,128)(2,1)S(1)}, u32[]{:S(2)}, u32[]{:S(2)}) collective-permute-start(bf16[3,512]{1,0:T(4,128)(2,1)S(1)} %pad_maximum_fusion.own_ref), channel_id=1, source_target_pairs={{0,2},{2,4},{4,6},{6,8},{8,10},{10,12},{12,14},{14,16},{16,18},{18... | collective-permute-start | bytes 9224 | tf_op jit(solution)/shard_map/ppermute | solution.py:249
  35.4 4.9 %collective-permute-start.4 = (bf16[1024,256]{1,0:T(8,128)(2,1)S(1)}, bf16[1024,256]{1,0:T(8,128)(2,1)S(1)}, u32[]{:S(2)}, u32[]{:S(2)}) collective-permute-start(bf16[1024,256]{1,0:T(8,128)(2,1)S(1)} %bitcast.31), channel_id=1, source_target_pairs={{0,1},{1,0},{2,3},{3,2},{4,5},{5,4},{6,7},{7,6},{8,9},{9,8},{10,11... | collective-permute-start | bytes 1572872 | tf_op jit(solution)/shard_map/ppermute | solution.py:244
  38.8 1.5 %collective-permute-start.3 = (bf16[3,512]{1,0:T(4,128)(2,1)S(1)}, bf16[3,512]{1,0:T(4,128)(2,1)S(1)}, u32[]{:S(2)}, u32[]{:S(2)}) collective-permute-start(bf16[3,512]{1,0:T(4,128)(2,1)S(1)} %broadcast_select_fusion), channel_id=1, source_target_pairs={{0,1},{1,0},{2,3},{3,2},{4,5},{5,4},{6,7},{7,6},{8,9},{9,8},{10,11... | collective-permute-start | bytes 9224 | tf_op jit(solution)/shard_map/ppermute | solution.py:244
  46.2 3.5 %collective-permute-start.5 = (bf16[3072,256]{1,0:T(8,128)(2,1)S(1)}, bf16[3072,256]{1,0:T(8,128)(2,1)S(1)}, u32[]{:S(2)}, u32[]{:S(2)}) collective-permute-start(bf16[3072,256]{1,0:T(8,128)(2,1)S(1)} %get-tuple-element.38), channel_id=1, source_target_pairs={{0,1},{1,0},{2,3},{3,2},{4,5},{5,4},{6,7},{7,6},{8,9},{9,8},{10,11... | collective-permute-start | bytes 4718600 | tf_op jit(solution)/shard_map/ppermute | solution.py:244
  77.6 6.0 %collective-permute-start.10 = (bf16[96,256]{1,0:T(8,128)(2,1)S(1)}, bf16[96,256]{1,0:T(8,128)(2,1)S(1)}, u32[]{:S(2)}, u32[]{:S(2)}) collective-permute-start(bf16[96,256]{1,0:T(8,128)(2,1)S(1)} %reduce_sum.22), channel_id=1, source_target_pairs={{0,48},{16,0},{32,16},{48,32},{1,49},{17,1},{33,17},{49,33},{2,50}... | collective-permute-start | bytes 147464 | tf_op jit(solution)/shard_map/ppermute | solution.py:338
  77.9 5.6 %collective-permute-start.9 = (bf16[96,256]{1,0:T(8,128)(2,1)S(1)}, bf16[96,256]{1,0:T(8,128)(2,1)S(1)}, u32[]{:S(2)}, u32[]{:S(2)}) collective-permute-start(bf16[96,256]{1,0:T(8,128)(2,1)S(1)} %reduce_sum.22), channel_id=1, source_target_pairs={{0,16},{16,32},{32,48},{48,0},{1,17},{17,33},{33,49},{49,1},{2,18}... | collective-permute-start | bytes 147464 | tf_op jit(solution)/shard_map/ppermute | solution.py:338
  80.0 6.8 %collective-permute-start.8 = (bf16[96,256]{1,0:T(8,128)(2,1)S(1)}, bf16[96,256]{1,0:T(8,128)(2,1)S(1)}, u32[]{:S(2)}, u32[]{:S(2)}) collective-permute-start(bf16[96,256]{1,0:T(8,128)(2,1)S(1)} %reduce_sum.22), channel_id=1, source_target_pairs={{0,32},{16,48},{32,0},{48,16},{1,33},{17,49},{33,1},{49,17},{2,34}... | collective-permute-start | bytes 147464 | tf_op jit(solution)/shard_map/ppermute | solution.py:338
  81.2 5.7 %collective-permute-start.6 = (f32[2,512]{1,0:T(2,128)S(1)}, f32[2,512]{1,0:T(2,128)S(1)}, u32[]{:S(2)}, u32[]{:S(2)}) collective-permute-start(f32[2,512]{1,0:T(2,128)S(1)} %get-tuple-element.39), channel_id=1, source_target_pairs={{0,1},{1,0},{2,3},{3,2},{4,5},{5,4},{6,7},{7,6},{8,9},{9,8},{10,11... | collective-permute-start | bytes 12296 | tf_op jit(solution)/shard_map/ppermute | solution.py:244
  83.3 3.6 %collective-permute-start.7 = (f32[2,512]{1,0:T(2,128)S(1)}, f32[2,512]{1,0:T(2,128)S(1)}, u32[]{:S(2)}, u32[]{:S(2)}) collective-permute-start(f32[2,512]{1,0:T(2,128)S(1)} %get-tuple-element.40), channel_id=1, source_target_pairs={{0,255},{1,2},{2,1},{3,4},{4,3},{5,6},{6,5},{7,8},{8,7},{9,10},{10... | collective-permute-start | bytes 12296 | tf_op jit(solution)/shard_map/ppermute | solution.py:344
  106.8 6.9 %collective-permute-start.12 = (bf16[2048,256]{1,0:T(8,128)(2,1)S(1)}, bf16[2048,256]{1,0:T(8,128)(2,1)S(1)}, u32[]{:S(2)}, u32[]{:S(2)}) collective-permute-start(bf16[2048,256]{1,0:T(8,128)(2,1)S(1)} %bitcast.29), channel_id=1, source_target_pairs={{0,1},{1,0},{2,3},{3,2},{4,5},{5,4},{6,7},{7,6},{8,9},{9,8},{10,11... | collective-permute-start | bytes 3145736 | tf_op jit(solution)/shard_map/ppermute | solution.py:244
  110.9 2.2 %collective-permute-start.11 = (bf16[8,256]{1,0:T(8,128)(2,1)S(1)}, bf16[8,256]{1,0:T(8,128)(2,1)S(1)}, u32[]{:S(2)}, u32[]{:S(2)}) collective-permute-start(bf16[8,256]{1,0:T(8,128)(2,1)S(1)} %constant_dynamic-slice_fusion), channel_id=1, source_target_pairs={{0,1},{1,0},{2,3},{3,2},{4,5},{5,4},{6,7},{7,6},{8,9},{9,8},{10,11... | collective-permute-start | bytes 12296 | tf_op jit(solution)/shard_map/ppermute | solution.py:244
